TPU v7x, 32 devices: a whole 2x2x4 slice. The times are simulated.
32 devices in a mesh: seq: 8 (over z, y), tensor: 4 (over x, core).
Axes of the slice: x: 2, y: 2, z: 4, core: 2. Of those that a mesh axis runs over, the one named last changes fastest.
Arguments:
- inputs: bfloat16 [1024, 3, 4096], P('seq', None, 'tensor'), may hold values from -6 to 6
- short_taps: float32 [7, 3, 4096], P(None, None, 'tensor'), may hold values from -2 to 2
- medium_taps: float32 [120, 4096], P(None, 'tensor'), may hold values from -0.5 to 0.5
- long_filter: float32 [1024, 4096], P('seq', 'tensor'), may hold values from -4 to 4
- out_weight: bfloat16 [8192, 4096], P(None, 'tensor'), may hold values from -0.09375 to 0.09375
- out_cotangent: bfloat16 [1024, 8192], P('seq', 'tensor'), may hold values from -6 to 6
Outputs:
- output: bfloat16 [1024, 8192], P('seq', 'tensor')
- input_grad: bfloat16 [1024, 3, 4096], P('seq', None, 'tensor')
- filter_grad: float32 [1024, 4096], P('seq', 'tensor')
- medium_grad: float32 [120, 4096], P(None, 'tensor')
- short_grad: float32 [7, 3, 4096], P(None, None, 'tensor')
All inputs are finite; a program needn't handle non-finite values.
Results may differ from a plain program's by a relative error of at most 0.013.
Values may be sent and summed in bfloat16 or wider, within the bound.
No kernel may reach another device: no remote copies, remote signals or barrier semaphores. Data moves between devices by JAX's collectives and lax.ppermute only.
A program may use at most 128 MiB of HBM per device.

v0:
```python
import math

import jax
import jax.numpy as jnp
from jax import lax
from jax.sharding import PartitionSpec as P

precise = lax.Precision.HIGHEST


def from_behind(value, axis, steps):
    count = lax.axis_size(axis)
    leading, last = (max(0, -steps), min(count, count - steps))
    return lax.ppermute(value, axis, [(source, source + steps) for source in range(leading, last)])


def as_sent(shard):

    def short(part):
        return part.astype(jnp.bfloat16) if part.dtype == jnp.float32 else part

    return jax.tree.map(short, shard)


def correlate(signal, kernel):
    channels = kernel.shape[1]
    result = lax.conv_general_dilated(
        signal[None],
        kernel[:, None, :],
        (1,),
        "VALID",
        dimension_numbers=("NWC", "WIO", "NWC"),
        feature_group_count=channels,
        precision=precise,
    )
    return result[0]


def angles(left_index, right_index, modulus):
    return (left_index * right_index % modulus).astype(jnp.float32) * (2.0 * math.pi / modulus)


def to_spectrum(signals, cos_table, sin_table):
    signal_count = signals.shape[0]
    length = signals.shape[1]
    channels = signals.shape[2]
    devices = lax.axis_size("seq")
    position = lax.axis_index("seq")
    stride = length // devices
    modulus = 2 * devices * length
    columns = lax.all_to_all(
        signals.reshape(signal_count, devices, stride, channels),
        "seq",
        split_axis=1,
        concat_axis=1,
        tiled=True,
    )
    coarse = jnp.arange(2 * devices, dtype=jnp.int32)
    sources = jnp.arange(devices, dtype=jnp.int32)
    coarse_angle = angles(coarse[:, None], sources[None, :], 2 * devices)
    first_real = jnp.einsum("kp,spmc->skmc", jnp.cos(coarse_angle), columns, precision=precise)
    first_imag = -jnp.einsum("kp,spmc->skmc", jnp.sin(coarse_angle), columns, precision=precise)
    local_rows = position * stride + jnp.arange(stride, dtype=jnp.int32)
    twiddle = angles(coarse[:, None], local_rows[None, :], modulus)
    cosine_values = jnp.cos(twiddle)[None, :, :, None]
    sine_part = jnp.sin(twiddle)[None, :, :, None]
    turned = jnp.stack(
        [
            first_real * cosine_values + first_imag * sine_part,
            first_imag * cosine_values - first_real * sine_part,
        ]
    )
    arrived = lax.all_to_all(turned, "seq", split_axis=2, concat_axis=3, tiled=True)
    spec_real = jnp.einsum("km,sjmc->sjkc", cos_table, arrived[0], precision=precise) + jnp.einsum(
        "km,sjmc->sjkc", sin_table, arrived[1], precision=precise
    )
    spec_imag = jnp.einsum("km,sjmc->sjkc", cos_table, arrived[1], precision=precise) - jnp.einsum(
        "km,sjmc->sjkc", sin_table, arrived[0], precision=precise
    )
    return (spec_real, spec_imag)


def from_spectrum(spec_real, spec_imag, cos_table, sin_table):
    signal_count = spec_real.shape[0]
    length = spec_real.shape[2]
    channels = spec_real.shape[3]
    devices = lax.axis_size("seq")
    position = lax.axis_index("seq")
    modulus = 2 * devices * length
    fine_real = jnp.einsum("mk,sjkc->sjmc", cos_table, spec_real, precision=precise) - jnp.einsum(
        "mk,sjkc->sjmc", sin_table, spec_imag, precision=precise
    )
    fine_imag = jnp.einsum("mk,sjkc->sjmc", cos_table, spec_imag, precision=precise) + jnp.einsum(
        "mk,sjkc->sjmc", sin_table, spec_real, precision=precise
    )
    held = 2 * position + jnp.arange(2, dtype=jnp.int32)
    all_rows = jnp.arange(length, dtype=jnp.int32)
    twiddle = angles(held[:, None], all_rows[None, :], modulus)
    cosine_values = jnp.cos(twiddle)[None, :, :, None]
    sine_part = jnp.sin(twiddle)[None, :, :, None]
    turned = jnp.stack(
        [
            fine_real * cosine_values - fine_imag * sine_part,
            fine_real * sine_part + fine_imag * cosine_values,
        ]
    )
    arrived = lax.all_to_all(turned, "seq", split_axis=3, concat_axis=2, tiled=True)
    coarse = jnp.arange(2 * devices, dtype=jnp.int32)
    sources = jnp.arange(devices, dtype=jnp.int32)
    coarse_angle = angles(sources[:, None], coarse[None, :], 2 * devices)
    blocks = (
        jnp.einsum("pk,skmc->spmc", jnp.cos(coarse_angle), arrived[0], precision=precise)
        - jnp.einsum("pk,skmc->spmc", jnp.sin(coarse_angle), arrived[1], precision=precise)
    ) / modulus
    returned = lax.all_to_all(blocks, "seq", split_axis=1, concat_axis=1, tiled=True)
    return returned.reshape(signal_count, length, channels)


def local(inputs, short_taps, medium_taps, long_filter, out_weight, out_cotangent):
    length = inputs.shape[0]
    groups = inputs.shape[1]
    channels = inputs.shape[2]
    short_reach = short_taps.shape[0]
    medium_reach = medium_taps.shape[0]
    devices = lax.axis_size("seq")
    scale = 1.0 / math.sqrt(length * devices)
    flat_inputs = inputs.reshape(length, groups * channels)
    short_flat = short_taps.reshape(short_reach, groups * channels)
    input_edge = from_behind(flat_inputs[length - (short_reach - 1) :], "seq", 1)
    extended_inputs = jnp.concatenate([input_edge, flat_inputs], 0).astype(jnp.float32)
    featured = correlate(extended_inputs, short_flat[::-1])
    gated = featured[:, channels : 2 * channels] * featured[:, 2 * channels :]
    gated_edge = from_behind(as_sent(gated[length - (medium_reach - 1) :]), "seq", 1)
    extended_gated = jnp.concatenate([gated_edge, gated], 0)
    query_branch = featured[:, :channels]
    key_branch = featured[:, channels : 2 * channels]
    value_branch = featured[:, 2 * channels :]
    mixed = correlate(extended_gated, medium_taps[::-1])
    all_rows = jnp.arange(length, dtype=jnp.int32)
    grid_angle = angles(all_rows[:, None], all_rows[None, :], length)
    cos_table = jnp.cos(grid_angle)
    sin_table = jnp.sin(grid_angle)
    spec_real, spec_imag = to_spectrum(jnp.stack([mixed, long_filter]), cos_table, sin_table)
    mixed_real = spec_real[0]
    mixed_imag = spec_imag[0]
    filter_real = spec_real[1]
    filter_imag = spec_imag[1]
    conv_real = mixed_real * filter_real - mixed_imag * filter_imag
    conv_imag = mixed_real * filter_imag + mixed_imag * filter_real
    convolved = from_spectrum(conv_real[None], conv_imag[None], cos_table, sin_table)[0]
    product = (query_branch * convolved).astype(jnp.bfloat16)
    partial_out = lax.dot_general(
        product, out_weight, (((1,), (1,)), ((), ())), preferred_element_type=jnp.float32
    )
    output = lax.psum_scatter(partial_out, "tensor", scatter_dimension=1, tiled=True).astype(
        jnp.bfloat16
    )
    full_cotangent = lax.all_gather(out_cotangent, "tensor", axis=1, tiled=True)
    product_grad = jnp.dot(full_cotangent, out_weight, preferred_element_type=jnp.float32)
    query_grad = product_grad * convolved
    convolved_grad = product_grad * query_branch
    grad_real, grad_imag = to_spectrum(convolved_grad[None], cos_table, sin_table)
    grad_real = grad_real[0]
    grad_imag = grad_imag[0]
    back_real = jnp.stack(
        [
            filter_real * grad_real + filter_imag * grad_imag,
            mixed_real * grad_real + mixed_imag * grad_imag,
        ]
    )
    back_imag = jnp.stack(
        [
            filter_real * grad_imag - filter_imag * grad_real,
            mixed_real * grad_imag - mixed_imag * grad_real,
        ]
    )
    timed = from_spectrum(back_real, back_imag, cos_table, sin_table)
    mixed_grad = timed[0]
    filter_grad = timed[1] * scale
    mixed_edge = from_behind(as_sent(mixed_grad[: medium_reach - 1]), "seq", -1)
    gated_grad = correlate(jnp.concatenate([mixed_grad, mixed_edge], 0), medium_taps)
    medium_part = correlate(extended_gated, mixed_grad)[::-1]
    feature_gradient = jnp.concatenate(
        [query_grad, gated_grad * value_branch, gated_grad * key_branch], 1
    )
    featured_edge = from_behind(as_sent(feature_gradient[: short_reach - 1]), "seq", -1)
    input_grad = (
        correlate(jnp.concatenate([feature_gradient, featured_edge], 0), short_flat)
        .astype(jnp.bfloat16)
        .reshape(length, groups, channels)
    )
    short_part = correlate(extended_inputs, feature_gradient)[::-1]
    medium_sum, short_sum = (
        lax.psum(medium_part.astype(jnp.bfloat16), "seq").astype(jnp.float32),
        lax.psum(short_part.astype(jnp.bfloat16), "seq").astype(jnp.float32),
    )
    medium_grad = medium_sum * scale
    short_grad = (short_sum * scale).reshape(short_reach, groups, channels)
    return (output, input_grad, filter_grad, medium_grad, short_grad)


def solution(mesh):
    return jax.shard_map(
        local,
        mesh=mesh,
        in_specs=(
            P("seq", None, "tensor"),
            P(None, None, "tensor"),
            P(None, "tensor"),
            P("seq", "tensor"),
            P(None, "tensor"),
            P("seq", "tensor"),
        ),
        out_specs=(
            P("seq", "tensor"),
            P("seq", None, "tensor"),
            P("seq", "tensor"),
            P(None, "tensor"),
            P(None, None, "tensor"),
        ),
        check_vma=False,
    )
```

profile of v0, /device:TPU:0, one launch (start us, length us, event | category | flops | bytes accessed | tf_op | source)
XLA Modules:
  0.0 607.2 jit_solution(8944364279748115227)
XLA Ops:
  8.7 4.9 collective-permute-start
  23.4 11.5 %all-gather.2.cloned.1.call-done = bf16[128,8192]{1,0:T(8,128)(2,1)} async-done(((bf16[128,2048]{1,0:T(8,128)(2,1)}), bf16[128,8192]{1,0:T(8,128)(2,1)}) %all-gather.2.cloned.1.call-update) | async-done | bytes 2097168 | tf_op jit(solution)/shard_map/all_gather | solution.py:158
  34.9 9.8 %slice_multiply_fusion.1 = (f32[128,1024]{1,0:T(8,128)}, f32[128,1024]{1,0:T(8,128)S(1)}, f32[128,1024]{1,0:T(8,128)}) fusion(f32[128,3072]{1,0:T(8,128)S(1)} %slice_bitcast_fusion, bf16[128,8192]{1,0:T(8,128)(2,1)} %all-gather.2.cloned.1.call-done, bf16[8192,1024]{1,0:T(8,128)(2,1)} %param.10), kind=kOutput, calls=%fused_computation.100 | convolution fusion | flops 2147745792 | bytes 22020096 | tf_op jit(solution)/shard_map/dot_general | solution.py:159
  48.4 4.6 all-to-all-start.4
  55.0 5.3 fusion.57
  61.7 5.9 all-to-all-done.4
  67.6 4.1 all-to-all-start
  77.5 20.0 %all-to-all-done = f32[2,8,16,1024]{3,2,0,1:T(8,128)S(1)} async-done(((f32[2,8,16,1024]{3,2,0,1:T(8,128)}), f32[2,8,16,1024]{3,2,0,1:T(8,128)S(1)}, u32[]{:S(2)}, u32[]{:S(2)}) %all-to-all-start) | async-done | bytes 1048608 | tf_op jit(solution)/shard_map/all_to_all | solution.py:51
  107.1 4.4 copy.127
  111.5 38.0 %all-to-all-done.5 = f32[2,1,16,16,1024]{4,3,1,0,2:T(8,128)S(1)} async-done(((f32[2,1,16,16,1024]{4,3,1,0,2:T(8,128)}), f32[2,1,16,16,1024]{4,3,1,0,2:T(8,128)S(1)}, u32[]{:S(2)}, u32[]{:S(2)}) %all-to-all-start.5) | async-done | bytes 2097184 | tf_op jit(solution)/shard_map/all_to_all | solution.py:73
  149.5 5.0 all-to-all-start.1
  163.1 83.5 %all-to-all-done.1 = f32[2,2,16,16,1024]{4,3,1,0,2:T(8,128)} async-done(((f32[2,2,16,16,1024]{4,3,1,0,2:T(8,128)}), f32[2,2,16,16,1024]{4,3,1,0,2:T(8,128)}, u32[]{:S(2)}, u32[]{:S(2)}) %all-to-all-start.1) | async-done | bytes 4194336 | tf_op jit(solution)/shard_map/all_to_all | solution.py:73
  253.8 3.8 fusion.79
  257.6 3.7 add_bitcast_fusion.1
  261.3 3.7 subtract_bitcast_fusion.1
  279.1 7.3 %copy.150 = f32[2,2,2,128,1024]{4,2,1,0,3:T(2,128)} copy(f32[2,2,2,128,1024]{3,4,2,1,0:T(8,128)} %pad_maximum_fusion.1) | data formatting | bytes 8388608 | tf_op jit(solution)/shard_map/stack | solution.py:101
  286.4 4.6 all-to-all-start.6
  298.7 84.8 %all-to-all-done.6 = f32[2,2,2,128,1024]{4,2,1,0,3:T(2,128)} async-done(((f32[2,2,2,128,1024]{4,2,1,0,3:T(2,128)}), f32[2,2,2,128,1024]{4,2,1,0,3:T(2,128)}, u32[]{:S(2)}, u32[]{:S(2)}) %all-to-all-start.6) | async-done | bytes 4194336 | tf_op jit(solution)/shard_map/all_to_all | solution.py:107
  383.5 3.8 all-to-all-start.2
  387.3 4.6 copy.151
  396.7 3.7 squeeze.21
  400.4 4.6 copy.153
  414.6 21.1 %all-to-all-done.2 = f32[2,1,2,128,1024]{4,2,1,0,3:T(2,128)S(1)} async-done(((f32[2,1,2,128,1024]{4,2,1,0,3:T(2,128)}), f32[2,1,2,128,1024]{4,2,1,0,3:T(2,128)S(1)}, u32[]{:S(2)}, u32[]{:S(2)}) %all-to-all-start.2) | async-done | bytes 2097184 | tf_op jit(solution)/shard_map/all_to_all | solution.py:107
  435.7 3.9 all-to-all-start.7
  451.0 14.5 %all-to-all-done.7 = f32[2,8,16,1024]{3,2,0,1:T(8,128)S(1)} async-done(((f32[2,8,16,1024]{3,2,0,1:T(8,128)}), f32[2,8,16,1024]{3,2,0,1:T(8,128)S(1)}, u32[]{:S(2)}, u32[]{:S(2)}) %all-to-all-start.7) | async-done | bytes 1048608 | tf_op jit(solution)/shard_map/all_to_all | solution.py:115
  471.3 5.3 fusion.51
  479.4 3.7 collective-permute-done.2
  484.2 6.2 %fusion.55 = f32[1,128,1024]{2,0,1:T(1,128)} fusion(f32[1,247,1024]{2,0,1:T(1,128)S(1)} %broadcast_in_dim.20, f32[120,1,1024]{2,0,1:T(8,128)S(1)} %bitcast.294), kind=kOutput, calls=%fused_computation.106 | convolution fusion | flops 188743680 | bytes 2027520 | tf_op jit(solution)/shard_map/conv_general_dilated | solution.py:27
  492.9 13.3 %fusion.276 = f32[128,8192]{1,0:T(8,128)} fusion(bf16[128,1024]{1,0:T(8,128)(2,1)S(1)} %get-tuple-element.49, bf16[8192,1024]{1,0:T(8,128)(2,1)} %param.10), kind=kOutput, calls=%fused_computation.310 | convolution fusion | flops 2147483648 | bytes 21233664 | tf_op jit(solution)/shard_map/dot_general | solution.py:152
  508.8 3.7 fusion.14
  514.6 39.4 %psum.15 = bf16[7,3072]{1,0:T(8,128)(2,1)S(1)} all-reduce(bf16[7,3072]{1,0:T(8,128)(2,1)S(1)} %rev.15), channel_id=1, replica_groups=mesh['seq'=8,'tensor'=4] {'seq'}, use_global_device_ids=true, to_apply=%region_2.3 | all-reduce | flops 21504 | bytes 86016 | tf_op jit(solution)/shard_map/psum | solution.py:195
  562.9 35.2 %reduce-scatter.2.cloned.1.call-done = f32[128,2048]{1,0:T(8,128)} async-done(((f32[128,8192]{1,0:T(8,128)}), f32[128,2048]{1,0:T(8,128)}) %reduce-scatter.2.cloned.1.call-update) | async-done | bytes 1048592 | tf_op jit(solution)/shard_map/reduce_scatter | solution.py:155
  (156 shorter events, 124.3 us)
Async XLA Ops:
  7.2 8.0 %copy-start.15 = (f32[7,3,1024]{2,0,1:T(8,128)S(1)}, f32[7,3,1024]{2,0,1:T(8,128)}, u32[]{:S(2)}) copy-start(f32[7,3,1024]{2,0,1:T(8,128)} %param.7) | copy-start | bytes 258052
  7.2 27.7 %all-gather.2.cloned.1.call-start = ((), (), s32[]{:S(2)}) async-start(), calls=%async_computation.10 | async-start | bytes 2621440 | tf_op jit(solution)/shard_map/all_gather | solution.py:158
  8.7 7.1 %collective-permute-start = (bf16[6,3072]{1,0:T(8,128)(2,1)S(1)}, bf16[6,3072]{1,0:T(8,128)(2,1)S(1)}, u32[]{:S(2)}, u32[]{:S(2)}) collective-permute-start(bf16[6,3072]{1,0:T(8,128)(2,1)S(1)} %bitcast.300), channel_id=1, source_target_pairs={{0,4},{4,8},{8,12},{12,16},{16,20},{20,24},{24,28},{1,5},{5,9},{9,... | collective-permute-start | bytes 110600 | tf_op jit(solution)/shard_map/ppermute | solution.py:14
  17.5 0.9 copy-start.7
  17.6 0.9 copy-start.17
  23.4 21.3 %copy-start = (f32[128,3072]{1,0:T(8,128)}, f32[128,3072]{1,0:T(8,128)S(1)}, u32[]{:S(2)}) copy-start(f32[128,3072]{1,0:T(8,128)S(1)} %slice_bitcast_fusion) | copy-start | bytes 4718596
  23.4 24.7 %copy-start.13 = (f32[120,1024]{1,0:T(8,128)S(1)}, f32[120,1024]{1,0:T(8,128)}, u32[]{:S(2)}) copy-start(f32[120,1024]{1,0:T(8,128)} %param.8) | copy-start | bytes 1474564
  44.7 9.4 %collective-permute-start.1 = (bf16[119,1024]{1,0:T(8,128)(2,1)S(1)}, bf16[119,1024]{1,0:T(8,128)(2,1)S(1)}, u32[]{:S(2)}, u32[]{:S(2)}) collective-permute-start(bf16[119,1024]{1,0:T(8,128)(2,1)S(1)} %slice.165), channel_id=1, source_target_pairs={{0,4},{4,8},{8,12},{12,16},{16,20},{20,24},{24,28},{1,5},{5,9},{9,... | collective-permute-start | bytes 731144 | tf_op jit(solution)/shard_map/ppermute | solution.py:14
  48.4 19.2 %all-to-all-start.4 = ((f32[1,8,16,1024]{3,2,0,1:T(8,128)}), f32[1,8,16,1024]{3,2,0,1:T(8,128)S(1)}, u32[]{:S(2)}, u32[]{:S(2)}) async-start(f32[1,8,16,1024]{3,2,0,1:T(8,128)} %bitcast.49), calls=%async_computation.5 | async-start | bytes 1048576 | tf_op jit(solution)/shard_map/all_to_all | solution.py:51
  54.9 5.4 copy-start.10
  55.0 5.5 copy-start.12
  67.6 29.9 %all-to-all-start = ((f32[2,8,16,1024]{3,2,0,1:T(8,128)}), f32[2,8,16,1024]{3,2,0,1:T(8,128)S(1)}, u32[]{:S(2)}, u32[]{:S(2)}) async-start(f32[2,8,16,1024]{3,2,0,1:T(8,128)} %copy.124), calls=%async_computation | async-start | bytes 2097152 | tf_op jit(solution)/shard_map/all_to_all | solution.py:51
  97.5 52.1 %all-to-all-start.5 = ((f32[2,1,16,16,1024]{4,3,1,0,2:T(8,128)}), f32[2,1,16,16,1024]{4,3,1,0,2:T(8,128)S(1)}, u32[]{:S(2)}, u32[]{:S(2)}) async-start(f32[2,1,16,16,1024]{4,3,1,0,2:T(8,128)} %copy.142), calls=%async_computation.6 | async-start | bytes 4194304 | tf_op jit(solution)/shard_map/all_to_all | solution.py:73
  149.5 97.1 %all-to-all-start.1 = ((f32[2,2,16,16,1024]{4,3,1,0,2:T(8,128)}), f32[2,2,16,16,1024]{4,3,1,0,2:T(8,128)}, u32[]{:S(2)}, u32[]{:S(2)}) async-start(f32[2,2,16,16,1024]{4,3,1,0,2:T(8,128)} %copy.127), calls=%async_computation.1 | async-start | bytes 8388608 | tf_op jit(solution)/shard_map/all_to_all | solution.py:73
  261.2 3.7 copy-start.5
  261.2 3.7 copy-start.6
  286.4 97.1 %all-to-all-start.6 = ((f32[2,2,2,128,1024]{4,2,1,0,3:T(2,128)}), f32[2,2,2,128,1024]{4,2,1,0,3:T(2,128)}, u32[]{:S(2)}, u32[]{:S(2)}) async-start(f32[2,2,2,128,1024]{4,2,1,0,3:T(2,128)} %copy.150), calls=%async_computation.7 | async-start | bytes 8388608 | tf_op jit(solution)/shard_map/all_to_all | solution.py:107
  383.5 52.2 %all-to-all-start.2 = ((f32[2,1,2,128,1024]{4,2,1,0,3:T(2,128)}), f32[2,1,2,128,1024]{4,2,1,0,3:T(2,128)S(1)}, u32[]{:S(2)}, u32[]{:S(2)}) async-start(f32[2,1,2,128,1024]{4,2,1,0,3:T(2,128)} %copy.135), calls=%async_computation.2 | async-start | bytes 4194304 | tf_op jit(solution)/shard_map/all_to_all | solution.py:107
  408.6 3.0 copy-start.2
  435.7 29.8 %all-to-all-start.7 = ((f32[2,8,16,1024]{3,2,0,1:T(8,128)}), f32[2,8,16,1024]{3,2,0,1:T(8,128)S(1)}, u32[]{:S(2)}, u32[]{:S(2)}) async-start(f32[2,8,16,1024]{3,2,0,1:T(8,128)} %copy.154), calls=%async_computation.8 | async-start | bytes 2097152 | tf_op jit(solution)/shard_map/all_to_all | solution.py:115
  449.9 21.3 %copy-start.11 = (f32[1,247,1024]{2,0,1:T(1,128)S(1)}, f32[1,247,1024]{2,0,1:T(1,128)}, u32[]{:S(2)}) copy-start(f32[1,247,1024]{2,0,1:T(1,128)} %copy-done.10) | copy-start | bytes 3035140
  465.5 11.1 %copy-start.3 = (f32[2,8,16,1024]{3,2,0,1:T(8,128)}, f32[2,8,16,1024]{3,2,0,1:T(8,128)S(1)}, u32[]{:S(2)}) copy-start(f32[2,8,16,1024]{3,2,0,1:T(8,128)S(1)} %all-to-all-done.7) | copy-start | bytes 3145732
  465.5 24.9 %all-to-all-start.3 = ((f32[1,8,16,1024]{3,2,0,1:T(8,128)}), f32[1,8,16,1024]{3,2,0,1:T(8,128)S(1)}, u32[]{:S(2)}, u32[]{:S(2)}) async-start(f32[1,8,16,1024]{3,2,0,1:T(8,128)} %copy.139), calls=%async_computation.3 | async-start | bytes 1048576 | tf_op jit(solution)/shard_map/all_to_all | solution.py:115
  469.1 85.5 %all-reduce.2.cloned.1.call-start = ((), (), s32[]{:S(2)}) async-start(), calls=%async_computation.11 | async-start | bytes 491520 | tf_op jit(solution)/shard_map/psum | solution.py:194
  470.0 13.1 %collective-permute-start.2 = (bf16[119,1024]{1,0:T(8,128)(2,1)}, bf16[119,1024]{1,0:T(8,128)(2,1)S(1)}, u32[]{:S(2)}, u32[]{:S(2)}) collective-permute-start(bf16[119,1024]{1,0:T(8,128)(2,1)} %slice.164), channel_id=1, source_target_pairs={{4,0},{8,4},{12,8},{16,12},{20,16},{24,20},{28,24},{5,1},{9,5},{13... | collective-permute-start | bytes 731144 | tf_op jit(solution)/shard_map/ppermute | solution.py:14
  479.3 118.9 %reduce-scatter.2.cloned.1.call-start = ((), (), s32[]{:S(2)}) async-start(), calls=%async_computation.9 | async-start | bytes 5242880 | tf_op jit(solution)/shard_map/reduce_scatter | solution.py:155
  483.1 1.0 copy-start.14
  484.2 7.0 %copy-start.1 = (f32[128,3072]{1,0:T(8,128)S(1)}, f32[128,3072]{1,0:T(8,128)}, u32[]{:S(2)}) copy-start(f32[128,3072]{1,0:T(8,128)} %copy-done) | copy-start | bytes 4718596
  506.2 1.2 copy-start.4
  507.4 1.3 copy-start.8
  513.3 43.2 %collective-permute-start.3 = (bf16[6,3072]{1,0:T(8,128)(2,1)S(1)}, bf16[6,3072]{1,0:T(8,128)(2,1)S(1)}, u32[]{:S(2)}, u32[]{:S(2)}) collective-permute-start(bf16[6,3072]{1,0:T(8,128)(2,1)S(1)} %slice.166), channel_id=1, source_target_pairs={{4,0},{8,4},{12,8},{16,12},{20,16},{24,20},{28,24},{5,1},{9,5},{13... | collective-permute-start | bytes 110600 | tf_op jit(solution)/shard_map/ppermute | solution.py:14
  558.7 0.9 copy-start.16
  (2 other events, 1.7 us)
Sparse Core Ops, SparseCore 0:
  9.5 25.2 all-gather.1
  479.4 72.5 all-reduce.1
  554.6 43.5 reduce-scatter.1
where the time goes:
time: 616 us; the launch traced here: 607 us
  waiting for transfers between devices  320 us (52%)
  matrix products  98.7 us (16%)
  local copies, waits for them, and re-layouts  77.8 us (13%)
  starting transfers between devices  44.2 us (7%)
  blocking collectives  39.4 us (6%)
  between operations  15.1 us (2%)
  other arithmetic  11.9 us (2%)
    all_to_all x2, waiting for transfers between devices, to_spectrum(): lax.all_to_all(turned, 'seq', split_axis=2, concat_axis=3, tiled=True)  122 us
    all_to_all x2, waiting for transfers between devices, from_spectrum(): lax.all_to_all(turned, 'seq', split_axis=3, concat_axis=2, tiled=True)  106 us
    psum x1, blocking collectives, local(): lax.psum(short_part.astype(jnp.bfloat16), 'seq').astype(jnp.float32)  39.4 us
    reduce_scatter x1, waiting for transfers between devices, local(): lax.psum_scatter(partial_out, 'tensor', scatter_dimension=1, tiled=True)  35.2 us
    all_to_all x2, waiting for transfers between devices, to_spectrum(): lax.all_to_all(signals.reshape(signal_count, devices, stride, channels),...  25.9 us
    conv_general_dilated x6, matrix products, correlate(): lax.conv_general_dilated(signal[None], kernel[:, None, :], (1,), 'VALID',...  22.3 us
    all_to_all x2, waiting for transfers between devices, from_spectrum(): lax.all_to_all(blocks, 'seq', split_axis=1, concat_axis=1, tiled=True)  14.5 us
    dot_general x1, matrix products, local(): lax.dot_general(product, out_weight, (((1,), (1,)), ((), ())), preferred_...  13.3 us
  transfers between devices with their start and end apart: 15, of which 11 were waited for; matrix products, arithmetic and copies ran while one was open for 22% of the time, Pallas kernels for 0%

commit v1 on v0

v1 whole, which is shorter than its diff:
```python
import math
from functools import partial

import jax
import jax.numpy as jnp
import numpy as np
from jax import lax
from jax.experimental import pallas as pl
from jax.experimental.pallas import tpu as pltpu
from jax.sharding import PartitionSpec as P

F32 = jnp.float32
BF16 = jnp.bfloat16
HALO = 8
GROUP = 32
TABLE_LIMIT = 1 << 23


def dot(a, b):
    return lax.dot_general(a, b, (((1,), (0,)), ((), ())), preferred_element_type=F32)


def back_to_time(columns, spectrum):
    contracted = 0 if columns.shape[0] == spectrum.shape[0] and columns.shape[1] != spectrum.shape[0] else 1
    return lax.dot_general(
        columns, spectrum, (((contracted,), (0,)), ((), ())), preferred_element_type=F32
    )


def exchange(value, axis, flip):
    count = lax.axis_size(axis)
    return lax.ppermute(value, axis, [(source, source ^ flip) for source in range(count)])


def shift(value, axis, steps):
    count = lax.axis_size(axis)
    pairs = [(s, s + steps) for s in range(count) if 0 <= s + steps < count]
    return lax.ppermute(value, axis, pairs)


def whole(shape):
    return pl.BlockSpec(shape, lambda *_: (0,) * len(shape))


def bit_reverse(value, bits):
    return sum(((value >> i) & 1) << (bits - 1 - i) for i in range(bits))


def spectral_sizes(tokens, medium_reach):
    need = tokens + -(-(medium_reach - 2) // 2)
    block = 384
    blocks = -(-need // block)
    return blocks * block, block


def dft_tables(tokens, freqs, block):
    period = 4 * freqs
    unit = 2.0 * math.pi / period

    def turned(coarse, fine):
        first = (coarse % period).astype(F32) * unit
        second = (fine % period).astype(F32) * unit
        return (jnp.cos(first) * jnp.cos(second) - jnp.sin(first) * jnp.sin(second)).astype(BF16)

    blocks = freqs // block
    time = jnp.arange(tokens, dtype=jnp.int32)
    base = GROUP * jnp.arange(2 * freqs // GROUP, dtype=jnp.int32)
    within = base % (2 * block)
    first_freq = base // (2 * block) * block + within % block
    quarter = jnp.where(within >= block, freqs, 0)
    coarse = 2 * first_freq[:, None] * time[None, :] + (period - quarter)[:, None]
    inner = jnp.arange(GROUP, dtype=jnp.int32)
    fine = (2 * inner[:, None] + 1) * time[None, :]
    rows = turned(coarse[:, None, :], fine[None, :, :]).reshape(blocks, 2 * block, tokens)
    if rows.size > TABLE_LIMIT:
        return rows, rows

    column = jnp.arange(2 * block, dtype=jnp.int32)
    freq = jnp.arange(blocks, dtype=jnp.int32)[:, None] * block + column[None, :] % block
    odd = 2 * freq + 1
    offset = jnp.where(column >= block, freqs, 0)
    start = GROUP * jnp.arange(tokens // GROUP, dtype=jnp.int32)
    coarse = odd[:, None, :] * start[None, :, None] + (period - offset)[None, None, :]
    fine = odd[:, None, :] * inner[None, :, None]
    columns = turned(coarse[:, :, None, :], fine[:, None, :, :]).reshape(blocks, tokens, 2 * block)
    return rows, columns


def pack_kernel(x_ref, filter_ref, out_ref):
    parts, rows, width = out_ref.shape
    length = rows // 3
    for j in range(parts):
        lanes = slice(j * width, (j + 1) * width)
        out_ref[j, 0:length, :] = x_ref[1, :, lanes]
        out_ref[j, length : 2 * length, :] = x_ref[2, :, lanes]
        out_ref[j, 2 * length :, :] = filter_ref[:, lanes].astype(BF16)


def query_kernel(x_ref, edge_ref, taps_ref, out_ref, ext):
    length = out_ref.shape[0]
    reach = taps_ref.shape[0]
    ext[0:HALO, :] = edge_ref[...].astype(F32)
    ext[HALO:, :] = x_ref[0].astype(F32)
    total = taps_ref[0:1, :] * ext[HALO : HALO + length, :]
    for i in range(1, reach):
        total = total + taps_ref[i : i + 1, :] * ext[HALO - i : HALO - i + length, :]
    out_ref[...] = total


def grad_first_kernel(_, x0_ref, x1_ref, w_ref, out_ref, *, per):
    step = pl.program_id(0)

    @pl.when(step == 0)
    def _():
        out_ref[...] = jnp.zeros_like(out_ref)

    @pl.when(step < per)
    def _():
        out_ref[...] += dot(x0_ref[...], w_ref[...])

    @pl.when(step >= per)
    def _():
        out_ref[...] += dot(x1_ref[...], w_ref[...])


def grad_second_kernel(_, x0_ref, x1_ref, w_ref, acc_ref, query_ref, out_ref, sent_ref, *, per):
    step = pl.program_id(0)

    @pl.when(step == 0)
    def _():
        out_ref[...] = acc_ref[...]

    @pl.when(step < per)
    def _():
        out_ref[...] += dot(x0_ref[...], w_ref[...])

    @pl.when(step >= per)
    def _():
        out_ref[...] += dot(x1_ref[...], w_ref[...])

    @pl.when(step == 2 * per - 1)
    def _():
        parts, _, width = sent_ref.shape
        for j in range(parts):
            lanes = slice(j * width, (j + 1) * width)
            sent_ref[j] = (out_ref[:, lanes] * query_ref[:, lanes]).astype(BF16)


def product_grad_of(x0, x1, weight, shards, acc=None, query=None, parts=None):
    length, features = x0.shape
    channels = weight.shape[1]
    deep = math.gcd(features, 1024)
    per = features // deep
    in_specs = [
        pl.BlockSpec((length, deep), lambda k, s: (0, jnp.minimum(k, per - 1))),
        pl.BlockSpec((length, deep), lambda k, s: (0, jnp.maximum(k - per, 0))),
        pl.BlockSpec((deep, channels), lambda k, s: (s[k // per] * per + k % per, 0)),
    ]
    full = whole((length, channels))
    if acc is None:
        return pl.pallas_call(
            partial(grad_first_kernel, per=per),
            grid_spec=pltpu.PrefetchScalarGridSpec(
                num_scalar_prefetch=1, grid=(2 * per,), in_specs=in_specs, out_specs=full
            ),
            out_shape=jax.ShapeDtypeStruct((length, channels), F32),
            name="grad_first",
        )(shards, x0, x1, weight)
    width = channels // parts
    return pl.pallas_call(
        partial(grad_second_kernel, per=per),
        grid_spec=pltpu.PrefetchScalarGridSpec(
            num_scalar_prefetch=1,
            grid=(2 * per,),
            in_specs=in_specs + [full, full],
            out_specs=[full, pl.BlockSpec((parts, length, width), lambda k, s: (0, 1, 0))],
        ),
        out_shape=[
            jax.ShapeDtypeStruct((length, channels), F32),
            jax.ShapeDtypeStruct((parts, 2 * length, width), BF16),
        ],
        name="grad_second",
    )(shards, x0, x1, weight, acc, query)


def forward_kernel(
    got_ref, taps_ref, medium_ref, rows_ref, columns_ref, _,
    out_ref, key_ref, value_ref, a_ref, m_ref, h_ref,
    ext, signals, medium, acc, *, length, freqs,
):
    step = pl.program_id(0)
    parts, _, width = got_ref.shape
    reach = taps_ref.shape[0]
    block = rows_ref.shape[1] // 2

    @pl.when(step == 0)
    def _():
        ext[:, 0:HALO, :] = jnp.zeros((2, HALO, width), F32)
        for s in range(parts):
            here = slice(HALO + s * length, HALO + (s + 1) * length)
            ext[0, here, :] = got_ref[s, 0:length, :].astype(F32)
            ext[1, here, :] = got_ref[s, length : 2 * length, :].astype(F32)
        for s in range(parts):
            begin = HALO + s * length
            here = slice(s * length, (s + 1) * length)
            key = taps_ref[0, 0:1, :] * ext[0, begin : begin + length, :]
            value = taps_ref[0, 1:2, :] * ext[1, begin : begin + length, :]
            for i in range(1, reach):
                key = key + taps_ref[i, 0:1, :] * ext[0, begin - i : begin - i + length, :]
                value = value + taps_ref[i, 1:2, :] * ext[1, begin - i : begin - i + length, :]
            key_ref[here, :] = key
            value_ref[here, :] = value
            signals[here, 0:width] = (key * value).astype(BF16)
            signals[here, width : 2 * width] = got_ref[s, 2 * length : 3 * length, :]
        medium[...] = jnp.zeros_like(medium)
        medium[0 : medium_ref.shape[0], :] = medium_ref[...].astype(BF16)
        acc[...] = jnp.zeros_like(acc)

    rows = rows_ref[0]
    spectra = dot(rows, signals[...])
    m = dot(rows[:, 0 : medium.shape[0]], medium[...])
    a = spectra[:, 0:width]
    h = spectra[:, width : 2 * width]
    a_ref[0] = a
    m_ref[0] = m
    h_ref[0] = h
    ac, as_, mc, ms = (a[:block], a[block:], m[:block], m[block:])
    hc, hs = (h[:block], h[block:])
    xc = ac * mc - as_ * ms
    xs = ac * ms + as_ * mc
    y = jnp.concatenate([xc * hc - xs * hs, xc * hs + xs * hc], 0).astype(BF16)
    acc[...] += back_to_time(columns_ref[0], y)

    @pl.when(step == pl.num_programs(0) - 1)
    def _():
        for s in range(parts):
            out_ref[s] = (acc[s * length : (s + 1) * length, :] * (1.0 / freqs)).astype(BF16)


def forward_call(got, taps, medium_taps, rows, columns, sent, freqs):
    parts, tall, width = got.shape
    length = tall // 3
    blocks, double, tokens = rows.shape
    padded = -(-medium_taps.shape[0] // 128) * 128
    per_block = pl.BlockSpec((1, double, width), lambda j: (j, 0, 0))
    spectrum = jax.ShapeDtypeStruct((blocks, double, width), F32)
    timed = jax.ShapeDtypeStruct((tokens, width), F32)
    return pl.pallas_call(
        partial(forward_kernel, length=length, freqs=freqs),
        grid=(blocks,),
        in_specs=[
            whole(got.shape),
            whole(taps.shape),
            whole(medium_taps.shape),
            pl.BlockSpec((1, double, tokens), lambda j: (j, 0, 0)),
            pl.BlockSpec((1,) + columns.shape[1:], lambda j: (j, 0, 0)),
            pl.BlockSpec(memory_space=pl.ANY),
        ],
        out_specs=[
            pl.BlockSpec((parts, length, width), lambda j: (0, 0, 0)),
            whole((tokens, width)),
            whole((tokens, width)),
            per_block,
            per_block,
            per_block,
        ],
        out_shape=[jax.ShapeDtypeStruct(sent.shape, BF16), timed, timed, spectrum, spectrum, spectrum],
        scratch_shapes=[
            pltpu.VMEM((2, tokens + HALO, width), F32),
            pltpu.VMEM((tokens, 2 * width), BF16),
            pltpu.VMEM((padded, width), BF16),
            pltpu.VMEM((tokens, width), F32),
        ],
        input_output_aliases={5: 0},
        name="forward_spectral",
    )(got, taps, medium_taps, rows, columns, sent)


def backward_kernel(
    got_ref, grads_ref, taps_ref, key_ref, value_ref, a_ref, m_ref, h_ref, rows_ref, columns_ref,
    out_ref, small_ref,
    ext, after, signal, acc, tap_acc, *, length, freqs, scale, medium_reach,
):
    step = pl.program_id(0)
    parts, _, width = got_ref.shape
    reach = taps_ref.shape[0]
    block = rows_ref.shape[1] // 2
    tokens = signal.shape[0]

    @pl.when(step == 0)
    def _():
        for s in range(parts):
            signal[s * length : (s + 1) * length, :] = grads_ref[s]
        acc[...] = jnp.zeros_like(acc)
        tap_acc[...] = jnp.zeros_like(tap_acc)

    g = dot(rows_ref[0], signal[...])
    a, m, h = (a_ref[0], m_ref[0], h_ref[0])
    ac, as_, mc, ms = (a[:block], a[block:], m[:block], m[block:])
    hc, hs, gc, gs = (h[:block], h[block:], g[:block], g[block:])
    uc = hc * gc + hs * gs
    us = hc * gs - hs * gc
    xc = ac * mc - as_ * ms
    xs = ac * ms + as_ * mc
    filter_part = jnp.concatenate([xc * gc + xs * gs, xc * gs - xs * gc], 0)
    gated_part = jnp.concatenate([mc * uc + ms * us, mc * us - ms * uc], 0)
    taps_part = jnp.concatenate([ac * uc + as_ * us, ac * us - as_ * uc], 0)
    both = jnp.concatenate([filter_part, gated_part], 1).astype(BF16)
    columns = columns_ref[0]
    acc[...] += back_to_time(columns, both)
    kept = tap_acc.shape[0]
    first = columns[0:kept, :] if columns.shape[0] == tokens else columns[:, 0:kept]
    tap_acc[...] += back_to_time(first, taps_part.astype(BF16))

    @pl.when(step == pl.num_programs(0) - 1)
    def _():
        inverse = 1.0 / freqs
        small_ref[...] = jnp.zeros_like(small_ref)
        small_ref[0:medium_reach, :] = tap_acc[0:medium_reach, :] * (inverse * scale)
        ext[:, 0:HALO, :] = jnp.zeros((2, HALO, width), F32)
        after[:, tokens : tokens + HALO, :] = jnp.zeros((2, HALO, width), F32)
        for s in range(parts):
            here = slice(s * length, (s + 1) * length)
            there = slice(HALO + s * length, HALO + (s + 1) * length)
            out_ref[s, 2 * length : 3 * length, :] = (acc[here, 0:width] * (inverse * scale)).astype(BF16)
            gated = acc[here, width : 2 * width] * inverse
            after[0, here, :] = gated * value_ref[here, :]
            after[1, here, :] = gated * key_ref[here, :]
            ext[0, there, :] = got_ref[s, 0:length, :].astype(F32)
            ext[1, there, :] = got_ref[s, length : 2 * length, :].astype(F32)
        for j in range(2):
            sums = [jnp.zeros((8, width), F32) for _ in range(reach)]
            for s in range(parts):
                begin = s * length
                own = after[j, begin : begin + length, :]
                total = taps_ref[0, j : j + 1, :] * own
                for i in range(reach):
                    if i:
                        total = total + taps_ref[i, j : j + 1, :] * after[j, begin + i : begin + i + length, :]
                    moved = ext[j, HALO + begin - i : HALO + begin - i + length, :]
                    sums[i] = sums[i] + jnp.sum((moved * own).reshape(length // 8, 8, width), 0)
                out_ref[s, j * length : (j + 1) * length, :] = total.astype(BF16)
            for i in range(reach):
                row = medium_reach + j * reach + i
                small_ref[row : row + 1, :] = jnp.sum(sums[i], 0, keepdims=True) * scale


def backward_call(got, grads, taps, key, value, spectra, rows, columns, freqs, scale, medium_reach):
    parts, tall, width = got.shape
    length = tall // 3
    reach = taps.shape[0]
    blocks, double, tokens = rows.shape
    padded = -(-medium_reach // 128) * 128
    small = -(-(medium_reach + 2 * reach) // 16) * 16
    per_block = pl.BlockSpec((1, double, width), lambda j: (j, 0, 0))
    return pl.pallas_call(
        partial(backward_kernel, length=length, freqs=freqs, scale=scale, medium_reach=medium_reach),
        grid=(blocks,),
        in_specs=[
            whole(got.shape),
            pl.BlockSpec((parts, length, width), lambda j: (0, 1, 0)),
            whole(taps.shape),
            whole((tokens, width)),
            whole((tokens, width)),
            per_block,
            per_block,
            per_block,
            pl.BlockSpec((1, double, tokens), lambda j: (j, 0, 0)),
            pl.BlockSpec((1,) + columns.shape[1:], lambda j: (j, 0, 0)),
        ],
        out_specs=[whole(got.shape), whole((small, width))],
        out_shape=[
            jax.ShapeDtypeStruct(got.shape, BF16),
            jax.ShapeDtypeStruct((small, width), F32),
        ],
        scratch_shapes=[
            pltpu.VMEM((2, tokens + HALO, width), F32),
            pltpu.VMEM((2, tokens + HALO, width), F32),
            pltpu.VMEM((tokens, width), BF16),
            pltpu.VMEM((tokens, 2 * width), F32),
            pltpu.VMEM((padded, width), F32),
        ],
        name="backward_spectral",
    )(got, grads, taps, key, value, *spectra, rows, columns)


def product_kernel(got_ref, query_ref, grad_ref, x_ref, edge_ref, product_ref, query_grad_ref, taps_ref, ext):
    parts, length, width = got_ref.shape
    reach = taps_ref.shape[0] - 1
    for j in range(parts):
        lanes = slice(j * width, (j + 1) * width)
        convolved = got_ref[j].astype(F32)
        product_ref[:, lanes] = (query_ref[:, lanes] * convolved).astype(BF16)
        query_grad_ref[:, lanes] = grad_ref[:, lanes] * convolved
    ext[0:HALO, :] = edge_ref[...].astype(F32)
    ext[HALO:, :] = x_ref[0].astype(F32)
    own = query_grad_ref[...]
    taps_ref[...] = jnp.zeros_like(taps_ref)
    for i in range(reach):
        moved = ext[HALO - i : HALO - i + length, :]
        taps_ref[i : i + 1, :] = jnp.sum(moved * own, 0, keepdims=True)


def project_kernel(_, product_ref, w_ref, out_ref):
    out_ref[...] = lax.dot_general(
        product_ref[...], w_ref[...], (((1,), (1,)), ((), ())), preferred_element_type=F32
    ).astype(out_ref.dtype)


def project(product, weight, shard, features, dtype):
    length, channels = product.shape
    deep = math.gcd(features, 1024)
    per = features // deep
    return pl.pallas_call(
        project_kernel,
        grid_spec=pltpu.PrefetchScalarGridSpec(
            num_scalar_prefetch=1,
            grid=(per,),
            in_specs=[
                whole((length, channels)),
                pl.BlockSpec((deep, channels), lambda k, s: (s[0] * per + k, 0)),
            ],
            out_specs=pl.BlockSpec((length, deep), lambda k, s: (0, k)),
        ),
        out_shape=jax.ShapeDtypeStruct((length, features), dtype),
        name="project",
    )(shard, product, weight)


def finish_kernel(
    where_ref, got_ref, query_grad_ref, next_ref, taps_ref, small_ref, query_short_ref,
    input_grad_ref, filter_ref, medium_ref, short_ref, ext, *, scale,
):
    parts, rows, width = got_ref.shape
    length = rows // 3
    reach = taps_ref.shape[0]
    medium_reach = medium_ref.shape[0]
    bits = parts.bit_length() - 1
    for j in range(parts):
        lanes = slice(j * width, (j + 1) * width)
        input_grad_ref[1, :, lanes] = got_ref[j, 0:length, :]
        input_grad_ref[2, :, lanes] = got_ref[j, length : 2 * length, :]
        filter_ref[:, lanes] = got_ref[j, 2 * length :, :].astype(F32)
        small = small_ref[jnp.bitwise_xor(where_ref[0], bit_reverse(j, bits))].astype(F32)
        medium_ref[:, lanes] = small[0:medium_reach, :]
        short_ref[1, :, lanes] = small[medium_reach : medium_reach + reach, :]
        short_ref[2, :, lanes] = small[medium_reach + reach : medium_reach + 2 * reach, :]
    short_ref[0] = query_short_ref[0:reach, :] * scale
    ext[0:length, :] = query_grad_ref[...]
    ext[length:, :] = next_ref[...]
    total = taps_ref[0:1, :] * ext[0:length, :]
    for i in range(1, reach):
        total = total + taps_ref[i : i + 1, :] * ext[i : i + length, :]
    input_grad_ref[0] = total.astype(BF16)


def reshard(value):
    return lax.all_to_all(value, "seq", split_axis=0, concat_axis=0, tiled=True)


def local(inputs, short_taps, medium_taps, long_filter, out_weight, out_cotangent):
    length, groups, channels = inputs.shape
    reach = short_taps.shape[0]
    medium_reach = medium_taps.shape[0]
    parts = lax.axis_size("seq")
    bits = parts.bit_length() - 1
    position = lax.axis_index("seq")
    place = lax.axis_index("tensor")
    features = out_cotangent.shape[1]
    width = channels // parts
    tokens = length * parts
    scale = 1.0 / math.sqrt(tokens)
    freqs, block = spectral_sizes(tokens, medium_reach)

    streams = inputs.transpose(1, 0, 2)
    cot_x = exchange(out_cotangent, "tensor", 2)
    cot_core = exchange(out_cotangent, "tensor", 1)
    query_edge = shift(streams[0, length - HALO :], "seq", 1)

    packed = pl.pallas_call(
        pack_kernel,
        out_shape=jax.ShapeDtypeStruct((parts, 3 * length, width), BF16),
        name="pack",
    )(streams, long_filter)
    got = reshard(packed)

    rows, columns = dft_tables(tokens, freqs, block)
    own_taps = lax.dynamic_slice_in_dim(short_taps[:, 1:], position * width, width, 2)
    own_medium = lax.dynamic_slice_in_dim(medium_taps, position * width, width, 1)
    query_taps = short_taps[:, 0]

    query = pl.pallas_call(
        query_kernel,
        out_shape=jax.ShapeDtypeStruct((length, channels), F32),
        scratch_shapes=[pltpu.VMEM((length + HALO, channels), F32)],
        name="query",
    )(streams, query_edge, query_taps)

    def shard(flip):
        return jnp.bitwise_xor(place, flip).astype(jnp.int32)

    acc = product_grad_of(out_cotangent, cot_core, out_weight, jnp.stack([shard(0), shard(1)]))
    cot_far = exchange(cot_x, "tensor", 1)
    product_grad, sent = product_grad_of(
        cot_x, cot_far, out_weight, jnp.stack([shard(2), shard(3)]), acc, query, parts
    )

    sent, key, value, *spectra = forward_call(
        got, own_taps, own_medium, rows, columns, sent, freqs
    )
    crossed = reshard(sent)

    product, query_grad, query_short = pl.pallas_call(
        product_kernel,
        grid=(1,),
        in_specs=[
            pl.BlockSpec((parts, length, width), lambda j: (0, 0, 0)),
            whole((length, channels)),
            whole((length, channels)),
            whole(streams.shape),
            whole((HALO, channels)),
        ],
        out_specs=[whole((length, channels)), whole((length, channels)), whole((reach + 1, channels))],
        out_shape=[
            jax.ShapeDtypeStruct((length, channels), BF16),
            jax.ShapeDtypeStruct((length, channels), F32),
            jax.ShapeDtypeStruct((reach + 1, channels), F32),
        ],
        scratch_shapes=[pltpu.VMEM((length + HALO, channels), F32)],
        name="product",
    )(crossed, query, product_grad, streams, query_edge)

    far = project(product, out_weight, shard(3)[None], features, BF16)
    far_core = exchange(far, "tensor", 1)
    across = project(product, out_weight, shard(2)[None], features, F32)
    across_sum = exchange((across + far_core.astype(F32)).astype(BF16), "tensor", 2)
    near = project(product, out_weight, shard(1)[None], features, BF16)
    near_core = exchange(near, "tensor", 1)
    own = project(product, out_weight, shard(0)[None], features, F32)

    back, small = backward_call(
        got, crossed, own_taps, key, value, spectra, rows, columns, freqs, scale, medium_reach
    )
    returned = reshard(back)

    gathered = small.astype(BF16)[None]
    for step in range(bits):
        gathered = jnp.concatenate([gathered, exchange(gathered, "seq", parts >> (step + 1))], 0)
    next_grad = shift(query_grad[:HALO].astype(BF16), "seq", -1).astype(F32)
    for step in range(bits):
        query_short = query_short + exchange(query_short, "seq", 1 << step)

    where = jnp.int32(0)
    for i in range(bits):
        where = where + (((position >> i) & 1) << (bits - 1 - i)).astype(jnp.int32)
    vmem = pl.BlockSpec(memory_space=pltpu.VMEM)
    input_grad, filter_grad, medium_grad, short_grad = pl.pallas_call(
        partial(finish_kernel, scale=scale),
        in_specs=[pl.BlockSpec(memory_space=pltpu.SMEM)] + [vmem] * 6,
        out_specs=[vmem] * 4,
        out_shape=[
            jax.ShapeDtypeStruct((groups, length, channels), BF16),
            jax.ShapeDtypeStruct((length, channels), F32),
            jax.ShapeDtypeStruct((medium_reach, channels), F32),
            jax.ShapeDtypeStruct((groups, reach, channels), F32),
        ],
        scratch_shapes=[pltpu.VMEM((length + HALO, channels), F32)],
        name="finish",
    )(where[None], returned, query_grad, next_grad, query_taps, gathered, query_short)

    output = (own + near_core.astype(F32) + across_sum.astype(F32)).astype(BF16)
    return (
        output,
        input_grad.transpose(1, 0, 2),
        filter_grad,
        medium_grad,
        short_grad.transpose(1, 0, 2),
    )


def solution(mesh):
    return jax.shard_map(
        local,
        mesh=mesh,
        in_specs=(
            P("seq", None, "tensor"),
            P(None, None, "tensor"),
            P(None, "tensor"),
            P("seq", "tensor"),
            P(None, "tensor"),
            P("seq", "tensor"),
        ),
        out_specs=(
            P("seq", "tensor"),
            P("seq", None, "tensor"),
            P("seq", "tensor"),
            P(None, "tensor"),
            P(None, None, "tensor"),
        ),
        check_vma=False,
    )
```

time: 616 us -> 161 us (0.26); the launches traced: 607 us -> 160 us
  waiting for transfers between devices: 320 us -> 16.2 us
  matrix products: 98.7 us -> 0 us
  local copies, waits for them, and re-layouts: 77.8 us -> 8.14 us
  Pallas kernels: 0 us -> 63.4 us
  blocking collectives: 39.4 us -> 21.3 us
  starting transfers between devices: 44.2 us -> 28.7 us
  between operations: 15.1 us -> 0.78 us
  other arithmetic: 11.9 us -> 21.2 us
    all_to_all x8 -> x2, waiting for transfers between devices: 268 us -> 0.01 us  [reshard(): return lax.all_to_all(value, 'seq', split_axis=0, concat_axis=0, tiled=True)]
    dot_general x26 -> x0, matrix products: 76.4 us -> none  [the longest x1 13.3 us: local(): lax.dot_general(product, out_weight, (((1,), (1,)), ((), ())), preferred_...]
    pallas_call x0 -> x12, Pallas kernels: none -> 63.4 us  [the longest x4 16.1 us: project(): pl.pallas_call(project_kernel, grid_spec=pltpu.PrefetchScalarGridSpec(num...]
    psum x1 -> x0, blocking collectives: 39.4 us -> none  [local(): lax.psum(short_part.astype(jnp.bfloat16), 'seq').astype(jnp.float32)]
    reduce_scatter x1 -> x0, waiting for transfers between devices: 35.2 us -> none  [local(): lax.psum_scatter(partial_out, 'tensor', scatter_dimension=1, tiled=True)]
    all_to_all x8 -> x2, starting transfers between devices: 33.3 us -> 9.16 us  [reshard(): return lax.all_to_all(value, 'seq', split_axis=0, concat_axis=0, tiled=True)]
    conv_general_dilated x6 -> x0, matrix products: 22.3 us -> none  [correlate(): lax.conv_general_dilated(signal[None], kernel[:, None, :], (1,), 'VALID',...]
    all_to_all x0 -> x1, blocking collectives: none -> 21.3 us  [reshard(): return lax.all_to_all(value, 'seq', split_axis=0, concat_axis=0, tiled=True)]
  transfers between devices with their start and end apart: 15 -> 16, of which waited for: 11 -> 4; matrix products, arithmetic and copies ran while one was open for 22% -> 16% of each run, Pallas kernels for 0% -> 27%
where the time goes in v1:
time: 161 us; the launch traced here: 160 us
  Pallas kernels  63.4 us (39%)
  starting transfers between devices  28.7 us (18%)
  blocking collectives  21.3 us (13%)
  other arithmetic  21.2 us (13%)
  waiting for transfers between devices  16.2 us (10%)
  local copies, waits for them, and re-layouts  8.14 us (5%)
    all_to_all x1, blocking collectives, reshard(): return lax.all_to_all(value, 'seq', split_axis=0, concat_axis=0, tiled=True)  21.3 us
    pallas_call x4, Pallas kernels, project(): pl.pallas_call(project_kernel, grid_spec=pltpu.PrefetchScalarGridSpec(num...  16.1 us
    ppermute x12, waiting for transfers between devices, exchange(): lax.ppermute(value, axis, [(source, source ^ flip) for source in range(co...  16 us
    ppermute x12, starting transfers between devices, exchange(): lax.ppermute(value, axis, [(source, source ^ flip) for source in range(co...  14.9 us
    pallas_call x1, Pallas kernels, backward_call(): pl.pallas_call(partial(backward_kernel, length=length, freqs=freqs, scale...  11.4 us
    pallas_call x1, Pallas kernels, forward_call(): pl.pallas_call(partial(forward_kernel, length=length, freqs=freqs), grid=...  10.5 us
    all_to_all x2, starting transfers between devices, reshard(): return lax.all_to_all(value, 'seq', split_axis=0, concat_axis=0, tiled=True)  9.16 us
    convert_element_type x2, other arithmetic, turned(): (jnp.cos(first) * jnp.cos(second) - jnp.sin(first) * jnp.sin(second)).ast...  8.57 us
  transfers between devices with their start and end apart: 16, of which 4 were waited for; matrix products, arithmetic and copies ran while one was open for 16% of the time, Pallas kernels for 27%

profile of v1, /device:TPU:0, one launch (start us, length us, event | category | flops | bytes accessed | tf_op | source)
XLA Modules:
  0.0 159.8 jit_solution(2578255866818632202)
XLA Ops:
  1.2 2.6 %collective-permute-start = (bf16[128,2048]{1,0:T(8,128)(2,1)}, bf16[128,2048]{1,0:T(8,128)(2,1)}, u32[]{:S(2)}, u32[]{:S(2)}) collective-permute-start(bf16[128,2048]{1,0:T(8,128)(2,1)} %x0_ref.1), channel_id=1, source_target_pairs={{0,2},{1,3},{2,0},{3,1},{4,6},{5,7},{6,4},{7,5},{8,10},{9,11},{10,... | collective-permute-start | bytes 1572872 | tf_op jit(solution)/shard_map/ppermute | solution.py:32
  4.5 3.4 %collective-permute-start.3 = (bf16[8,1024]{1,0:T(8,128)(2,1)S(1)}, bf16[8,1024]{1,0:T(8,128)(2,1)S(1)}, u32[]{:S(2)}, u32[]{:S(2)}) collective-permute-start(bf16[8,1024]{1,0:T(8,128)(2,1)S(1)} %slice_bitcast_fusion.1), channel_id=1, source_target_pairs={{0,4},{4,8},{8,12},{12,16},{16,20},{20,24},{24,28},{1,5},{5,9},{9,... | collective-permute-start | bytes 49160 | tf_op jit(solution)/shard_map/ppermute | solution.py:38
  7.9 2.3 %pack.1 = bf16[8,384,128]{2,1,0:T(8,128)(2,1)} custom-call(bf16[3,128,1024]{2,1,0:T(8,128)(2,1)} %bitcast.21, f32[128,1024]{1,0:T(8,128)} %filter_ref.1), custom_call_target="tpu_custom_call" | custom-call | tf_op jit(solution)/shard_map/pack/pallas_call | solution.py:480
  10.2 4.9 %all-to-all-start = ((bf16[8,384,128]{2,1,0:T(8,128)(2,1)}), bf16[8,384,128]{2,1,0:T(8,128)(2,1)S(1)}, u32[]{:S(2)}, u32[]{:S(2)}) async-start(bf16[8,384,128]{2,1,0:T(8,128)(2,1)} %pack.1), calls=%async_computation | async-start | bytes 1572864 | tf_op jit(solution)/shard_map/all_to_all | solution.py:458
  16.7 1.3 fusion.17
  18.0 2.4 %fusion.13 = (f32[3,32,768]{2,1,0:T(8,128)S(1)}, f32[3,32,768]{2,1,0:T(8,128)S(1)}, f32[3,32,768]{2,1,0:T(8,128)S(1)}, f32[3,32,768]{2,1,0:T(8,128)S(1)}) fusion(s32[768]{0:T(1024)S(1)} %select_subtract_fusion, s32[32]{0:T(128)S(1)} %iota_multiply_fusion, s32[3,768]{1,0:T(4,128)S(1)} %multiply_add_fusion), kind=kLoop, calls=%fused_computation.23 | loop fusion | flops 1400832 | bytes 1192064 | tf_op jit(solution)/shard_map/cos | solution.py:63
  20.4 1.4 slice_bitcast_fusion.taps_ref
  22.4 4.1 %subtract_convert_fusion.1 = bf16[72,32,1024]{2,1,0:T(8,128)(2,1)} fusion(f32[32,1024]{1,0:T(8,128)S(1)} %get-tuple-element.46, f32[72,1024]{1,0:T(8,128)S(1)} %get-tuple-element.44, f32[32,1024]{1,0:T(8,128)S(1)} %get-tuple-element.45, f32[72,1024]{1,0:T(8,128)S(1)} %get-tuple-element.43), kind=kLoop, calls=%fused_computation.1 | loop fusion | flops 9437184 | bytes 5570560 | tf_op jit(solution)/shard_map/convert_element_type | solution.py:63
  27.1 4.5 %subtract_convert_fusion = bf16[3,32,32,768]{3,2,1,0:T(8,128)(2,1)} fusion(f32[3,32,768]{2,1,0:T(8,128)S(1)} %get-tuple-element.41, f32[3,32,768]{2,1,0:T(8,128)S(1)} %get-tuple-element.40, f32[3,32,768]{2,1,0:T(8,128)S(1)} %get-tuple-element.42, f32[3,32,768]{2,1,0:T(8,128)S(1)} %get-tuple-element.39), kind=kLoop, calls=%fused_computation | loop fusion | flops 9437184 | bytes 5898240 | tf_op jit(solution)/shard_map/convert_element_type | solution.py:63
  33.4 2.7 %query.1.query_ref = f32[128,1024]{1,0:T(8,128)} custom-call(bf16[3,128,1024]{2,1,0:T(8,128)(2,1)} %bitcast.22, bf16[8,1024]{1,0:T(8,128)(2,1)} %copy-done.6, f32[7,1024]{1,0:T(8,128)} %slice_bitcast_fusion.taps_ref), custom_call_target="tpu_custom_call" | custom-call | tf_op jit(solution)/shard_map/query/pallas_call | solution.py:492
  36.1 6.7 %grad_first.1.acc_ref = f32[128,1024]{1,0:T(8,128)} custom-call(s32[2]{0:T(128)} %pad_add_fusion.1._, bf16[128,2048]{1,0:T(8,128)(2,1)} %x0_ref.1, bf16[128,2048]{1,0:T(8,128)(2,1)} %collective-permute-done.2.x1_ref, bf16[8192,1024]{1,0:T(8,128)(2,1)} %w_ref.11), custom_call_target="tpu_custom_call" | custom-call | tf_op jit(solution)/shard_map/grad_first/pallas_call | solution.py:161
  43.6 7.2 %grad_second.1 = (f32[128,1024]{1,0:T(8,128)}, bf16[8,256,128]{2,1,0:T(8,128)(2,1)}) custom-call(s32[2]{0:T(128)} %pad_add_fusion._, bf16[128,2048]{1,0:T(8,128)(2,1)} %collective-permute-done.x0_ref, bf16[128,2048]{1,0:T(8,128)(2,1)} %copy-done.5, bf16[8192,1024]{1,0:T(8,128)(2,1)} %w_ref.11, f32[128,1024]{1,0:T(8,128)} %grad_first.1.acc_ref, ...), custom_call_target="tpu_custom_call" | custom-call | tf_op jit(solution)/shard_map/grad_second/pallas_call | solution.py:170
  51.7 10.5 %forward_spectral.1 = (bf16[8,256,128]{2,1,0:T(8,128)(2,1)}, f32[1024,128]{1,0:T(8,128)}, f32[1024,128]{1,0:T(8,128)}, f32[3,768,128]{2,1,0:T(8,128)}, f32[3,768,128]{2,1,0:T(8,128)}, /*index=5*/f32[3,768,128]{2,1,0:T(8,128)}) custom-call(bf16[8,384,128]{2,1,0:T(8,128)(2,1)} %copy-done.1, ...), custom_call_target="tpu_custom_call", output_to_operand_aliasing={{0}: (5, {})} | custom-call | tf_op jit(solution)/shard_map/forward_spectral/pallas_call | solution.py:248
  62.2 21.3 %all_to_all.15.got_ref.grads_ref = bf16[8,256,128]{2,1,0:T(8,128)(2,1)} all-to-all(bf16[8,256,128]{2,1,0:T(8,128)(2,1)} %get-tuple-element.23), channel_id=1, replica_groups=mesh['seq'=8,'tensor'=4] {'seq'}, dimensions={0} | all-to-all | bytes 1048576 | tf_op jit(solution)/shard_map/all_to_all | solution.py:458
  83.4 3.3 %product.1 = (bf16[128,1024]{1,0:T(8,128)(2,1)}, f32[128,1024]{1,0:T(8,128)}, f32[8,1024]{1,0:T(8,128)}) custom-call(bf16[8,256,128]{2,1,0:T(8,128)(2,1)} %all_to_all.15.got_ref.grads_ref, f32[128,1024]{1,0:T(8,128)} %query.1.query_ref, f32[128,1024]{1,0:T(8,128)} %get-tuple-element.24.grad_ref, bf16[3,128,1024]{2,1,0:T(8,128)(2,1)} %bitcast.23, ...), custom_call_target="tpu_custom_call" | custom-call | tf_op jit(solution)/shard_map/product/pallas_call | solution.py:513
  86.7 3.9 %project.7 = bf16[128,2048]{1,0:T(8,128)(2,1)} custom-call(s32[1]{0:T(128)} %bitcast.5._, bf16[128,1024]{1,0:T(8,128)(2,1)} %get-tuple-element.25.product_ref, bf16[8192,1024]{1,0:T(8,128)(2,1)} %w_ref.11), custom_call_target="tpu_custom_call" | custom-call | tf_op jit(solution)/shard_map/project/pallas_call | solution.py:414
  90.6 4.1 %project.6 = f32[128,2048]{1,0:T(8,128)} custom-call(s32[1]{0:T(128)} %bitcast.4._, bf16[128,1024]{1,0:T(8,128)(2,1)} %get-tuple-element.25.product_ref, bf16[8192,1024]{1,0:T(8,128)(2,1)} %w_ref.11), custom_call_target="tpu_custom_call" | custom-call | tf_op jit(solution)/shard_map/project/pallas_call | solution.py:414
  94.7 4.0 %project.5 = bf16[128,2048]{1,0:T(8,128)(2,1)} custom-call(s32[1]{0:T(128)} %bitcast.6._, bf16[128,1024]{1,0:T(8,128)(2,1)} %get-tuple-element.25.product_ref, bf16[8192,1024]{1,0:T(8,128)(2,1)} %w_ref.11), custom_call_target="tpu_custom_call" | custom-call | tf_op jit(solution)/shard_map/project/pallas_call | solution.py:414
  98.7 11.4 %backward_spectral.1 = (bf16[8,384,128]{2,1,0:T(8,128)(2,1)}, f32[144,128]{1,0:T(8,128)}) custom-call(bf16[8,384,128]{2,1,0:T(8,128)(2,1)} %copy-done.1, bf16[8,256,128]{2,1,0:T(8,128)(2,1)} %all_to_all.15.got_ref.grads_ref, f32[7,2,128]{2,1,0:T(2,128)} %copy.14.taps_ref, f32[1024,128]{1,0:T(8,128)} %get-tuple-element.26.key_ref, ...), custom_call_target="tpu_custom_call" | custom-call | tf_op jit(solution)/shard_map/backward_spectral/pallas_call | solution.py:356
  111.8 4.3 %all-to-all-start.2 = ((bf16[8,384,128]{2,1,0:T(8,128)(2,1)}), bf16[8,384,128]{2,1,0:T(8,128)(2,1)S(1)}, u32[]{:S(2)}, u32[]{:S(2)}) async-start(bf16[8,384,128]{2,1,0:T(8,128)(2,1)} %get-tuple-element.31), calls=%async_computation.2 | async-start | bytes 1572864 | tf_op jit(solution)/shard_map/all_to_all | solution.py:458
  116.2 2.0 %add_convert_fusion.1 = bf16[128,2048]{1,0:T(8,128)(2,1)} fusion(f32[128,2048]{1,0:T(8,128)S(1)} %copy-done.2, bf16[128,2048]{1,0:T(8,128)(2,1)} %collective-permute-done.5), kind=kLoop, calls=%fused_computation.3 | loop fusion | flops 786432 | bytes 2097152 | tf_op jit(solution)/shard_map/convert_element_type | solution.py:536
  118.7 2.0 %collective-permute-start.9 = (bf16[2,144,128]{2,1,0:T(8,128)(2,1)S(1)}, bf16[2,144,128]{2,1,0:T(8,128)(2,1)S(1)}, u32[]{:S(2)}, u32[]{:S(2)}) collective-permute-start(bf16[2,144,128]{2,1,0:T(8,128)(2,1)S(1)} %pad_maximum_fusion.2), channel_id=1, source_target_pairs={{0,8},{4,12},{8,0},{12,4},{16,24},{20,28},{24,16},{28,20},{1,9},{5... | collective-permute-start | bytes 221192 | tf_op jit(solution)/shard_map/ppermute | solution.py:32
  120.7 10.3 %collective-permute-done.9 = bf16[2,144,128]{2,1,0:T(8,128)(2,1)S(1)} collective-permute-done((bf16[2,144,128]{2,1,0:T(8,128)(2,1)S(1)}, bf16[2,144,128]{2,1,0:T(8,128)(2,1)S(1)}, u32[]{:S(2)}, u32[]{:S(2)}) %collective-permute-start.9) | collective-permute-done | bytes 73760 | tf_op jit(solution)/shard_map/ppermute | solution.py:32
  131.0 1.7 %collective-permute-start.10 = (bf16[4,144,128]{2,1,0:T(8,128)(2,1)S(1)}, bf16[4,144,128]{2,1,0:T(8,128)(2,1)S(1)}, u32[]{:S(2)}, u32[]{:S(2)}) collective-permute-start(bf16[4,144,128]{2,1,0:T(8,128)(2,1)S(1)} %pad_maximum_fusion.1), channel_id=1, source_target_pairs={{0,4},{4,0},{8,12},{12,8},{16,20},{20,16},{24,28},{28,24},{1,5},{5... | collective-permute-start | bytes 442376 | tf_op jit(solution)/shard_map/ppermute | solution.py:32
  133.1 3.8 %collective-permute-done.11 = f32[8,1024]{1,0:T(8,128)S(1)} collective-permute-done((f32[8,1024]{1,0:T(8,128)S(1)}, f32[8,1024]{1,0:T(8,128)S(1)}, u32[]{:S(2)}, u32[]{:S(2)}) %collective-permute-start.11) | collective-permute-done | bytes 32800 | tf_op jit(solution)/shard_map/ppermute | solution.py:32
  136.9 3.1 %collective-permute-start.12 = (f32[8,1024]{1,0:T(8,128)S(1)}, f32[8,1024]{1,0:T(8,128)S(1)}, u32[]{:S(2)}, u32[]{:S(2)}) collective-permute-start(f32[8,1024]{1,0:T(8,128)S(1)} %add.255), channel_id=1, source_target_pairs={{0,8},{4,12},{8,0},{12,4},{16,24},{20,28},{24,16},{28,20},{1,9},{5... | collective-permute-start | bytes 98312 | tf_op jit(solution)/shard_map/ppermute | solution.py:32
  140.0 1.9 %collective-permute-done.12 = f32[8,1024]{1,0:T(8,128)S(1)} collective-permute-done((f32[8,1024]{1,0:T(8,128)S(1)}, f32[8,1024]{1,0:T(8,128)S(1)}, u32[]{:S(2)}, u32[]{:S(2)}) %collective-permute-start.12) | collective-permute-done | bytes 32800 | tf_op jit(solution)/shard_map/ppermute | solution.py:32
  141.9 3.1 %collective-permute-start.13 = (f32[8,1024]{1,0:T(8,128)S(1)}, f32[8,1024]{1,0:T(8,128)S(1)}, u32[]{:S(2)}, u32[]{:S(2)}) collective-permute-start(f32[8,1024]{1,0:T(8,128)S(1)} %add.256), channel_id=1, source_target_pairs={{0,16},{4,20},{8,24},{12,28},{16,0},{20,4},{24,8},{28,12},{1,17},{... | collective-permute-start | bytes 98312 | tf_op jit(solution)/shard_map/ppermute | solution.py:32
  145.8 1.3 collective-permute-start.7
  147.1 4.1 %project.4 = f32[128,2048]{1,0:T(8,128)} custom-call(s32[1]{0:T(128)} %bitcast._, bf16[128,1024]{1,0:T(8,128)(2,1)} %get-tuple-element.25.product_ref, bf16[8192,1024]{1,0:T(8,128)(2,1)} %w_ref.11), custom_call_target="tpu_custom_call" | custom-call | tf_op jit(solution)/shard_map/project/pallas_call | solution.py:414
  153.4 2.2 %add_convert_fusion = bf16[128,2048]{1,0:T(8,128)(2,1)} fusion(bf16[128,2048]{1,0:T(8,128)(2,1)S(1)} %collective-permute-done.6, f32[128,2048]{1,0:T(8,128)} %project.4, bf16[128,2048]{1,0:T(8,128)(2,1)S(1)} %collective-permute-done.4), kind=kLoop, calls=%fused_computation.2 | loop fusion | flops 1310720 | bytes 2621440 | tf_op jit(solution)/shard_map/convert_element_type | solution.py:571
  156.5 3.3 %finish.1 = (bf16[3,128,1024]{2,1,0:T(8,128)(2,1)}, f32[128,1024]{1,0:T(8,128)}, f32[120,1024]{1,0:T(8,128)}, f32[3,7,1024]{2,1,0:T(8,128)}) custom-call(s32[1]{0:T(128)} %bitcast.9.where_ref, bf16[8,384,128]{2,1,0:T(8,128)(2,1)} %copy-done.3, f32[128,1024]{1,0:T(8,128)} %get-tuple-element.32.query_grad_ref, f32[8,1024]{1,0:T(8,128)} %convert_element_type.109.next_ref, ...), custom_call_target="tpu_custom_call" | custom-call | tf_op jit(solution)/shard_map/finish/pallas_call | solution.py:557
  (60 shorter events, 14.2 us)
Async XLA Ops:
  0.6 21.1 %copy-start = (f32[120,1024]{1,0:T(8,128)S(1)}, f32[120,1024]{1,0:T(8,128)}, u32[]{:S(2)}) copy-start(f32[120,1024]{1,0:T(8,128)} %param.8) | copy-start | bytes 1474564
  0.6 35.4 %collective-permute-start.2 = (bf16[128,2048]{1,0:T(8,128)(2,1)}, bf16[128,2048]{1,0:T(8,128)(2,1)}, u32[]{:S(2)}, u32[]{:S(2)}) collective-permute-start(bf16[128,2048]{1,0:T(8,128)(2,1)} %x0_ref.1), channel_id=1, source_target_pairs={{0,1},{1,0},{2,3},{3,2},{4,5},{5,4},{6,7},{7,6},{8,9},{9,8},{10,11... | collective-permute-start | bytes 1572872 | tf_op jit(solution)/shard_map/ppermute | solution.py:32
  1.2 25.3 %collective-permute-start = (bf16[128,2048]{1,0:T(8,128)(2,1)}, bf16[128,2048]{1,0:T(8,128)(2,1)}, u32[]{:S(2)}, u32[]{:S(2)}) collective-permute-start(bf16[128,2048]{1,0:T(8,128)(2,1)} %x0_ref.1), channel_id=1, source_target_pairs={{0,2},{1,3},{2,0},{3,1},{4,6},{5,7},{6,4},{7,5},{8,10},{9,11},{10,... | collective-permute-start | bytes 1572872 | tf_op jit(solution)/shard_map/ppermute | solution.py:32
  4.5 28.3 %collective-permute-start.3 = (bf16[8,1024]{1,0:T(8,128)(2,1)S(1)}, bf16[8,1024]{1,0:T(8,128)(2,1)S(1)}, u32[]{:S(2)}, u32[]{:S(2)}) collective-permute-start(bf16[8,1024]{1,0:T(8,128)(2,1)S(1)} %slice_bitcast_fusion.1), channel_id=1, source_target_pairs={{0,4},{4,8},{8,12},{12,16},{16,20},{20,24},{24,28},{1,5},{5,9},{9,... | collective-permute-start | bytes 49160 | tf_op jit(solution)/shard_map/ppermute | solution.py:38
  10.2 40.6 %all-to-all-start = ((bf16[8,384,128]{2,1,0:T(8,128)(2,1)}), bf16[8,384,128]{2,1,0:T(8,128)(2,1)S(1)}, u32[]{:S(2)}, u32[]{:S(2)}) async-start(bf16[8,384,128]{2,1,0:T(8,128)(2,1)} %pack.1), calls=%async_computation | async-start | bytes 1572864 | tf_op jit(solution)/shard_map/all_to_all | solution.py:458
  26.5 16.3 %collective-permute-start.1 = (bf16[128,2048]{1,0:T(8,128)(2,1)}, bf16[128,2048]{1,0:T(8,128)(2,1)S(1)}, u32[]{:S(2)}, u32[]{:S(2)}) collective-permute-start(bf16[128,2048]{1,0:T(8,128)(2,1)} %collective-permute-done.x0_ref), channel_id=1, source_target_pairs={{0,1},{1,0},{2,3},{3,2},{4,5},{5,4},{6,7},{7,6},{8,9},{9,8},{10,11... | collective-permute-start | bytes 1572872 | tf_op jit(solution)/shard_map/ppermute | solution.py:32
  32.7 0.6 copy-start.6
  42.8 0.8 copy-start.5
  50.8 0.9 copy-start.1
  90.6 25.5 %collective-permute-start.5 = (bf16[128,2048]{1,0:T(8,128)(2,1)}, bf16[128,2048]{1,0:T(8,128)(2,1)}, u32[]{:S(2)}, u32[]{:S(2)}) collective-permute-start(bf16[128,2048]{1,0:T(8,128)(2,1)} %project.7), channel_id=1, source_target_pairs={{0,1},{1,0},{2,3},{3,2},{4,5},{5,4},{6,7},{7,6},{8,9},{9,8},{10,11... | collective-permute-start | bytes 1572872 | tf_op jit(solution)/shard_map/ppermute | solution.py:32
  98.7 17.4 %copy-start.4 = (bf16[128,2048]{1,0:T(8,128)(2,1)S(1)}, bf16[128,2048]{1,0:T(8,128)(2,1)}, u32[]{:S(2)}) copy-start(bf16[128,2048]{1,0:T(8,128)(2,1)} %project.5) | copy-start | bytes 1572868
  98.7 17.5 %copy-start.2 = (f32[128,2048]{1,0:T(8,128)S(1)}, f32[128,2048]{1,0:T(8,128)}, u32[]{:S(2)}) copy-start(f32[128,2048]{1,0:T(8,128)} %project.6) | copy-start | bytes 3145732
  98.7 34.0 %copy-start.7 = (f32[8,1024]{1,0:T(8,128)S(1)}, f32[8,1024]{1,0:T(8,128)}, u32[]{:S(2)}) copy-start(f32[8,1024]{1,0:T(8,128)} %get-tuple-element.34) | copy-start | bytes 98308
  111.0 7.7 %collective-permute-start.8 = (bf16[1,144,128]{2,1,0:T(8,128)(2,1)S(1)}, bf16[1,144,128]{2,1,0:T(8,128)(2,1)S(1)}, u32[]{:S(2)}, u32[]{:S(2)}) collective-permute-start(bf16[1,144,128]{2,1,0:T(8,128)(2,1)S(1)} %convert_bitcast_fusion), channel_id=1, source_target_pairs={{0,16},{4,20},{8,24},{12,28},{16,0},{20,4},{24,8},{28,12},{1,17},{... | collective-permute-start | bytes 110600 | tf_op jit(solution)/shard_map/ppermute | solution.py:32
  111.8 43.8 %all-to-all-start.2 = ((bf16[8,384,128]{2,1,0:T(8,128)(2,1)}), bf16[8,384,128]{2,1,0:T(8,128)(2,1)S(1)}, u32[]{:S(2)}, u32[]{:S(2)}) async-start(bf16[8,384,128]{2,1,0:T(8,128)(2,1)} %get-tuple-element.31), calls=%async_computation.2 | async-start | bytes 1572864 | tf_op jit(solution)/shard_map/all_to_all | solution.py:458
  116.1 37.3 %collective-permute-start.4 = (bf16[128,2048]{1,0:T(8,128)(2,1)S(1)}, bf16[128,2048]{1,0:T(8,128)(2,1)S(1)}, u32[]{:S(2)}, u32[]{:S(2)}) collective-permute-start(bf16[128,2048]{1,0:T(8,128)(2,1)S(1)} %copy-done.4), channel_id=1, source_target_pairs={{0,1},{1,0},{2,3},{3,2},{4,5},{5,4},{6,7},{7,6},{8,9},{9,8},{10,11... | collective-permute-start | bytes 1572872 | tf_op jit(solution)/shard_map/ppermute | solution.py:32
  118.1 35.3 %collective-permute-start.6 = (bf16[128,2048]{1,0:T(8,128)(2,1)}, bf16[128,2048]{1,0:T(8,128)(2,1)S(1)}, u32[]{:S(2)}, u32[]{:S(2)}) collective-permute-start(bf16[128,2048]{1,0:T(8,128)(2,1)} %add_convert_fusion.1), channel_id=1, source_target_pairs={{0,2},{1,3},{2,0},{3,1},{4,6},{5,7},{6,4},{7,5},{8,10},{9,11},{10,... | collective-permute-start | bytes 1572872 | tf_op jit(solution)/shard_map/ppermute | solution.py:32
  118.7 12.3 %collective-permute-start.9 = (bf16[2,144,128]{2,1,0:T(8,128)(2,1)S(1)}, bf16[2,144,128]{2,1,0:T(8,128)(2,1)S(1)}, u32[]{:S(2)}, u32[]{:S(2)}) collective-permute-start(bf16[2,144,128]{2,1,0:T(8,128)(2,1)S(1)} %pad_maximum_fusion.2), channel_id=1, source_target_pairs={{0,8},{4,12},{8,0},{12,4},{16,24},{20,28},{24,16},{28,20},{1,9},{5... | collective-permute-start | bytes 221192 | tf_op jit(solution)/shard_map/ppermute | solution.py:32
  131.0 21.6 %collective-permute-start.10 = (bf16[4,144,128]{2,1,0:T(8,128)(2,1)S(1)}, bf16[4,144,128]{2,1,0:T(8,128)(2,1)S(1)}, u32[]{:S(2)}, u32[]{:S(2)}) collective-permute-start(bf16[4,144,128]{2,1,0:T(8,128)(2,1)S(1)} %pad_maximum_fusion.1), channel_id=1, source_target_pairs={{0,4},{4,0},{8,12},{12,8},{16,20},{20,16},{24,28},{28,24},{1,5},{5... | collective-permute-start | bytes 442376 | tf_op jit(solution)/shard_map/ppermute | solution.py:32
  132.7 4.2 %collective-permute-start.11 = (f32[8,1024]{1,0:T(8,128)S(1)}, f32[8,1024]{1,0:T(8,128)S(1)}, u32[]{:S(2)}, u32[]{:S(2)}) collective-permute-start(f32[8,1024]{1,0:T(8,128)S(1)} %copy-done.7), channel_id=1, source_target_pairs={{0,4},{4,0},{8,12},{12,8},{16,20},{20,16},{24,28},{28,24},{1,5},{5... | collective-permute-start | bytes 98312 | tf_op jit(solution)/shard_map/ppermute | solution.py:32
  136.9 5.0 %collective-permute-start.12 = (f32[8,1024]{1,0:T(8,128)S(1)}, f32[8,1024]{1,0:T(8,128)S(1)}, u32[]{:S(2)}, u32[]{:S(2)}) collective-permute-start(f32[8,1024]{1,0:T(8,128)S(1)} %add.255), channel_id=1, source_target_pairs={{0,8},{4,12},{8,0},{12,4},{16,24},{20,28},{24,16},{28,20},{1,9},{5... | collective-permute-start | bytes 98312 | tf_op jit(solution)/shard_map/ppermute | solution.py:32
  141.9 10.1 %collective-permute-start.13 = (f32[8,1024]{1,0:T(8,128)S(1)}, f32[8,1024]{1,0:T(8,128)S(1)}, u32[]{:S(2)}, u32[]{:S(2)}) collective-permute-start(f32[8,1024]{1,0:T(8,128)S(1)} %add.256), channel_id=1, source_target_pairs={{0,16},{4,20},{8,24},{12,28},{16,0},{20,4},{24,8},{28,12},{1,17},{... | collective-permute-start | bytes 98312 | tf_op jit(solution)/shard_map/ppermute | solution.py:32
  145.8 5.6 %collective-permute-start.7 = (bf16[8,1024]{1,0:T(8,128)(2,1)S(1)}, bf16[8,1024]{1,0:T(8,128)(2,1)S(1)}, u32[]{:S(2)}, u32[]{:S(2)}) collective-permute-start(bf16[8,1024]{1,0:T(8,128)(2,1)S(1)} %slice.22), channel_id=1, source_target_pairs={{4,0},{8,4},{12,8},{16,12},{20,16},{24,20},{28,24},{5,1},{9,5},{13... | collective-permute-start | bytes 49160 | tf_op jit(solution)/shard_map/ppermute | solution.py:38
  155.6 0.9 copy-start.3

commit v2 on v0

v2 whole, which is shorter than its diff:
```python
import math
from functools import partial

import jax
import jax.numpy as jnp
from jax import lax
from jax.experimental import pallas as pl
from jax.experimental.pallas import tpu as pltpu
from jax.sharding import PartitionSpec as P


F32 = jnp.float32
BF16 = jnp.bfloat16
HALO = 8
GROUP = 32
CHUNK = 512
VMEM_SPECTRAL = 24
TABLE_LIMIT = 1 << 22


def dot(a, b):
    return lax.dot_general(a, b, (((1,), (0,)), ((), ())), preferred_element_type=F32)


def exchange(value, axis, flip):
    count = lax.axis_size(axis)
    return lax.ppermute(value, axis, [(source, source ^ flip) for source in range(count)])


def shift(value, axis, steps):
    count = lax.axis_size(axis)
    pairs = [(s, s + steps) for s in range(count) if 0 <= s + steps < count]
    return lax.ppermute(value, axis, pairs)


def whole(shape):
    return pl.BlockSpec(shape, lambda *_: (0,) * len(shape))


def spectral_sizes(tokens, medium_reach):
    need = tokens + -(-(medium_reach - 2) // 2)
    freqs = -(-need // 384) * 384
    return freqs, 384


def dft_tables(freqs):
    period = 8 * freqs
    unit = 2.0 * math.pi / period
    odd = 2 * jnp.arange(freqs, dtype=jnp.int32) + 1
    start = 2 * GROUP * jnp.arange(freqs // GROUP, dtype=jnp.int32)
    inner = 2 * jnp.arange(GROUP, dtype=jnp.int32) + 1
    first = (start[:, None] * odd[None, :] % period).astype(F32) * unit
    second = (inner[:, None] * odd[None, :] % period).astype(F32) * unit
    fc, fs = jnp.cos(first)[:, None], jnp.sin(first)[:, None]
    sc, ss = jnp.cos(second)[None], jnp.sin(second)[None]
    cosine = (fc * sc - fs * ss).astype(BF16).reshape(freqs, freqs)
    sine = (fs * sc + fc * ss).astype(BF16).reshape(freqs, freqs)
    return cosine, sine


def limit(mebibytes):
    return pltpu.CompilerParams(vmem_limit_bytes=mebibytes << 20)


def pack_kernel(x_ref, filter_ref, out_ref):
    parts, rows, width = out_ref.shape
    length = rows // 3
    for j in range(parts):
        lanes = slice(j * width, (j + 1) * width)
        out_ref[j, 0:length, :] = x_ref[1, :, lanes]
        out_ref[j, length : 2 * length, :] = x_ref[2, :, lanes]
        out_ref[j, 2 * length :, :] = filter_ref[:, lanes].astype(BF16)


def query_kernel(x_ref, edge_ref, taps_ref, out_ref, ext):
    length = out_ref.shape[0]
    reach = taps_ref.shape[1]
    ext[0:HALO, :] = edge_ref[...].astype(F32)
    ext[HALO:, :] = x_ref[0].astype(F32)
    total = taps_ref[0, 0:1, :] * ext[HALO : HALO + length, :]
    for i in range(1, reach):
        total = total + taps_ref[0, i : i + 1, :] * ext[HALO - i : HALO - i + length, :]
    out_ref[...] = total


def weight_chunks(place_ref, weight_ref, buffer, sems, flips, features):
    deep = buffer.shape[1]
    per = features // deep
    copies = []
    for i, flip in enumerate(flips):
        for k in range(per):
            start = jnp.bitwise_xor(place_ref[0], flip) * features + k * deep
            slot = i * per + k
            copies.append(
                pltpu.make_async_copy(
                    weight_ref.at[pl.ds(pl.multiple_of(start, deep), deep), :], buffer.at[slot], sems.at[slot]
                )
            )
    return copies


def chunk_scratch(weight, features, shards):
    deep = math.gcd(features, CHUNK)
    count = shards * (features // deep)
    return [pltpu.VMEM((count, deep, weight.shape[1]), weight.dtype), pltpu.SemaphoreType.DMA((count,))]


def summed(x_refs, copies, buffer, total):
    deep = buffer.shape[1]
    per = len(copies) // len(x_refs)
    for slot, copy in enumerate(copies):
        copy.wait()
        lanes = slice(slot % per * deep, (slot % per + 1) * deep)
        part = dot(x_refs[slot // per][:, lanes], buffer[slot])
        total = part if total is None else total + part
    return total


def grad_first_kernel(place_ref, x0_ref, x1_ref, w_ref, out_ref, buffer, sems, *, flips):
    copies = weight_chunks(place_ref, w_ref, buffer, sems, flips, x0_ref.shape[1])
    for copy in copies:
        copy.start()
    out_ref[...] = summed((x0_ref, x1_ref), copies, buffer, None)


def grad_second_kernel(
    place_ref, x0_ref, x1_ref, w_ref, acc_ref, query_ref, out_ref, sent_ref, buffer, sems, *, flips
):
    copies = weight_chunks(place_ref, w_ref, buffer, sems, flips, x0_ref.shape[1])
    for copy in copies:
        copy.start()
    total = summed((x0_ref, x1_ref), copies, buffer, acc_ref[...])
    out_ref[...] = total
    parts, _, width = sent_ref.shape
    for j in range(parts):
        lanes = slice(j * width, (j + 1) * width)
        sent_ref[j] = (total[:, lanes] * query_ref[:, lanes]).astype(BF16)


def product_grad_of(x0, x1, weight, place, flips, acc=None, query=None, parts=None):
    length, features = x0.shape
    channels = weight.shape[1]
    smem = pl.BlockSpec(memory_space=pltpu.SMEM)
    vmem = pl.BlockSpec(memory_space=pltpu.VMEM)
    in_specs = [smem, vmem, vmem, pl.BlockSpec(memory_space=pltpu.HBM)]
    full = jax.ShapeDtypeStruct((length, channels), F32)
    scratch = chunk_scratch(weight, features, 2)
    if acc is None:
        return pl.pallas_call(
            partial(grad_first_kernel, flips=flips),
            in_specs=in_specs,
            out_specs=vmem,
            out_shape=full,
            scratch_shapes=scratch,
            compiler_params=limit(16),
            name="grad_first",
        )(place, x0, x1, weight)
    width = channels // parts
    return pl.pallas_call(
        partial(grad_second_kernel, flips=flips),
        grid=(1,),
        in_specs=in_specs + [vmem, vmem],
        out_specs=[vmem, pl.BlockSpec((parts, length, width), lambda j: (0, 1, 0))],
        out_shape=[full, jax.ShapeDtypeStruct((parts, 2 * length, width), BF16)],
        scratch_shapes=scratch,
        compiler_params=limit(16),
        name="grad_second",
    )(place, x0, x1, weight, acc, query)


def filtered(taps_ref, stream, ext, begin, length):
    total = taps_ref[stream + 1, 0:1, :] * ext[stream, HALO + begin : HALO + begin + length, :]
    for i in range(1, taps_ref.shape[1]):
        first = HALO + begin - i
        total = total + taps_ref[stream + 1, i : i + 1, :] * ext[stream, first : first + length, :]
    return total


def extend(got_ref, ext):
    parts, rows, width = got_ref.shape
    length = rows // 3
    ext[:, 0:HALO, :] = jnp.zeros((2, HALO, width), F32)
    for s in range(parts):
        here = slice(HALO + s * length, HALO + (s + 1) * length)
        ext[0, here, :] = got_ref[s, 0:length, :].astype(F32)
        ext[1, here, :] = got_ref[s, length : 2 * length, :].astype(F32)


def forward_begin(got_ref, taps_ref, medium_ref, key_ref, value_ref, ext, signals, medium):
    parts, rows, width = got_ref.shape
    length = rows // 3
    extend(got_ref, ext)
    for s in range(parts):
        here = slice(s * length, (s + 1) * length)
        key = filtered(taps_ref, 0, ext, s * length, length)
        value = filtered(taps_ref, 1, ext, s * length, length)
        key_ref[here, :] = key
        value_ref[here, :] = value
        signals[here, 0:width] = (key * value).astype(BF16)
        signals[here, width : 2 * width] = got_ref[s, 2 * length : 3 * length, :]
    medium[...] = jnp.zeros_like(medium)
    medium[0 : medium_ref.shape[0], :] = medium_ref[...].astype(BF16)


def forward_spectra(cosine, sine, signals, medium):
    tokens, double = signals.shape
    width = double // 2
    kept = medium.shape[0]
    both_c = dot(cosine[:, 0:tokens], signals[...])
    both_s = dot(sine[:, 0:tokens], signals[...])
    mc = dot(cosine[:, 0:kept], medium[...])
    ms = dot(sine[:, 0:kept], medium[...])
    ac, hc, as_, hs = (both_c[:, :width], both_c[:, width:], both_s[:, :width], both_s[:, width:])
    xc = ac * mc - as_ * ms
    xs = ac * ms + as_ * mc
    saved = (ac, as_, mc, ms, hc, hs)
    return saved, (xc * hc - xs * hs).astype(BF16), (xc * hs + xs * hc).astype(BF16)


def forward_end(out_ref, acc, freqs):
    parts, length, _ = out_ref.shape
    for s in range(parts):
        first = s * length + 1
        out_ref[s, 0:length, :] = (acc[first : first + length, :] * (1.0 / freqs)).astype(BF16)


def forward_kernel(
    got_ref, taps_ref, medium_ref, cos_ref, sin_ref, cos_across_ref, sin_across_ref, _,
    out_ref, key_ref, value_ref, spectra_ref, ext, signals, medium, acc, *, freqs,
):
    step = pl.program_id(0)

    @pl.when(step == 0)
    def _():
        forward_begin(got_ref, taps_ref, medium_ref, key_ref, value_ref, ext, signals, medium)
        acc[...] = jnp.zeros_like(acc)

    saved, yc, ys = forward_spectra(cos_ref[...], sin_ref[...], signals, medium)
    for i, spectrum in enumerate(saved):
        spectra_ref[i] = spectrum
    rows = acc.shape[0]
    acc[...] += dot(cos_across_ref[0:rows, :], yc) + dot(sin_across_ref[0:rows, :], ys)

    @pl.when(step == pl.num_programs(0) - 1)
    def _():
        forward_end(out_ref, acc, freqs)


def backward_begin(got_ref, grads_ref, delayed, signal, ext):
    parts, rows, _ = got_ref.shape
    length = rows // 3
    delayed[...] = jnp.zeros_like(delayed)
    for s in range(parts):
        delayed[s * length + 1 : (s + 1) * length + 1, :] = grads_ref[s].astype(F32)
    signal[...] = delayed[...].astype(BF16)
    extend(got_ref, ext)


def backward_spectra(cosine, sine, signal, spectra):
    gc = dot(cosine, signal[...])
    gs = dot(sine, signal[...])
    ac, as_, mc, ms, hc, hs = spectra
    uc = hc * gc + hs * gs
    us = hc * gs - hs * gc
    xc = ac * mc - as_ * ms
    xs = ac * ms + as_ * mc
    both_c = jnp.concatenate([xc * gc + xs * gs, mc * uc + ms * us], 1).astype(BF16)
    both_s = jnp.concatenate([xc * gs - xs * gc, mc * us - ms * uc], 1).astype(BF16)
    return both_c, both_s, (ac * uc + as_ * us).astype(BF16), (ac * us - as_ * uc).astype(BF16)


def backward_end(
    taps_ref, query_short_ref, key_ref, value_ref, out_ref, small_ref, ext, after, acc, tap_acc, freqs, scale, medium_reach
):
    parts, _, width = out_ref.shape
    length = (ext.shape[1] - HALO) // parts
    tokens = parts * length
    reach = taps_ref.shape[1]
    inverse = 1.0 / freqs
    small_ref[...] = jnp.zeros_like(small_ref)
    small_ref[0:medium_reach, :] = tap_acc[0:medium_reach, :] * (inverse * scale)
    after[:, tokens : tokens + HALO, :] = jnp.zeros((2, HALO, width), F32)
    for s in range(parts):
        here = slice(s * length, (s + 1) * length)
        out_ref[s, 2 * length : 3 * length, :] = (acc[here, 0:width] * (inverse * scale)).astype(BF16)
        gated = acc[here, width : 2 * width] * inverse
        after[0, here, :] = gated * value_ref[here, :]
        after[1, here, :] = gated * key_ref[here, :]
    for j in range(2):
        sums = [jnp.zeros((8, width), F32) for _ in range(reach)]
        for s in range(parts):
            begin = s * length
            own = after[j, begin : begin + length, :]
            total = taps_ref[j + 1, 0:1, :] * own
            for i in range(reach):
                if i:
                    total = total + taps_ref[j + 1, i : i + 1, :] * after[j, begin + i : begin + i + length, :]
                moved = ext[j, HALO + begin - i : HALO + begin - i + length, :]
                sums[i] = sums[i] + jnp.sum((moved * own).reshape(length // 8, 8, width), 0)
            out_ref[s, j * length : (j + 1) * length, :] = total.astype(BF16)
        for i in range(reach):
            row = medium_reach + j * reach + i
            small_ref[row : row + 1, :] = jnp.sum(sums[i], 0, keepdims=True) * scale
    row = medium_reach + 2 * reach
    small_ref[row : row + query_short_ref.shape[0], :] = query_short_ref[...]
    small = small_ref[...].astype(BF16)
    for s in range(parts):
        out_ref[s, 3 * length :, :] = small


def backward_kernel(
    got_ref, grads_ref, taps_ref, query_short_ref, key_ref, value_ref, spectra_ref,
    cos_ref, sin_ref, cos_across_ref, sin_across_ref,
    out_ref, small, delayed, signal, ext, after, acc, tap_acc, *, freqs, scale, medium_reach,
):
    step = pl.program_id(0)

    @pl.when(step == 0)
    def _():
        backward_begin(got_ref, grads_ref, delayed, signal, ext)
        acc[...] = jnp.zeros_like(acc)
        tap_acc[...] = jnp.zeros_like(tap_acc)

    spectra = [spectra_ref[i] for i in range(spectra_ref.shape[0])]
    size = signal.shape[0]
    both_c, both_s, taps_c, taps_s = backward_spectra(cos_ref[:, 0:size], sin_ref[:, 0:size], signal, spectra)
    rows, kept = (acc.shape[0], tap_acc.shape[0])
    acc[...] += dot(cos_across_ref[0:rows, :], both_c) + dot(sin_across_ref[0:rows, :], both_s)
    tap_acc[...] += dot(cos_across_ref[0:kept, :], taps_c) + dot(sin_across_ref[0:kept, :], taps_s)

    @pl.when(step == pl.num_programs(0) - 1)
    def _():
        backward_end(
            taps_ref, query_short_ref, key_ref, value_ref, out_ref, small, ext, after, acc, tap_acc,
            freqs, scale, medium_reach,
        )


def table_specs(freqs, block):
    rows = pl.BlockSpec((block, freqs), lambda j: (j, 0))
    columns = pl.BlockSpec((freqs, block), lambda j: (0, j))
    return [rows, rows, columns, columns]


def forward_call(got, taps, medium_taps, tables, sent, freqs, block):
    parts, tall, width = got.shape
    length = tall // 3
    tokens = parts * length
    padded = -(-medium_taps.shape[0] // 128) * 128
    timed = jax.ShapeDtypeStruct((tokens, width), F32)
    return pl.pallas_call(
        partial(forward_kernel, freqs=freqs),
        grid=(freqs // block,),
        in_specs=[whole(got.shape), whole(taps.shape), whole(medium_taps.shape)]
        + table_specs(freqs, block)
        + [pl.BlockSpec(memory_space=pl.ANY)],
        out_specs=[
            pl.BlockSpec((parts, length, width), lambda j: (0, 0, 0)),
            whole((tokens, width)),
            whole((tokens, width)),
            pl.BlockSpec((6, block, width), lambda j: (0, j, 0)),
        ],
        out_shape=[
            jax.ShapeDtypeStruct(sent.shape, BF16),
            timed,
            timed,
            jax.ShapeDtypeStruct((6, freqs, width), F32),
        ],
        scratch_shapes=[
            pltpu.VMEM((2, tokens + HALO, width), F32),
            pltpu.VMEM((tokens, 2 * width), BF16),
            pltpu.VMEM((padded, width), BF16),
            pltpu.VMEM((tokens + HALO, width), F32),
        ],
        input_output_aliases={7: 0},
        compiler_params=limit(VMEM_SPECTRAL if freqs * freqs <= TABLE_LIMIT else 60),
        name="forward_spectral",
    )(got, taps, medium_taps, *tables, *tables, sent)


def backward_call(got, grads, taps, query_short, key, value, spectra, tables, freqs, block, scale, medium_reach):
    parts, tall, width = got.shape
    length = tall // 3
    tokens = parts * length
    reach = taps.shape[1]
    padded = -(-medium_reach // 128) * 128
    small = -(-(medium_reach + 2 * reach + query_short.shape[0]) // 16) * 16
    late = -(-(tokens + 1) // 128) * 128
    return pl.pallas_call(
        partial(backward_kernel, freqs=freqs, scale=scale, medium_reach=medium_reach),
        grid=(freqs // block,),
        in_specs=[
            whole(got.shape),
            pl.BlockSpec((parts, length, width), lambda j: (0, 1, 0)),
            whole(taps.shape),
            whole(query_short.shape),
            whole((tokens, width)),
            whole((tokens, width)),
            pl.BlockSpec((6, block, width), lambda j: (0, j, 0)),
        ]
        + table_specs(freqs, block),
        out_specs=whole((parts, tall + small, width)),
        out_shape=jax.ShapeDtypeStruct((parts, tall + small, width), BF16),
        scratch_shapes=[
            pltpu.VMEM((small, width), F32),
            pltpu.VMEM((late, width), F32),
            pltpu.VMEM((late, width), BF16),
            pltpu.VMEM((2, tokens + HALO, width), F32),
            pltpu.VMEM((2, tokens + HALO, width), F32),
            pltpu.VMEM((tokens, 2 * width), F32),
            pltpu.VMEM((padded, width), F32),
        ],
        compiler_params=limit(VMEM_SPECTRAL if freqs * freqs <= TABLE_LIMIT else 60),
        name="backward_spectral",
    )(got, grads, taps, query_short, key, value, spectra, *tables, *tables)


def product_kernel(
    got_ref, query_ref, grad_ref, x_ref, edge_ref, product_ref, query_grad_ref, first_ref, taps_ref, ext, *, reach
):
    parts, length, width = got_ref.shape
    ext[0:HALO, :] = edge_ref[...].astype(F32)
    ext[HALO:, :] = x_ref[0].astype(F32)
    for j in range(parts):
        lanes = slice(j * width, (j + 1) * width)
        convolved = got_ref[j].astype(F32)
        product_ref[:, lanes] = (query_ref[:, lanes] * convolved).astype(BF16)
        own = grad_ref[:, lanes] * convolved
        query_grad_ref[:, lanes] = own
        first_ref[:, lanes] = own[0:HALO].astype(BF16)
        for i in range(reach):
            moved = ext[HALO - i : HALO - i + length, lanes]
            taps_ref[j * reach + i : j * reach + i + 1, :] = jnp.sum(moved * own, 0, keepdims=True)


def project_kernel(place_ref, product_ref, w_ref, sent_ref, kept_ref, buffer, sems, *, flips):
    copies = weight_chunks(place_ref, w_ref, buffer, sems, flips, sent_ref.shape[1])
    for copy in copies:
        copy.start()
    deep = buffer.shape[1]
    per = len(copies) // 2
    for slot, copy in enumerate(copies):
        copy.wait()
        part = lax.dot_general(
            product_ref[...], buffer[slot], (((1,), (1,)), ((), ())), preferred_element_type=F32
        )
        lanes = slice(slot % per * deep, (slot % per + 1) * deep)
        if slot < per:
            sent_ref[:, lanes] = part.astype(sent_ref.dtype)
        else:
            kept_ref[:, lanes] = part


def project(product, weight, place, flips, features):
    length = product.shape[0]
    vmem = pl.BlockSpec(memory_space=pltpu.VMEM)
    return pl.pallas_call(
        partial(project_kernel, flips=flips),
        in_specs=[pl.BlockSpec(memory_space=pltpu.SMEM), vmem, pl.BlockSpec(memory_space=pltpu.HBM)],
        out_specs=[vmem, vmem],
        out_shape=[
            jax.ShapeDtypeStruct((length, features), BF16),
            jax.ShapeDtypeStruct((length, features), F32),
        ],
        scratch_shapes=chunk_scratch(weight, features, 2),
        compiler_params=limit(16),
        name="project",
    )(place, product, weight)


def finish_kernel(
    got_ref, query_grad_ref, next_ref, taps_ref, input_grad_ref, filter_ref, medium_ref, short_ref, ext, *, scale
):
    parts, _, width = got_ref.shape
    length = filter_ref.shape[0]
    reach = taps_ref.shape[1]
    medium_reach = medium_ref.shape[0]
    total = None
    for j in range(parts):
        lanes = slice(j * width, (j + 1) * width)
        input_grad_ref[1, :, lanes] = got_ref[j, 0:length, :]
        input_grad_ref[2, :, lanes] = got_ref[j, length : 2 * length, :]
        filter_ref[:, lanes] = got_ref[j, 2 * length : 3 * length, :].astype(F32)
        small = got_ref[j, 3 * length :, :].astype(F32)
        medium_ref[:, lanes] = small[0:medium_reach, :]
        first = medium_reach + reach
        short_ref[1, :, lanes] = small[medium_reach:first, :]
        short_ref[2, :, lanes] = small[first : first + reach, :]
        sums = small[first + reach : first + reach + parts * reach, :]
        total = sums if total is None else total + sums
    for j in range(parts):
        short_ref[0, :, j * width : (j + 1) * width] = total[j * reach : (j + 1) * reach] * scale
    ext[0:length, :] = query_grad_ref[...]
    ext[length:, :] = next_ref[...].astype(F32)
    total = taps_ref[0, 0:1, :] * ext[0:length, :]
    for i in range(1, reach):
        total = total + taps_ref[0, i : i + 1, :] * ext[i : i + length, :]
    input_grad_ref[0] = total.astype(BF16)


def reshard(value):
    return lax.all_to_all(value, "seq", split_axis=0, concat_axis=0, tiled=True)


def local(inputs, short_taps, medium_taps, long_filter, out_weight, out_cotangent):
    length, groups, channels = inputs.shape
    reach = short_taps.shape[0]
    medium_reach = medium_taps.shape[0]
    parts = lax.axis_size("seq")
    position = lax.axis_index("seq")
    place = lax.axis_index("tensor").astype(jnp.int32)[None]
    features = out_cotangent.shape[1]
    width = channels // parts
    tokens = length * parts
    scale = 1.0 / math.sqrt(tokens)
    freqs, block = spectral_sizes(tokens, medium_reach)
    vmem = pl.BlockSpec(memory_space=pltpu.VMEM)

    weight = pltpu.with_memory_space_constraint(out_weight, pltpu.HBM)
    streams = inputs.transpose(1, 0, 2)
    taps = short_taps.transpose(1, 0, 2)
    query_edge = shift(streams[0, length - HALO :], "seq", 1)
    packed = pl.pallas_call(
        pack_kernel,
        in_specs=[vmem, vmem],
        out_specs=vmem,
        out_shape=jax.ShapeDtypeStruct((parts, 3 * length, width), BF16),
        compiler_params=limit(8),
        name="pack",
    )(streams, long_filter)
    got = reshard(packed)
    packed, cotangent = lax.optimization_barrier((packed, out_cotangent))
    cot_x = exchange(cotangent, "tensor", 2)
    cot_core = exchange(cotangent, "tensor", 1)

    tables = dft_tables(freqs)
    own_taps = lax.dynamic_slice_in_dim(taps, position * width, width, 2)
    own_medium = lax.dynamic_slice_in_dim(medium_taps, position * width, width, 1)

    query = pl.pallas_call(
        query_kernel,
        in_specs=[vmem] * 3,
        out_specs=vmem,
        out_shape=jax.ShapeDtypeStruct((length, channels), F32),
        scratch_shapes=[pltpu.VMEM((length + HALO, channels), F32)],
        compiler_params=limit(8),
        name="query",
    )(streams, query_edge, taps)

    acc = product_grad_of(out_cotangent, cot_core, weight, place, (0, 1))
    cot_far = exchange(cot_x, "tensor", 1)
    product_grad, sent = product_grad_of(cot_x, cot_far, weight, place, (2, 3), acc, query, parts)

    sent, key, value, spectra = forward_call(got, own_taps, own_medium, tables, sent, freqs, block)
    crossed = reshard(sent)

    product, query_grad, first_rows, query_short = pl.pallas_call(
        partial(product_kernel, reach=reach),
        grid=(1,),
        in_specs=[
            pl.BlockSpec((parts, length, width), lambda j: (0, 0, 0)),
            whole((length, channels)),
            whole((length, channels)),
            whole(streams.shape),
            whole((HALO, channels)),
        ],
        out_specs=[
            whole((length, channels)),
            whole((length, channels)),
            whole((HALO, channels)),
            whole((parts * reach, width)),
        ],
        out_shape=[
            jax.ShapeDtypeStruct((length, channels), BF16),
            jax.ShapeDtypeStruct((length, channels), F32),
            jax.ShapeDtypeStruct((HALO, channels), BF16),
            jax.ShapeDtypeStruct((parts * reach, width), F32),
        ],
        scratch_shapes=[pltpu.VMEM((length + HALO, channels), F32)],
        compiler_params=limit(12),
        name="product",
    )(crossed, query, product_grad, streams, query_edge)

    back = backward_call(
        got, crossed, own_taps, query_short, key, value, spectra, tables, freqs, block, scale, medium_reach
    )
    returned = reshard(back)
    back, product = lax.optimization_barrier((back, product))

    far, across = project(product, weight, place, (3, 2), features)
    far_core = exchange(far, "tensor", 1)
    across_sum = exchange((across + far_core.astype(F32)).astype(BF16), "tensor", 2)
    near, own = project(product, weight, place, (1, 0), features)
    near_core = exchange(near, "tensor", 1)

    next_grad = shift(first_rows, "seq", -1)

    input_grad, filter_grad, medium_grad, short_grad = pl.pallas_call(
        partial(finish_kernel, scale=scale),
        in_specs=[vmem] * 4,
        out_specs=[vmem] * 4,
        out_shape=[
            jax.ShapeDtypeStruct((groups, length, channels), BF16),
            jax.ShapeDtypeStruct((length, channels), F32),
            jax.ShapeDtypeStruct((medium_reach, channels), F32),
            jax.ShapeDtypeStruct((groups, reach, channels), F32),
        ],
        scratch_shapes=[pltpu.VMEM((length + HALO, channels), F32)],
        compiler_params=limit(12),
        name="finish",
    )(returned, query_grad, next_grad, taps)

    output = (own + near_core.astype(F32) + across_sum.astype(F32)).astype(BF16)
    return (
        output,
        input_grad.transpose(1, 0, 2),
        filter_grad,
        medium_grad,
        short_grad.transpose(1, 0, 2),
    )


def solution(mesh):
    return jax.shard_map(
        local,
        mesh=mesh,
        in_specs=(
            P("seq", None, "tensor"),
            P(None, None, "tensor"),
            P(None, "tensor"),
            P("seq", "tensor"),
            P(None, "tensor"),
            P("seq", "tensor"),
        ),
        out_specs=(
            P("seq", "tensor"),
            P("seq", None, "tensor"),
            P("seq", "tensor"),
            P(None, "tensor"),
            P(None, None, "tensor"),
        ),
        check_vma=False,
    )
```

time: 616 us -> 126 us (0.20); the launches traced: 607 us -> 125 us
  waiting for transfers between devices: 320 us -> 25.9 us
  matrix products: 98.7 us -> 0 us
  local copies, waits for them, and re-layouts: 77.8 us -> 11.6 us
  Pallas kernels: 0 us -> 39.6 us
  starting transfers between devices: 44.2 us -> 19.8 us
  blocking collectives: 39.4 us -> 20.9 us
  between operations: 15.1 us -> 0.91 us
    all_to_all x8 -> x2, waiting for transfers between devices: 268 us -> 7.71 us  [reshard(): return lax.all_to_all(value, 'seq', split_axis=0, concat_axis=0, tiled=True)]
    dot_general x26 -> x0, matrix products: 76.4 us -> none  [the longest x1 13.3 us: local(): lax.dot_general(product, out_weight, (((1,), (1,)), ((), ())), preferred_...]
    pallas_call x0 -> x10, Pallas kernels: none -> 39.6 us  [the longest x2 11.1 us: project(): pl.pallas_call(partial(project_kernel, flips=flips), in_specs=[pl.BlockSp...]
    psum x1 -> x0, blocking collectives: 39.4 us -> none  [local(): lax.psum(short_part.astype(jnp.bfloat16), 'seq').astype(jnp.float32)]
    reduce_scatter x1 -> x0, waiting for transfers between devices: 35.2 us -> none  [local(): lax.psum_scatter(partial_out, 'tensor', scatter_dimension=1, tiled=True)]
    all_to_all x8 -> x2, starting transfers between devices: 33.3 us -> 11 us  [reshard(): return lax.all_to_all(value, 'seq', split_axis=0, concat_axis=0, tiled=True)]
    conv_general_dilated x6 -> x0, matrix products: 22.3 us -> none  [correlate(): lax.conv_general_dilated(signal[None], kernel[:, None, :], (1,), 'VALID',...]
    all_to_all x0 -> x1, blocking collectives: none -> 20.9 us  [reshard(): return lax.all_to_all(value, 'seq', split_axis=0, concat_axis=0, tiled=True)]
  transfers between devices with their start and end apart: 15 -> 10, of which waited for: 11 -> 3; matrix products, arithmetic and copies ran while one was open for 22% -> 6% of each run, Pallas kernels for 0% -> 13%
where the time goes in v2:
time: 126 us; the launch traced here: 125 us
  Pallas kernels  39.6 us (31%)
  waiting for transfers between devices  25.9 us (21%)
  blocking collectives  20.9 us (17%)
  starting transfers between devices  19.8 us (16%)
  local copies, waits for them, and re-layouts  11.6 us (9%)
  other arithmetic  6.76 us (5%)
    all_to_all x1, blocking collectives, reshard(): return lax.all_to_all(value, 'seq', split_axis=0, concat_axis=0, tiled=True)  20.9 us
    ppermute x6, waiting for transfers between devices, exchange(): lax.ppermute(value, axis, [(source, source ^ flip) for source in range(co...  18.1 us
    pallas_call x2, Pallas kernels, project(): pl.pallas_call(partial(project_kernel, flips=flips), in_specs=[pl.BlockSp...  11.1 us
    all_to_all x2, starting transfers between devices, reshard(): return lax.all_to_all(value, 'seq', split_axis=0, concat_axis=0, tiled=True)  11 us
    unnamed x34, local copies, waits for them, and re-layouts  10.8 us
    all_to_all x2, waiting for transfers between devices, reshard(): return lax.all_to_all(value, 'seq', split_axis=0, concat_axis=0, tiled=True)  7.71 us
    pallas_call x1, Pallas kernels, backward_call(): pl.pallas_call(partial(backward_kernel, freqs=freqs, scale=scale, medium_...  7.52 us
    pallas_call x1, Pallas kernels, forward_call(): pl.pallas_call(partial(forward_kernel, freqs=freqs), grid=(freqs // block...  6.57 us
  transfers between devices with their start and end apart: 10, of which 3 were waited for; matrix products, arithmetic and copies ran while one was open for 6% of the time, Pallas kernels for 13%

profile of v2, /device:TPU:0, one launch (start us, length us, event | category | flops | bytes accessed | tf_op | source)
XLA Modules:
  0.0 125.4 jit_solution(2828749553720735584)
XLA Ops:
  0.7 1.2 copy-done.2
  1.8 1.0 copy-done.12
  2.9 1.0 pack.1
  3.9 7.3 %all-to-all-start = ((bf16[8,384,128]{2,1,0:T(8,128)(2,1)}), bf16[8,384,128]{2,1,0:T(8,128)(2,1)}, u32[]{:S(2)}, u32[]{:S(2)}) async-start(bf16[8,384,128]{2,1,0:T(8,128)(2,1)} %pack.1), calls=%async_computation | async-start | bytes 1572864 | tf_op jit(solution)/shard_map/all_to_all | solution.py:502
  11.2 1.6 %collective-permute-start = (bf16[128,2048]{1,0:T(8,128)(2,1)}, bf16[128,2048]{1,0:T(8,128)(2,1)}, u32[]{:S(2)}, u32[]{:S(2)}) collective-permute-start(bf16[128,2048]{1,0:T(8,128)(2,1)} %x0_ref.1), channel_id=1, source_target_pairs={{0,2},{1,3},{2,0},{3,1},{4,6},{5,7},{6,4},{7,5},{8,10},{9,11},{10,... | collective-permute-start | bytes 1572872 | tf_op jit(solution)/shard_map/ppermute | solution.py:27
  13.5 3.8 %collective-permute-start.3 = (bf16[8,1024]{1,0:T(8,128)(2,1)S(1)}, bf16[8,1024]{1,0:T(8,128)(2,1)S(1)}, u32[]{:S(2)}, u32[]{:S(2)}) collective-permute-start(bf16[8,1024]{1,0:T(8,128)(2,1)S(1)} %slice_bitcast_fusion), channel_id=1, source_target_pairs={{0,4},{4,8},{8,12},{12,16},{16,20},{20,24},{24,28},{1,5},{5,9},{9,... | collective-permute-start | bytes 49160 | tf_op jit(solution)/shard_map/ppermute | solution.py:33
  17.4 0.8 fusion.5
  18.9 7.0 %collective-permute-done.x0_ref = bf16[128,2048]{1,0:T(8,128)(2,1)} collective-permute-done((bf16[128,2048]{1,0:T(8,128)(2,1)}, bf16[128,2048]{1,0:T(8,128)(2,1)}, u32[]{:S(2)}, u32[]{:S(2)}) %collective-permute-start) | collective-permute-done | bytes 524320 | tf_op jit(solution)/shard_map/ppermute | solution.py:27
  25.9 3.1 %add_convert_fusion = (bf16[36,32,1152]{2,1,0:T(8,128)(2,1)S(1)}, bf16[36,32,1152]{2,1,0:T(8,128)(2,1)}) fusion(f32[32,1152]{1,0:T(8,128)S(1)} %get-tuple-element.50, f32[36,1152]{1,0:T(8,128)S(1)} %get-tuple-element.48, f32[32,1152]{1,0:T(8,128)S(1)} %get-tuple-element.49, f32[36,1152]{1,0:T(8,128)S(1)} %get-tuple-element.47), kind=kLoop, calls=%fused_computation | loop fusion | flops 10616832 | bytes 5935104 | tf_op jit(solution)/shard_map/convert_element_type | solution.py:57
  29.1 1.1 copy-done.3
  31.0 1.2 copy-done.15
  32.2 4.8 %grad_first.1.acc_ref = f32[128,1024]{1,0:T(8,128)S(1)} custom-call(s32[1]{0:T(128)} %bitcast.place_ref, bf16[128,2048]{1,0:T(8,128)(2,1)S(1)} %copy-done.15, bf16[128,2048]{1,0:T(8,128)(2,1)} %collective-permute-done.2.x1_ref, bf16[8192,1024]{1,0:T(8,128)(2,1)} %w_ref.7), custom_call_target="tpu_custom_call" | custom-call | tf_op jit(solution)/shard_map/grad_first/pallas_call | solution.py:149
  37.1 5.0 %grad_second.1 = (f32[128,1024]{1,0:T(8,128)S(1)}, bf16[8,256,128]{2,1,0:T(8,128)(2,1)S(1)}) custom-call(s32[1]{0:T(128)} %bitcast.place_ref, bf16[128,2048]{1,0:T(8,128)(2,1)} %collective-permute-done.x0_ref, bf16[128,2048]{1,0:T(8,128)(2,1)} %collective-permute-done.1.x1_ref, bf16[8192,1024]{1,0:T(8,128)(2,1)} %w_ref.7, ...), custom_call_target="tpu_custom_call" | custom-call | tf_op jit(solution)/shard_map/grad_second/pallas_call | solution.py:159
  42.9 0.8 copy-done.13
  43.7 1.7 %copy-done.1 = bf16[36,32,1152]{2,1,0:T(8,128)(2,1)S(1)} copy-done((bf16[36,32,1152]{2,1,0:T(8,128)(2,1)S(1)}, bf16[36,32,1152]{2,1,0:T(8,128)(2,1)}, u32[]{:S(2)}) %copy-start.1) | copy-done | bytes 2654232
  45.4 1.0 copy-done.9
  46.5 6.6 %forward_spectral.1 = (bf16[8,256,128]{2,1,0:T(8,128)(2,1)S(1)}, f32[1024,128]{1,0:T(8,128)S(1)}, f32[1024,128]{1,0:T(8,128)S(1)}, f32[6,1152,128]{2,1,0:T(8,128)S(1)}) custom-call(bf16[8,384,128]{2,1,0:T(8,128)(2,1)} %all-to-all-done.got_ref, f32[3,7,128]{2,1,0:T(8,128)S(1)} %dynamic-slice_bitcast_fusion.taps_ref, ...), custom_call_target="tpu_custom_call", output_to_operand_aliasing={{0}: (7, {})} | custom-call | tf_op jit(solution)/shard_map/forward_spectral/pallas_call | solution.py:351
  53.1 20.9 %all_to_all.15.got_ref.grads_ref = bf16[8,256,128]{2,1,0:T(8,128)(2,1)S(1)} all-to-all(bf16[8,256,128]{2,1,0:T(8,128)(2,1)S(1)} %get-tuple-element.27), channel_id=1, replica_groups=mesh['seq'=8,'tensor'=4] {'seq'}, dimensions={0} | all-to-all | bytes 1048576 | tf_op jit(solution)/shard_map/all_to_all | solution.py:502
  74.0 0.9 product.1
  75.0 0.8 copy-done.10
  75.7 7.5 %backward_spectral.1 = bf16[8,576,128]{2,1,0:T(8,128)(2,1)S(1)} custom-call(bf16[8,384,128]{2,1,0:T(8,128)(2,1)} %all-to-all-done.got_ref, bf16[8,256,128]{2,1,0:T(8,128)(2,1)S(1)} %all_to_all.15.got_ref.grads_ref, f32[3,7,128]{2,1,0:T(8,128)S(1)} %dynamic-slice_bitcast_fusion.taps_ref, f32[56,128]{1,0:T(8,128)S(1)} %get-tuple-element.29.query_short_ref, ...), custom_call_target="tpu_custom_call" | custom-call | tf_op jit(solution)/shard_map/backward_spectral/pallas_call | solution.py:389
  83.3 5.9 %project.3 = (bf16[128,2048]{1,0:T(8,128)(2,1)}, f32[128,2048]{1,0:T(8,128)S(1)}) custom-call(s32[1]{0:T(128)} %bitcast.place_ref, bf16[128,1024]{1,0:T(8,128)(2,1)S(1)} %get-tuple-element.34.product_ref, bf16[8192,1024]{1,0:T(8,128)(2,1)} %w_ref.7), custom_call_target="tpu_custom_call" | custom-call | tf_op jit(solution)/shard_map/project/pallas_call | solution.py:457
  89.3 3.7 %all-to-all-start.2 = ((bf16[8,576,128]{2,1,0:T(8,128)(2,1)}), bf16[8,576,128]{2,1,0:T(8,128)(2,1)S(1)}, u32[]{:S(2)}, u32[]{:S(2)}) async-start(bf16[8,576,128]{2,1,0:T(8,128)(2,1)} %copy-done.7), calls=%async_computation.2 | async-start | bytes 2359296 | tf_op jit(solution)/shard_map/all_to_all | solution.py:502
  93.0 5.2 %project.2 = (bf16[128,2048]{1,0:T(8,128)(2,1)S(1)}, f32[128,2048]{1,0:T(8,128)S(1)}) custom-call(s32[1]{0:T(128)} %bitcast.place_ref, bf16[128,1024]{1,0:T(8,128)(2,1)S(1)} %get-tuple-element.34.product_ref, bf16[8192,1024]{1,0:T(8,128)(2,1)} %w_ref.7), custom_call_target="tpu_custom_call" | custom-call | tf_op jit(solution)/shard_map/project/pallas_call | solution.py:457
  98.6 1.1 add_convert_fusion.2
  99.8 1.6 %collective-permute-start.6 = (bf16[128,2048]{1,0:T(8,128)(2,1)S(1)}, bf16[128,2048]{1,0:T(8,128)(2,1)S(1)}, u32[]{:S(2)}, u32[]{:S(2)}) collective-permute-start(bf16[128,2048]{1,0:T(8,128)(2,1)S(1)} %add_convert_fusion.2), channel_id=1, source_target_pairs={{0,2},{1,3},{2,0},{3,1},{4,6},{5,7},{6,4},{7,5},{8,10},{9,11},{10,... | collective-permute-start | bytes 1572872 | tf_op jit(solution)/shard_map/ppermute | solution.py:27
  101.4 1.3 %collective-permute-start.7 = (bf16[8,1024]{1,0:T(8,128)(2,1)S(1)}, bf16[8,1024]{1,0:T(8,128)(2,1)S(1)}, u32[]{:S(2)}, u32[]{:S(2)}) collective-permute-start(bf16[8,1024]{1,0:T(8,128)(2,1)S(1)} %get-tuple-element.40), channel_id=1, source_target_pairs={{4,0},{8,4},{12,8},{16,12},{20,16},{24,20},{28,24},{5,1},{9,5},{13... | collective-permute-start | bytes 49160 | tf_op jit(solution)/shard_map/ppermute | solution.py:33
  102.7 11.1 %collective-permute-done.6 = bf16[128,2048]{1,0:T(8,128)(2,1)S(1)} collective-permute-done((bf16[128,2048]{1,0:T(8,128)(2,1)S(1)}, bf16[128,2048]{1,0:T(8,128)(2,1)S(1)}, u32[]{:S(2)}, u32[]{:S(2)}) %collective-permute-start.6) | collective-permute-done | bytes 524320 | tf_op jit(solution)/shard_map/ppermute | solution.py:27
  113.8 1.0 add_convert_fusion.1
  114.8 7.7 %all-to-all-done.2.got_ref = bf16[8,576,128]{2,1,0:T(8,128)(2,1)S(1)} async-done(((bf16[8,576,128]{2,1,0:T(8,128)(2,1)}), bf16[8,576,128]{2,1,0:T(8,128)(2,1)S(1)}, u32[]{:S(2)}, u32[]{:S(2)}) %all-to-all-start.2) | async-done | bytes 1179680 | tf_op jit(solution)/shard_map/all_to_all | solution.py:502
  122.5 1.0 copy-done.11
  123.5 1.9 %finish.1 = (bf16[3,128,1024]{2,1,0:T(8,128)(2,1)}, f32[128,1024]{1,0:T(8,128)}, f32[120,1024]{1,0:T(8,128)}, f32[3,7,1024]{2,1,0:T(8,128)}) custom-call(bf16[8,576,128]{2,1,0:T(8,128)(2,1)S(1)} %all-to-all-done.2.got_ref, f32[128,1024]{1,0:T(8,128)S(1)} %copy-done.11, bf16[8,1024]{1,0:T(8,128)(2,1)S(1)} %collective-permute-done.7.next_ref, ...), custom_call_target="tpu_custom_call" | custom-call | tf_op jit(solution)/shard_map/finish/pallas_call | solution.py:598
  (44 shorter events, 3.6 us)
Async XLA Ops:
  0.6 28.4 %copy-start = (f32[120,1024]{1,0:T(8,128)S(1)}, f32[120,1024]{1,0:T(8,128)}, u32[]{:S(2)}) copy-start(f32[120,1024]{1,0:T(8,128)} %param.8) | copy-start | bytes 1474564
  0.6 1.2 copy-start.2
  1.8 1.0 copy-start.12
  2.9 26.1 %copy-start.16 = (f32[7,3,1024]{2,0,1:T(8,128)S(1)}, f32[7,3,1024]{2,0,1:T(8,128)}, u32[]{:S(2)}) copy-start(f32[7,3,1024]{2,0,1:T(8,128)} %param.7) | copy-start | bytes 258052
  3.9 39.8 %all-to-all-start = ((bf16[8,384,128]{2,1,0:T(8,128)(2,1)}), bf16[8,384,128]{2,1,0:T(8,128)(2,1)}, u32[]{:S(2)}, u32[]{:S(2)}) async-start(bf16[8,384,128]{2,1,0:T(8,128)(2,1)} %pack.1), calls=%async_computation | async-start | bytes 1572864 | tf_op jit(solution)/shard_map/all_to_all | solution.py:502
  11.2 19.8 %collective-permute-start.2 = (bf16[128,2048]{1,0:T(8,128)(2,1)}, bf16[128,2048]{1,0:T(8,128)(2,1)}, u32[]{:S(2)}, u32[]{:S(2)}) collective-permute-start(bf16[128,2048]{1,0:T(8,128)(2,1)} %x0_ref.1), channel_id=1, source_target_pairs={{0,1},{1,0},{2,3},{3,2},{4,5},{5,4},{6,7},{7,6},{8,9},{9,8},{10,11... | collective-permute-start | bytes 1572872 | tf_op jit(solution)/shard_map/ppermute | solution.py:27
  11.2 14.6 %collective-permute-start = (bf16[128,2048]{1,0:T(8,128)(2,1)}, bf16[128,2048]{1,0:T(8,128)(2,1)}, u32[]{:S(2)}, u32[]{:S(2)}) collective-permute-start(bf16[128,2048]{1,0:T(8,128)(2,1)} %x0_ref.1), channel_id=1, source_target_pairs={{0,2},{1,3},{2,0},{3,1},{4,6},{5,7},{6,4},{7,5},{8,10},{9,11},{10,... | collective-permute-start | bytes 1572872 | tf_op jit(solution)/shard_map/ppermute | solution.py:27
  13.5 15.6 %collective-permute-start.3 = (bf16[8,1024]{1,0:T(8,128)(2,1)S(1)}, bf16[8,1024]{1,0:T(8,128)(2,1)S(1)}, u32[]{:S(2)}, u32[]{:S(2)}) collective-permute-start(bf16[8,1024]{1,0:T(8,128)(2,1)S(1)} %slice_bitcast_fusion), channel_id=1, source_target_pairs={{0,4},{4,8},{8,12},{12,16},{16,20},{20,24},{24,28},{1,5},{5,9},{9,... | collective-permute-start | bytes 49160 | tf_op jit(solution)/shard_map/ppermute | solution.py:33
  25.9 11.2 %collective-permute-start.1 = (bf16[128,2048]{1,0:T(8,128)(2,1)}, bf16[128,2048]{1,0:T(8,128)(2,1)}, u32[]{:S(2)}, u32[]{:S(2)}) collective-permute-start(bf16[128,2048]{1,0:T(8,128)(2,1)} %collective-permute-done.x0_ref), channel_id=1, source_target_pairs={{0,1},{1,0},{2,3},{3,2},{4,5},{5,4},{6,7},{7,6},{8,9},{9,8},{10,11... | collective-permute-start | bytes 1572872 | tf_op jit(solution)/shard_map/ppermute | solution.py:27
  29.0 1.1 copy-start.3
  31.0 6.1 %copy-start.5 = (f32[128,1024]{1,0:T(8,128)}, f32[128,1024]{1,0:T(8,128)S(1)}, u32[]{:S(2)}) copy-start(f32[128,1024]{1,0:T(8,128)S(1)} %query.1.query_ref) | copy-start | bytes 1572868
  31.0 1.2 copy-start.15
  42.1 0.8 copy-start.8
  42.9 0.8 copy-start.13
  43.7 1.8 %copy-start.1 = (bf16[36,32,1152]{2,1,0:T(8,128)(2,1)S(1)}, bf16[36,32,1152]{2,1,0:T(8,128)(2,1)}, u32[]{:S(2)}) copy-start(bf16[36,32,1152]{2,1,0:T(8,128)(2,1)} %get-tuple-element.46) | copy-start | bytes 7962628
  45.4 1.0 copy-start.9
  46.5 27.5 %copy-start.4 = (bf16[128,3,1024]{2,0,1:T(8,128)(2,1)S(1)}, bf16[128,3,1024]{2,0,1:T(8,128)(2,1)}, u32[]{:S(2)}) copy-start(bf16[128,3,1024]{2,0,1:T(8,128)(2,1)} %param.6) | copy-start | bytes 2359300
  46.5 27.5 %copy-start.6 = (f32[128,1024]{1,0:T(8,128)S(1)}, f32[128,1024]{1,0:T(8,128)}, u32[]{:S(2)}) copy-start(f32[128,1024]{1,0:T(8,128)} %copy-done.5) | copy-start | bytes 1572868
  46.5 27.5 %copy-start.14 = (f32[128,1024]{1,0:T(8,128)S(1)}, f32[128,1024]{1,0:T(8,128)}, u32[]{:S(2)}) copy-start(f32[128,1024]{1,0:T(8,128)} %copy-done.13) | copy-start | bytes 1572868
  74.9 0.8 copy-start.10
  83.3 6.0 %copy-start.7 = (bf16[8,576,128]{2,1,0:T(8,128)(2,1)}, bf16[8,576,128]{2,1,0:T(8,128)(2,1)S(1)}, u32[]{:S(2)}) copy-start(bf16[8,576,128]{2,1,0:T(8,128)(2,1)S(1)} %backward_spectral.1) | copy-start | bytes 3538948
  89.2 9.4 %collective-permute-start.5 = (bf16[128,2048]{1,0:T(8,128)(2,1)}, bf16[128,2048]{1,0:T(8,128)(2,1)}, u32[]{:S(2)}, u32[]{:S(2)}) collective-permute-start(bf16[128,2048]{1,0:T(8,128)(2,1)} %get-tuple-element.38), channel_id=1, source_target_pairs={{0,1},{1,0},{2,3},{3,2},{4,5},{5,4},{6,7},{7,6},{8,9},{9,8},{10,11... | collective-permute-start | bytes 1572872 | tf_op jit(solution)/shard_map/ppermute | solution.py:27
  89.3 33.2 %all-to-all-start.2 = ((bf16[8,576,128]{2,1,0:T(8,128)(2,1)}), bf16[8,576,128]{2,1,0:T(8,128)(2,1)S(1)}, u32[]{:S(2)}, u32[]{:S(2)}) async-start(bf16[8,576,128]{2,1,0:T(8,128)(2,1)} %copy-done.7), calls=%async_computation.2 | async-start | bytes 2359296 | tf_op jit(solution)/shard_map/all_to_all | solution.py:502
  98.2 4.5 %collective-permute-start.4 = (bf16[128,2048]{1,0:T(8,128)(2,1)S(1)}, bf16[128,2048]{1,0:T(8,128)(2,1)S(1)}, u32[]{:S(2)}, u32[]{:S(2)}) collective-permute-start(bf16[128,2048]{1,0:T(8,128)(2,1)S(1)} %get-tuple-element.36), channel_id=1, source_target_pairs={{0,1},{1,0},{2,3},{3,2},{4,5},{5,4},{6,7},{7,6},{8,9},{9,8},{10,11... | collective-permute-start | bytes 1572872 | tf_op jit(solution)/shard_map/ppermute | solution.py:27
  99.8 14.0 %collective-permute-start.6 = (bf16[128,2048]{1,0:T(8,128)(2,1)S(1)}, bf16[128,2048]{1,0:T(8,128)(2,1)S(1)}, u32[]{:S(2)}, u32[]{:S(2)}) collective-permute-start(bf16[128,2048]{1,0:T(8,128)(2,1)S(1)} %add_convert_fusion.2), channel_id=1, source_target_pairs={{0,2},{1,3},{2,0},{3,1},{4,6},{5,7},{6,4},{7,5},{8,10},{9,11},{10,... | collective-permute-start | bytes 1572872 | tf_op jit(solution)/shard_map/ppermute | solution.py:27
  101.4 13.4 %collective-permute-start.7 = (bf16[8,1024]{1,0:T(8,128)(2,1)S(1)}, bf16[8,1024]{1,0:T(8,128)(2,1)S(1)}, u32[]{:S(2)}, u32[]{:S(2)}) collective-permute-start(bf16[8,1024]{1,0:T(8,128)(2,1)S(1)} %get-tuple-element.40), channel_id=1, source_target_pairs={{4,0},{8,4},{12,8},{16,12},{20,16},{24,20},{28,24},{5,1},{9,5},{13... | collective-permute-start | bytes 49160 | tf_op jit(solution)/shard_map/ppermute | solution.py:33
  122.5 1.0 copy-start.11

commit v3 on v2

--- a/solution.py
+++ b/solution.py
@@ -14,7 +14,6 @@
 HALO = 8
 GROUP = 32
 CHUNK = 512
-VMEM_SPECTRAL = 24
 TABLE_LIMIT = 1 << 22
 
 
@@ -62,25 +61,26 @@
     return pltpu.CompilerParams(vmem_limit_bytes=mebibytes << 20)
 
 
-def pack_kernel(x_ref, filter_ref, out_ref):
+def pack_kernel(x_ref, filter_ref, out_ref, streams, taps, rounded, sems):
     parts, rows, width = out_ref.shape
     length = rows // 3
+    read_filter = pltpu.make_async_copy(filter_ref, taps, sems.at[0])
+    read_streams = pltpu.make_async_copy(x_ref.at[pl.ds(1, 2)], streams, sems.at[1])
+    read_filter.start()
+    read_streams.start()
+    read_filter.wait()
+    for j in range(parts):
+        rounded[j, 2 * length :, :] = taps[:, j * width : (j + 1) * width].astype(BF16)
+    read_streams.wait()
+    writes = []
     for j in range(parts):
         lanes = slice(j * width, (j + 1) * width)
-        out_ref[j, 0:length, :] = x_ref[1, :, lanes]
-        out_ref[j, length : 2 * length, :] = x_ref[2, :, lanes]
-        out_ref[j, 2 * length :, :] = filter_ref[:, lanes].astype(BF16)
-
-
-def query_kernel(x_ref, edge_ref, taps_ref, out_ref, ext):
-    length = out_ref.shape[0]
-    reach = taps_ref.shape[1]
-    ext[0:HALO, :] = edge_ref[...].astype(F32)
-    ext[HALO:, :] = x_ref[0].astype(F32)
-    total = taps_ref[0, 0:1, :] * ext[HALO : HALO + length, :]
-    for i in range(1, reach):
-        total = total + taps_ref[0, i : i + 1, :] * ext[HALO - i : HALO - i + length, :]
-    out_ref[...] = total
+        rounded[j, 0:length, :] = streams[0, :, lanes]
+        rounded[j, length : 2 * length, :] = streams[1, :, lanes]
+        writes.append(pltpu.make_async_copy(rounded.at[j], out_ref.at[j], sems.at[2 + j]))
+        writes[j].start()
+    for write in writes:
+        write.wait()
 
 
 def weight_chunks(place_ref, weight_ref, buffer, sems, flips, features):
@@ -116,56 +116,31 @@
     return total
 
 
-def grad_first_kernel(place_ref, x0_ref, x1_ref, w_ref, out_ref, buffer, sems, *, flips):
-    copies = weight_chunks(place_ref, w_ref, buffer, sems, flips, x0_ref.shape[1])
+def product_grad_kernel(place_ref, w_ref, *refs, flips, added):
+    x_refs = refs[: len(flips)]
+    out_ref, buffer, sems = refs[-3:]
+    copies = weight_chunks(place_ref, w_ref, buffer, sems, flips, x_refs[0].shape[1])
     for copy in copies:
         copy.start()
-    out_ref[...] = summed((x0_ref, x1_ref), copies, buffer, None)
-
-
-def grad_second_kernel(
-    place_ref, x0_ref, x1_ref, w_ref, acc_ref, query_ref, out_ref, sent_ref, buffer, sems, *, flips
-):
-    copies = weight_chunks(place_ref, w_ref, buffer, sems, flips, x0_ref.shape[1])
-    for copy in copies:
-        copy.start()
-    total = summed((x0_ref, x1_ref), copies, buffer, acc_ref[...])
-    out_ref[...] = total
-    parts, _, width = sent_ref.shape
-    for j in range(parts):
-        lanes = slice(j * width, (j + 1) * width)
-        sent_ref[j] = (total[:, lanes] * query_ref[:, lanes]).astype(BF16)
-
-
-def product_grad_of(x0, x1, weight, place, flips, acc=None, query=None, parts=None):
-    length, features = x0.shape
+    out_ref[...] = summed(x_refs, copies, buffer, refs[len(flips)][...] if added else None)
+
+
+def product_grad_of(shards, weight, place, flips, acc=None, out_memory=None):
+    length, features = shards[0].shape
     channels = weight.shape[1]
-    smem = pl.BlockSpec(memory_space=pltpu.SMEM)
     vmem = pl.BlockSpec(memory_space=pltpu.VMEM)
-    in_specs = [smem, vmem, vmem, pl.BlockSpec(memory_space=pltpu.HBM)]
-    full = jax.ShapeDtypeStruct((length, channels), F32)
-    scratch = chunk_scratch(weight, features, 2)
-    if acc is None:
-        return pl.pallas_call(
-            partial(grad_first_kernel, flips=flips),
-            in_specs=in_specs,
-            out_specs=vmem,
-            out_shape=full,
-            scratch_shapes=scratch,
-            compiler_params=limit(16),
-            name="grad_first",
-        )(place, x0, x1, weight)
-    width = channels // parts
+    extra = [] if acc is None else [acc]
+    make = out_memory or jax.ShapeDtypeStruct
     return pl.pallas_call(
-        partial(grad_second_kernel, flips=flips),
-        grid=(1,),
-        in_specs=in_specs + [vmem, vmem],
-        out_specs=[vmem, pl.BlockSpec((parts, length, width), lambda j: (0, 1, 0))],
-        out_shape=[full, jax.ShapeDtypeStruct((parts, 2 * length, width), BF16)],
-        scratch_shapes=scratch,
+        partial(product_grad_kernel, flips=flips, added=bool(extra)),
+        in_specs=[pl.BlockSpec(memory_space=pltpu.SMEM), pl.BlockSpec(memory_space=pltpu.HBM)]
+        + [vmem] * (len(shards) + len(extra)),
+        out_specs=vmem,
+        out_shape=make((length, channels), F32),
+        scratch_shapes=chunk_scratch(weight, features, len(flips)),
         compiler_params=limit(16),
-        name="grad_second",
-    )(place, x0, x1, weight, acc, query)
+        name="product_grad",
+    )(place, weight, *shards, *extra)
 
 
 def filtered(taps_ref, stream, ext, begin, length):
@@ -221,29 +196,85 @@
     parts, length, _ = out_ref.shape
     for s in range(parts):
         first = s * length + 1
-        out_ref[s, 0:length, :] = (acc[first : first + length, :] * (1.0 / freqs)).astype(BF16)
+        out_ref[s] = (acc[first : first + length, :] * (1.0 / freqs)).astype(BF16)
+
+
+def query_part(x_ref, edge_ref, taps_ref, grad_ref, query_ref, out_ref, own):
+    parts, rows, width = out_ref.shape
+    length = rows // 2
+    own[0:HALO, :] = edge_ref[...].astype(F32)
+    own[HALO:, :] = x_ref[0].astype(F32)
+    for j in range(parts):
+        lanes = slice(j * width, (j + 1) * width)
+        query = taps_ref[0, 0:1, lanes] * own[HALO : HALO + length, lanes]
+        for i in range(1, taps_ref.shape[1]):
+            query = query + taps_ref[0, i : i + 1, lanes] * own[HALO - i : HALO - i + length, lanes]
+        query_ref[:, lanes] = query
+        out_ref[j, length:, :] = (grad_ref[:, lanes] * query).astype(BF16)
+
+
+def table_copies(tables, held, sems, blocks):
+    size = held.shape[1] // blocks
+    return [
+        [
+            pltpu.make_async_copy(
+                table.at[pl.ds(b * size, size), :], held.at[i, pl.ds(b * size, size), :], sems.at[i, b]
+            )
+            for i, table in enumerate(tables)
+        ]
+        for b in range(blocks)
+    ]
 
 
 def forward_kernel(
-    got_ref, taps_ref, medium_ref, cos_ref, sin_ref, cos_across_ref, sin_across_ref, _,
-    out_ref, key_ref, value_ref, spectra_ref, ext, signals, medium, acc, *, freqs,
+    got_ref, x_ref, edge_ref, all_taps_ref, grad_ref, taps_ref, medium_ref, cos_ref, sin_ref, *refs, freqs, block,
+    resident,
 ):
+    if not resident:
+        cos_across_ref, sin_across_ref, *refs = refs
+    out_ref, query_ref, key_ref, value_ref, spectra_ref, ext, signals, medium, acc, own, *refs = refs
+    rows = acc.shape[0]
     step = pl.program_id(0)
+    length = x_ref.shape[1]
+    half = out_ref.at[:, pl.ds(0, length), :]
+
+    def begin():
+        forward_begin(got_ref, taps_ref, medium_ref, key_ref, value_ref, ext, signals, medium)
+        query_part(x_ref, edge_ref, all_taps_ref, grad_ref, query_ref, out_ref, own)
+
+    if resident:
+        held, yc_all, ys_all, sems = refs
+        copies = table_copies((cos_ref, sin_ref), held, sems, freqs // block)
+        for pair in copies:
+            for copy in pair:
+                copy.start()
+        begin()
+        for b, pair in enumerate(copies):
+            for copy in pair:
+                copy.wait()
+            here = slice(b * block, (b + 1) * block)
+            saved, yc, ys = forward_spectra(held[0, here, :], held[1, here, :], signals, medium)
+            for i, spectrum in enumerate(saved):
+                spectra_ref[i, here, :] = spectrum
+            yc_all[here, :] = yc
+            ys_all[here, :] = ys
+        acc[...] = dot(held[0, 0:rows, :], yc_all[...]) + dot(held[1, 0:rows, :], ys_all[...])
+        forward_end(half, acc, freqs)
+        return
 
     @pl.when(step == 0)
     def _():
-        forward_begin(got_ref, taps_ref, medium_ref, key_ref, value_ref, ext, signals, medium)
+        begin()
         acc[...] = jnp.zeros_like(acc)
 
     saved, yc, ys = forward_spectra(cos_ref[...], sin_ref[...], signals, medium)
     for i, spectrum in enumerate(saved):
         spectra_ref[i] = spectrum
-    rows = acc.shape[0]
     acc[...] += dot(cos_across_ref[0:rows, :], yc) + dot(sin_across_ref[0:rows, :], ys)
 
     @pl.when(step == pl.num_programs(0) - 1)
     def _():
-        forward_end(out_ref, acc, freqs)
+        forward_end(half, acc, freqs)
 
 
 def backward_begin(got_ref, grads_ref, delayed, signal, ext):
@@ -309,11 +340,41 @@
 
 
 def backward_kernel(
-    got_ref, grads_ref, taps_ref, query_short_ref, key_ref, value_ref, spectra_ref,
-    cos_ref, sin_ref, cos_across_ref, sin_across_ref,
-    out_ref, small, delayed, signal, ext, after, acc, tap_acc, *, freqs, scale, medium_reach,
+    got_ref, grads_ref, taps_ref, query_short_ref, key_ref, value_ref, spectra_ref, cos_ref, sin_ref, *refs,
+    freqs, block, scale, medium_reach, resident,
 ):
+    if not resident:
+        cos_across_ref, sin_across_ref, *refs = refs
+    out_ref, small, delayed, signal, ext, after, acc, tap_acc, *refs = refs
     step = pl.program_id(0)
+    size = signal.shape[0]
+    rows, kept = (acc.shape[0], tap_acc.shape[0])
+
+    def end():
+        backward_end(
+            taps_ref, query_short_ref, key_ref, value_ref, out_ref, small, ext, after, acc, tap_acc,
+            freqs, scale, medium_reach,
+        )
+
+    if resident:
+        held, both_c_all, both_s_all, taps_c_all, taps_s_all, sems = refs
+        copies = table_copies((cos_ref, sin_ref), held, sems, freqs // block)
+        for pair in copies:
+            for copy in pair:
+                copy.start()
+        backward_begin(got_ref, grads_ref, delayed, signal, ext)
+        for b, pair in enumerate(copies):
+            for copy in pair:
+                copy.wait()
+            here = slice(b * block, (b + 1) * block)
+            spectra = [spectra_ref[i, here, :] for i in range(spectra_ref.shape[0])]
+            both_c_all[here, :], both_s_all[here, :], taps_c_all[here, :], taps_s_all[here, :] = backward_spectra(
+                held[0, here, 0:size], held[1, here, 0:size], signal, spectra
+            )
+        acc[...] = dot(held[0, 0:rows, :], both_c_all[...]) + dot(held[1, 0:rows, :], both_s_all[...])
+        tap_acc[...] = dot(held[0, 0:kept, :], taps_c_all[...]) + dot(held[1, 0:kept, :], taps_s_all[...])
+        end()
+        return
 
     @pl.when(step == 0)
     def _():
@@ -322,46 +383,61 @@
         tap_acc[...] = jnp.zeros_like(tap_acc)
 
     spectra = [spectra_ref[i] for i in range(spectra_ref.shape[0])]
-    size = signal.shape[0]
     both_c, both_s, taps_c, taps_s = backward_spectra(cos_ref[:, 0:size], sin_ref[:, 0:size], signal, spectra)
-    rows, kept = (acc.shape[0], tap_acc.shape[0])
     acc[...] += dot(cos_across_ref[0:rows, :], both_c) + dot(sin_across_ref[0:rows, :], both_s)
     tap_acc[...] += dot(cos_across_ref[0:kept, :], taps_c) + dot(sin_across_ref[0:kept, :], taps_s)
-
-    @pl.when(step == pl.num_programs(0) - 1)
-    def _():
-        backward_end(
-            taps_ref, query_short_ref, key_ref, value_ref, out_ref, small, ext, after, acc, tap_acc,
-            freqs, scale, medium_reach,
-        )
-
-
-def table_specs(freqs, block):
+    pl.when(step == pl.num_programs(0) - 1)(end)
+
+
+def spectral_plan(freqs, block, tables):
+    if freqs * freqs <= TABLE_LIMIT:
+        hbm = pl.BlockSpec(memory_space=pltpu.HBM)
+        return True, 1, [hbm, hbm], [pltpu.with_memory_space_constraint(t, pltpu.HBM) for t in tables]
     rows = pl.BlockSpec((block, freqs), lambda j: (j, 0))
     columns = pl.BlockSpec((freqs, block), lambda j: (0, j))
-    return [rows, rows, columns, columns]
-
-
-def forward_call(got, taps, medium_taps, tables, sent, freqs, block):
+    return False, freqs // block, [rows, rows, columns, columns], [*tables, *tables]
+
+
+def held_scratch(freqs, block, widths):
+    return (
+        [pltpu.VMEM((2, freqs, freqs), BF16)]
+        + [pltpu.VMEM((freqs, width), BF16) for width in widths]
+        + [pltpu.SemaphoreType.DMA((2, freqs // block))]
+    )
+
+
+def forward_call(got, streams, edge, all_taps, grad, taps, medium_taps, tables, freqs, block):
     parts, tall, width = got.shape
     length = tall // 3
     tokens = parts * length
+    channels = parts * width
     padded = -(-medium_taps.shape[0] // 128) * 128
     timed = jax.ShapeDtypeStruct((tokens, width), F32)
+    resident, steps, specs, operands = spectral_plan(freqs, block, tables)
+    per = freqs // steps
     return pl.pallas_call(
-        partial(forward_kernel, freqs=freqs),
-        grid=(freqs // block,),
-        in_specs=[whole(got.shape), whole(taps.shape), whole(medium_taps.shape)]
-        + table_specs(freqs, block)
-        + [pl.BlockSpec(memory_space=pl.ANY)],
+        partial(forward_kernel, freqs=freqs, block=block, resident=resident),
+        grid=(steps,),
+        in_specs=[
+            whole(got.shape),
+            whole((1, length, channels)),
+            whole(edge.shape),
+            whole(all_taps.shape),
+            whole(grad.shape),
+            whole(taps.shape),
+            whole(medium_taps.shape),
+        ]
+        + specs,
         out_specs=[
-            pl.BlockSpec((parts, length, width), lambda j: (0, 0, 0)),
+            whole((parts, 2 * length, width)),
+            whole((length, channels)),
             whole((tokens, width)),
             whole((tokens, width)),
-            pl.BlockSpec((6, block, width), lambda j: (0, j, 0)),
+            pl.BlockSpec((6, per, width), lambda j: (0, j, 0)),
         ],
         out_shape=[
-            jax.ShapeDtypeStruct(sent.shape, BF16),
+            jax.ShapeDtypeStruct((parts, 2 * length, width), BF16),
+            jax.ShapeDtypeStruct((length, channels), F32),
             timed,
             timed,
             jax.ShapeDtypeStruct((6, freqs, width), F32),
@@ -371,11 +447,12 @@
             pltpu.VMEM((tokens, 2 * width), BF16),
             pltpu.VMEM((padded, width), BF16),
             pltpu.VMEM((tokens + HALO, width), F32),
-        ],
-        input_output_aliases={7: 0},
-        compiler_params=limit(VMEM_SPECTRAL if freqs * freqs <= TABLE_LIMIT else 60),
+            pltpu.VMEM((length + HALO, channels), F32),
+        ]
+        + (held_scratch(freqs, block, (width, width)) if resident else []),
+        compiler_params=limit(32 if resident else 60),
         name="forward_spectral",
-    )(got, taps, medium_taps, *tables, *tables, sent)
+    )(got, streams, edge, all_taps, grad, taps, medium_taps, *operands)
 
 
 def backward_call(got, grads, taps, query_short, key, value, spectra, tables, freqs, block, scale, medium_reach):
@@ -386,9 +463,13 @@
     padded = -(-medium_reach // 128) * 128
     small = -(-(medium_reach + 2 * reach + query_short.shape[0]) // 16) * 16
     late = -(-(tokens + 1) // 128) * 128
+    resident, steps, specs, operands = spectral_plan(freqs, block, tables)
+    per = freqs // steps
     return pl.pallas_call(
-        partial(backward_kernel, freqs=freqs, scale=scale, medium_reach=medium_reach),
-        grid=(freqs // block,),
+        partial(
+            backward_kernel, freqs=freqs, block=block, scale=scale, medium_reach=medium_reach, resident=resident
+        ),
+        grid=(steps,),
         in_specs=[
             whole(got.shape),
             pl.BlockSpec((parts, length, width), lambda j: (0, 1, 0)),
@@ -396,11 +477,11 @@
             whole(query_short.shape),
             whole((tokens, width)),
             whole((tokens, width)),
-            pl.BlockSpec((6, block, width), lambda j: (0, j, 0)),
+            pl.BlockSpec((6, per, width), lambda j: (0, j, 0)),
         ]
-        + table_specs(freqs, block),
+        + specs,
         out_specs=whole((parts, tall + small, width)),
-        out_shape=jax.ShapeDtypeStruct((parts, tall + small, width), BF16),
+        out_shape=pltpu.HBM((parts, tall + small, width), BF16),
         scratch_shapes=[
             pltpu.VMEM((small, width), F32),
             pltpu.VMEM((late, width), F32),
@@ -409,10 +490,11 @@
             pltpu.VMEM((2, tokens + HALO, width), F32),
             pltpu.VMEM((tokens, 2 * width), F32),
             pltpu.VMEM((padded, width), F32),
-        ],
-        compiler_params=limit(VMEM_SPECTRAL if freqs * freqs <= TABLE_LIMIT else 60),
+        ]
+        + (held_scratch(freqs, block, (2 * width, 2 * width, width, width)) if resident else []),
+        compiler_params=limit(32 if resident else 60),
         name="backward_spectral",
-    )(got, grads, taps, query_short, key, value, spectra, *tables, *tables)
+    )(got, grads, taps, query_short, key, value, spectra, *operands)
 
 
 def product_kernel(
@@ -519,39 +601,42 @@
     weight = pltpu.with_memory_space_constraint(out_weight, pltpu.HBM)
     streams = inputs.transpose(1, 0, 2)
     taps = short_taps.transpose(1, 0, 2)
-    query_edge = shift(streams[0, length - HALO :], "seq", 1)
+    hbm = pl.BlockSpec(memory_space=pltpu.HBM)
     packed = pl.pallas_call(
         pack_kernel,
-        in_specs=[vmem, vmem],
-        out_specs=vmem,
-        out_shape=jax.ShapeDtypeStruct((parts, 3 * length, width), BF16),
+        in_specs=[hbm, hbm],
+        out_specs=hbm,
+        out_shape=pltpu.HBM((parts, 3 * length, width), BF16),
+        scratch_shapes=[
+            pltpu.VMEM((2, length, channels), BF16),
+            pltpu.VMEM((length, channels), F32),
+            pltpu.VMEM((parts, 3 * length, width), BF16),
+            pltpu.SemaphoreType.DMA((2 + parts,)),
+        ],
         compiler_params=limit(8),
         name="pack",
-    )(streams, long_filter)
+    )(
+        pltpu.with_memory_space_constraint(streams, pltpu.HBM),
+        pltpu.with_memory_space_constraint(long_filter, pltpu.HBM),
+    )
     got = reshard(packed)
-    packed, cotangent = lax.optimization_barrier((packed, out_cotangent))
-    cot_x = exchange(cotangent, "tensor", 2)
-    cot_core = exchange(cotangent, "tensor", 1)
+    query_edge = shift(streams[0, length - HALO :], "seq", 1)
+    cot_x = exchange(out_cotangent, "tensor", 2)
+    cot_core = exchange(out_cotangent, "tensor", 1)
 
     tables = dft_tables(freqs)
     own_taps = lax.dynamic_slice_in_dim(taps, position * width, width, 2)
     own_medium = lax.dynamic_slice_in_dim(medium_taps, position * width, width, 1)
 
-    query = pl.pallas_call(
-        query_kernel,
-        in_specs=[vmem] * 3,
-        out_specs=vmem,
-        out_shape=jax.ShapeDtypeStruct((length, channels), F32),
-        scratch_shapes=[pltpu.VMEM((length + HALO, channels), F32)],
-        compiler_params=limit(8),
-        name="query",
-    )(streams, query_edge, taps)
-
-    acc = product_grad_of(out_cotangent, cot_core, weight, place, (0, 1))
+    acc = product_grad_of((out_cotangent, cot_core), weight, place, (0, 1))
     cot_far = exchange(cot_x, "tensor", 1)
-    product_grad, sent = product_grad_of(cot_x, cot_far, weight, place, (2, 3), acc, query, parts)
-
-    sent, key, value, spectra = forward_call(got, own_taps, own_medium, tables, sent, freqs, block)
+    acc = product_grad_of((cot_x,), weight, place, (2,), acc)
+    product_grad = product_grad_of((cot_far,), weight, place, (3,), acc, pltpu.HBM)
+    product_grad = pltpu.with_memory_space_constraint(product_grad, pltpu.HBM)
+
+    sent, query, key, value, spectra = forward_call(
+        got, streams, query_edge, taps, product_grad, own_taps, own_medium, tables, freqs, block
+    )
     crossed = reshard(sent)
 
     product, query_grad, first_rows, query_short = pl.pallas_call(
@@ -572,7 +657,7 @@
         ],
         out_shape=[
             jax.ShapeDtypeStruct((length, channels), BF16),
-            jax.ShapeDtypeStruct((length, channels), F32),
+            pltpu.HBM((length, channels), F32),
             jax.ShapeDtypeStruct((HALO, channels), BF16),
             jax.ShapeDtypeStruct((parts * reach, width), F32),
         ],

time: 126 us -> 113 us (0.90)
  local copies, waits for them, and re-layouts: 11.6 us -> 3.64 us
  waiting for transfers between devices: 25.9 us -> 21.7 us
  Pallas kernels: 39.6 us -> 42 us
  blocking collectives: 20.9 us -> 18.7 us
  starting transfers between devices: 19.8 us -> 17.9 us
    unnamed x34 -> x14, local copies, waits for them, and re-layouts: 10.8 us -> 2.9 us
    ppermute x6, waiting for transfers between devices: 18.1 us -> 11.8 us  [exchange(): lax.ppermute(value, axis, [(source, source ^ flip) for source in range(co...]
    all_to_all x2, starting transfers between devices: 11 us -> 8.56 us  [reshard(): return lax.all_to_all(value, 'seq', split_axis=0, concat_axis=0, tiled=True)]
    all_to_all x1, blocking collectives: 20.9 us -> 18.7 us  [reshard(): return lax.all_to_all(value, 'seq', split_axis=0, concat_axis=0, tiled=True)]
    all_to_all x2, waiting for transfers between devices: 7.71 us -> 9.91 us  [reshard(): return lax.all_to_all(value, 'seq', split_axis=0, concat_axis=0, tiled=True)]
    pallas_call x1, Pallas kernels: 0.91 us -> 2.65 us  [local(): pl.pallas_call(partial(product_kernel, reach=reach), grid=(1,), in_specs=...]
  transfers between devices with their start and end apart: 10 -> 10, of which waited for: 3 -> 3; matrix products, arithmetic and copies ran while one was open for 6% -> 7% of each run, Pallas kernels for 13% -> 16%
where the time goes in v3:
time: 113 us; the launch traced here: 112 us
  Pallas kernels  42 us (37%)
  waiting for transfers between devices  21.7 us (19%)
  blocking collectives  18.7 us (17%)
  starting transfers between devices  17.9 us (16%)
  other arithmetic  7.65 us (7%)
  local copies, waits for them, and re-layouts  3.64 us (3%)
    all_to_all x1, blocking collectives, reshard(): return lax.all_to_all(value, 'seq', split_axis=0, concat_axis=0, tiled=True)  18.7 us
    ppermute x6, waiting for transfers between devices, exchange(): lax.ppermute(value, axis, [(source, source ^ flip) for source in range(co...  11.8 us
    pallas_call x3, Pallas kernels, product_grad_of(): pl.pallas_call(partial(product_grad_kernel, flips=flips, added=bool(extra...  10.7 us
    pallas_call x2, Pallas kernels, project(): pl.pallas_call(partial(project_kernel, flips=flips), in_specs=[pl.BlockSp...  10.7 us
    all_to_all x2, waiting for transfers between devices, reshard(): return lax.all_to_all(value, 'seq', split_axis=0, concat_axis=0, tiled=True)  9.91 us
    all_to_all x2, starting transfers between devices, reshard(): return lax.all_to_all(value, 'seq', split_axis=0, concat_axis=0, tiled=True)  8.56 us
    pallas_call x1, Pallas kernels, backward_call(): pl.pallas_call(partial(backward_kernel, freqs=freqs, block=block, scale=s...  7.84 us
    pallas_call x1, Pallas kernels, forward_call(): pl.pallas_call(partial(forward_kernel, freqs=freqs, block=block, resident...  5.99 us
  transfers between devices with their start and end apart: 10, of which 3 were waited for; matrix products, arithmetic and copies ran while one was open for 7% of the time, Pallas kernels for 16%

profile of v3, /device:TPU:0, one launch (start us, length us, event | category | flops | bytes accessed | tf_op | source)
XLA Modules:
  0.0 112.4 jit_solution(344105551445909482)
XLA Ops:
  0.7 3.0 %collective-permute-start.1 = (bf16[128,2048]{1,0:T(8,128)(2,1)}, bf16[128,2048]{1,0:T(8,128)(2,1)S(1)}, u32[]{:S(2)}, u32[]{:S(2)}) collective-permute-start(bf16[128,2048]{1,0:T(8,128)(2,1)} %refs_0_.1), channel_id=1, source_target_pairs={{0,2},{1,3},{2,0},{3,1},{4,6},{5,7},{6,4},{7,5},{8,10},{9,11},{10,... | collective-permute-start | bytes 1572872 | tf_op jit(solution)/shard_map/ppermute | solution.py:26
  3.7 0.7 slice_bitcast_fusion
  4.4 3.4 %collective-permute-start = (bf16[8,1024]{1,0:T(8,128)(2,1)S(1)}, bf16[8,1024]{1,0:T(8,128)(2,1)S(1)}, u32[]{:S(2)}, u32[]{:S(2)}) collective-permute-start(bf16[8,1024]{1,0:T(8,128)(2,1)S(1)} %slice_bitcast_fusion), channel_id=1, source_target_pairs={{0,4},{4,8},{8,12},{12,16},{16,20},{20,24},{24,28},{1,5},{5,9},{9,... | collective-permute-start | bytes 49160 | tf_op jit(solution)/shard_map/ppermute | solution.py:32
  7.8 2.2 %pack.1 = bf16[8,384,128]{2,1,0:T(8,128)(2,1)} custom-call(bf16[3,128,1024]{2,1,0:T(8,128)(2,1)} %bitcast.12, f32[128,1024]{1,0:T(8,128)} %filter_ref.1), custom_call_target="tpu_custom_call" | custom-call | tf_op jit(solution)/shard_map/pack/pallas_call | solution.py:605
  10.0 4.9 %all-to-all-start = ((bf16[8,384,128]{2,1,0:T(8,128)(2,1)}), bf16[8,384,128]{2,1,0:T(8,128)(2,1)S(1)}, u32[]{:S(2)}, u32[]{:S(2)}) async-start(bf16[8,384,128]{2,1,0:T(8,128)(2,1)} %pack.1), calls=%async_computation | async-start | bytes 1572864 | tf_op jit(solution)/shard_map/all_to_all | solution.py:584
  14.9 0.8 fusion.5
  15.8 0.7 fusion.12
  16.5 0.1 collective-permute-start.2
  16.5 4.0 %add_convert_fusion = (bf16[36,32,1152]{2,1,0:T(8,128)(2,1)}, bf16[36,32,1152]{2,1,0:T(8,128)(2,1)}) fusion(f32[32,1152]{1,0:T(8,128)S(1)} %get-tuple-element.46, f32[36,1152]{1,0:T(8,128)S(1)} %get-tuple-element.44, f32[32,1152]{1,0:T(8,128)S(1)} %get-tuple-element.45, f32[36,1152]{1,0:T(8,128)S(1)} %get-tuple-element.43), kind=kLoop, calls=%fused_computation | loop fusion | flops 10616832 | bytes 5935104 | tf_op jit(solution)/shard_map/convert_element_type | solution.py:56
  20.6 0.8 copy-done.4
  21.4 1.0 copy-done.5
  22.4 3.8 %product_grad.3.refs_1_ = f32[128,1024]{1,0:T(8,128)S(1)} custom-call(s32[1]{0:T(128)} %bitcast.place_ref, bf16[8192,1024]{1,0:T(8,128)(2,1)} %w_ref.9, bf16[128,2048]{1,0:T(8,128)(2,1)S(1)} %copy-done.3, bf16[128,2048]{1,0:T(8,128)(2,1)S(1)} %copy-done.5), custom_call_target="tpu_custom_call" | custom-call | tf_op jit(solution)/shard_map/product_grad/pallas_call | solution.py:134
  26.2 2.5 %product_grad.4.refs_1_ = f32[128,1024]{1,0:T(8,128)S(1)} custom-call(s32[1]{0:T(128)} %bitcast.place_ref, bf16[8192,1024]{1,0:T(8,128)(2,1)} %w_ref.9, bf16[128,2048]{1,0:T(8,128)(2,1)S(1)} %collective-permute-done.1.refs_0_, f32[128,1024]{1,0:T(8,128)S(1)} %product_grad.3.refs_1_), custom_call_target="tpu_custom_call" | custom-call | tf_op jit(solution)/shard_map/product_grad/pallas_call | solution.py:134
  28.8 4.4 %product_grad.5.grad_ref = f32[128,1024]{1,0:T(8,128)} custom-call(s32[1]{0:T(128)} %bitcast.place_ref, bf16[8192,1024]{1,0:T(8,128)(2,1)} %w_ref.9, bf16[128,2048]{1,0:T(8,128)(2,1)} %collective-permute-done.2.refs_0_, f32[128,1024]{1,0:T(8,128)S(1)} %product_grad.4.refs_1_), custom_call_target="tpu_custom_call" | custom-call | tf_op jit(solution)/shard_map/product_grad/pallas_call | solution.py:134
  33.2 2.2 %all-to-all-done.got_ref = bf16[8,384,128]{2,1,0:T(8,128)(2,1)S(1)} async-done(((bf16[8,384,128]{2,1,0:T(8,128)(2,1)}), bf16[8,384,128]{2,1,0:T(8,128)(2,1)S(1)}, u32[]{:S(2)}, u32[]{:S(2)}) %all-to-all-start) | async-done | bytes 786464 | tf_op jit(solution)/shard_map/all_to_all | solution.py:584
  35.5 6.0 %forward_spectral.1 = (bf16[8,256,128]{2,1,0:T(8,128)(2,1)S(1)}, f32[128,1024]{1,0:T(8,128)S(1)}, f32[1024,128]{1,0:T(8,128)S(1)}, f32[1024,128]{1,0:T(8,128)S(1)}, f32[6,1152,128]{2,1,0:T(8,128)S(1)}) custom-call(bf16[8,384,128]{2,1,0:T(8,128)(2,1)S(1)} %all-to-all-done.got_ref, bf16[3,128,1024]{2,1,0:T(8,128)(2,1)S(1)} %bitcast.13, ...), custom_call_target="tpu_custom_call" | custom-call | tf_op jit(solution)/shard_map/forward_spectral/pallas_call | solution.py:418
  41.5 18.7 %all_to_all.15.got_ref.grads_ref = bf16[8,256,128]{2,1,0:T(8,128)(2,1)S(1)} all-to-all(bf16[8,256,128]{2,1,0:T(8,128)(2,1)S(1)} %get-tuple-element.23), channel_id=1, replica_groups=mesh['seq'=8,'tensor'=4] {'seq'}, dimensions={0} | all-to-all | bytes 1048576 | tf_op jit(solution)/shard_map/all_to_all | solution.py:584
  60.2 2.6 %product.1 = (bf16[128,1024]{1,0:T(8,128)(2,1)S(1)}, f32[128,1024]{1,0:T(8,128)}, bf16[8,1024]{1,0:T(8,128)(2,1)S(1)}, f32[56,128]{1,0:T(8,128)S(1)}) custom-call(bf16[8,256,128]{2,1,0:T(8,128)(2,1)S(1)} %all_to_all.15.got_ref.grads_ref, f32[128,1024]{1,0:T(8,128)S(1)} %get-tuple-element.24.query_ref, f32[128,1024]{1,0:T(8,128)} %product_grad.5.grad_ref, ...), custom_call_target="tpu_custom_call" | custom-call | tf_op jit(solution)/shard_map/product/pallas_call | solution.py:642
  62.8 7.8 %backward_spectral.1 = bf16[8,576,128]{2,1,0:T(8,128)(2,1)} custom-call(bf16[8,384,128]{2,1,0:T(8,128)(2,1)S(1)} %all-to-all-done.got_ref, bf16[8,256,128]{2,1,0:T(8,128)(2,1)S(1)} %all_to_all.15.got_ref.grads_ref, f32[3,7,128]{2,1,0:T(8,128)S(1)} %dynamic-slice_bitcast_fusion.taps_ref, f32[56,128]{1,0:T(8,128)S(1)} %get-tuple-element.25.query_short_ref, ...), custom_call_target="tpu_custom_call" | custom-call | tf_op jit(solution)/shard_map/backward_spectral/pallas_call | solution.py:468
  70.7 5.5 %project.3 = (bf16[128,2048]{1,0:T(8,128)(2,1)}, f32[128,2048]{1,0:T(8,128)S(1)}) custom-call(s32[1]{0:T(128)} %bitcast.place_ref, bf16[128,1024]{1,0:T(8,128)(2,1)S(1)} %get-tuple-element.30.product_ref, bf16[8192,1024]{1,0:T(8,128)(2,1)} %w_ref.9), custom_call_target="tpu_custom_call" | custom-call | tf_op jit(solution)/shard_map/project/pallas_call | solution.py:539
  76.2 0.1 collective-permute-start.5
  76.3 3.7 %all-to-all-start.2 = ((bf16[8,576,128]{2,1,0:T(8,128)(2,1)}), bf16[8,576,128]{2,1,0:T(8,128)(2,1)S(1)}, u32[]{:S(2)}, u32[]{:S(2)}) async-start(bf16[8,576,128]{2,1,0:T(8,128)(2,1)} %backward_spectral.1), calls=%async_computation.2 | async-start | bytes 2359296 | tf_op jit(solution)/shard_map/all_to_all | solution.py:584
  79.9 5.2 %project.2 = (bf16[128,2048]{1,0:T(8,128)(2,1)S(1)}, f32[128,2048]{1,0:T(8,128)S(1)}) custom-call(s32[1]{0:T(128)} %bitcast.place_ref, bf16[128,1024]{1,0:T(8,128)(2,1)S(1)} %get-tuple-element.30.product_ref, bf16[8192,1024]{1,0:T(8,128)(2,1)} %w_ref.9), custom_call_target="tpu_custom_call" | custom-call | tf_op jit(solution)/shard_map/project/pallas_call | solution.py:539
  85.1 0.5 collective-permute-start.4
  85.6 1.2 %add_convert_fusion.2 = bf16[128,2048]{1,0:T(8,128)(2,1)S(1)} fusion(f32[128,2048]{1,0:T(8,128)S(1)} %get-tuple-element.33, bf16[128,2048]{1,0:T(8,128)(2,1)} %collective-permute-done.5), kind=kLoop, calls=%fused_computation.3 | loop fusion | flops 786432 | bytes 2097152 | tf_op jit(solution)/shard_map/convert_element_type | solution.py:677
  86.8 1.0 collective-permute-start.6
  87.7 1.3 %collective-permute-start.7 = (bf16[8,1024]{1,0:T(8,128)(2,1)S(1)}, bf16[8,1024]{1,0:T(8,128)(2,1)S(1)}, u32[]{:S(2)}, u32[]{:S(2)}) collective-permute-start(bf16[8,1024]{1,0:T(8,128)(2,1)S(1)} %get-tuple-element.36), channel_id=1, source_target_pairs={{4,0},{8,4},{12,8},{16,12},{20,16},{24,20},{28,24},{5,1},{9,5},{13... | collective-permute-start | bytes 49160 | tf_op jit(solution)/shard_map/ppermute | solution.py:32
  89.0 11.7 %collective-permute-done.6 = bf16[128,2048]{1,0:T(8,128)(2,1)S(1)} collective-permute-done((bf16[128,2048]{1,0:T(8,128)(2,1)S(1)}, bf16[128,2048]{1,0:T(8,128)(2,1)S(1)}, u32[]{:S(2)}, u32[]{:S(2)}) %collective-permute-start.6) | collective-permute-done | bytes 524320 | tf_op jit(solution)/shard_map/ppermute | solution.py:26
  100.8 1.0 add_convert_fusion.1
  101.8 7.7 %all-to-all-done.2.got_ref = bf16[8,576,128]{2,1,0:T(8,128)(2,1)S(1)} async-done(((bf16[8,576,128]{2,1,0:T(8,128)(2,1)}), bf16[8,576,128]{2,1,0:T(8,128)(2,1)S(1)}, u32[]{:S(2)}, u32[]{:S(2)}) %all-to-all-start.2) | async-done | bytes 1179680 | tf_op jit(solution)/shard_map/all_to_all | solution.py:584
  109.4 1.0 copy-done.2
  110.5 1.9 %finish.1 = (bf16[3,128,1024]{2,1,0:T(8,128)(2,1)}, f32[128,1024]{1,0:T(8,128)}, f32[120,1024]{1,0:T(8,128)}, f32[3,7,1024]{2,1,0:T(8,128)}) custom-call(bf16[8,576,128]{2,1,0:T(8,128)(2,1)S(1)} %all-to-all-done.2.got_ref, f32[128,1024]{1,0:T(8,128)S(1)} %copy-done.2, bf16[8,1024]{1,0:T(8,128)(2,1)S(1)} %collective-permute-done.7.next_ref, ...), custom_call_target="tpu_custom_call" | custom-call | tf_op jit(solution)/shard_map/finish/pallas_call | solution.py:683
  (24 shorter events, 0.1 us)
Async XLA Ops:
  0.6 19.9 %copy-start = (f32[120,1024]{1,0:T(8,128)S(1)}, f32[120,1024]{1,0:T(8,128)}, u32[]{:S(2)}) copy-start(f32[120,1024]{1,0:T(8,128)} %param.8) | copy-start | bytes 1474564
  0.6 20.7 %copy-start.3 = (bf16[128,2048]{1,0:T(8,128)(2,1)S(1)}, bf16[128,2048]{1,0:T(8,128)(2,1)}, u32[]{:S(2)}) copy-start(bf16[128,2048]{1,0:T(8,128)(2,1)} %refs_0_.1) | copy-start | bytes 1572868
  0.7 19.9 %copy-start.6 = (f32[7,3,1024]{2,0,1:T(8,128)S(1)}, f32[7,3,1024]{2,0,1:T(8,128)}, u32[]{:S(2)}) copy-start(f32[7,3,1024]{2,0,1:T(8,128)} %param.7) | copy-start | bytes 258052
  0.7 15.8 %collective-permute-start.1 = (bf16[128,2048]{1,0:T(8,128)(2,1)}, bf16[128,2048]{1,0:T(8,128)(2,1)S(1)}, u32[]{:S(2)}, u32[]{:S(2)}) collective-permute-start(bf16[128,2048]{1,0:T(8,128)(2,1)} %refs_0_.1), channel_id=1, source_target_pairs={{0,2},{1,3},{2,0},{3,1},{4,6},{5,7},{6,4},{7,5},{8,10},{9,11},{10,... | collective-permute-start | bytes 1572872 | tf_op jit(solution)/shard_map/ppermute | solution.py:26
  3.7 16.9 %collective-permute-start.3 = (bf16[128,2048]{1,0:T(8,128)(2,1)}, bf16[128,2048]{1,0:T(8,128)(2,1)S(1)}, u32[]{:S(2)}, u32[]{:S(2)}) collective-permute-start(bf16[128,2048]{1,0:T(8,128)(2,1)} %refs_0_.1), channel_id=1, source_target_pairs={{0,1},{1,0},{2,3},{3,2},{4,5},{5,4},{6,7},{7,6},{8,9},{9,8},{10,11... | collective-permute-start | bytes 1572872 | tf_op jit(solution)/shard_map/ppermute | solution.py:26
  4.4 28.8 %collective-permute-start = (bf16[8,1024]{1,0:T(8,128)(2,1)S(1)}, bf16[8,1024]{1,0:T(8,128)(2,1)S(1)}, u32[]{:S(2)}, u32[]{:S(2)}) collective-permute-start(bf16[8,1024]{1,0:T(8,128)(2,1)S(1)} %slice_bitcast_fusion), channel_id=1, source_target_pairs={{0,4},{4,8},{8,12},{12,16},{16,20},{20,24},{24,28},{1,5},{5,9},{9,... | collective-permute-start | bytes 49160 | tf_op jit(solution)/shard_map/ppermute | solution.py:32
  10.0 25.4 %all-to-all-start = ((bf16[8,384,128]{2,1,0:T(8,128)(2,1)}), bf16[8,384,128]{2,1,0:T(8,128)(2,1)S(1)}, u32[]{:S(2)}, u32[]{:S(2)}) async-start(bf16[8,384,128]{2,1,0:T(8,128)(2,1)} %pack.1), calls=%async_computation | async-start | bytes 1572864 | tf_op jit(solution)/shard_map/all_to_all | solution.py:584
  16.5 12.3 %collective-permute-start.2 = (bf16[128,2048]{1,0:T(8,128)(2,1)S(1)}, bf16[128,2048]{1,0:T(8,128)(2,1)}, u32[]{:S(2)}, u32[]{:S(2)}) collective-permute-start(bf16[128,2048]{1,0:T(8,128)(2,1)S(1)} %collective-permute-done.1.refs_0_), channel_id=1, source_target_pairs={{0,1},{1,0},{2,3},{3,2},{4,5},{5,4},{6,7},{7,6},{8,9},{9,8},{10,11... | collective-permute-start | bytes 1572872 | tf_op jit(solution)/shard_map/ppermute | solution.py:26
  20.6 0.8 copy-start.4
  21.4 1.0 copy-start.5
  28.7 6.7 %copy-start.1 = (bf16[128,3,1024]{2,0,1:T(8,128)(2,1)S(1)}, bf16[128,3,1024]{2,0,1:T(8,128)(2,1)}, u32[]{:S(2)}) copy-start(bf16[128,3,1024]{2,0,1:T(8,128)(2,1)} %param.6) | copy-start | bytes 2359300
  76.2 9.4 %collective-permute-start.5 = (bf16[128,2048]{1,0:T(8,128)(2,1)}, bf16[128,2048]{1,0:T(8,128)(2,1)}, u32[]{:S(2)}, u32[]{:S(2)}) collective-permute-start(bf16[128,2048]{1,0:T(8,128)(2,1)} %get-tuple-element.34), channel_id=1, source_target_pairs={{0,1},{1,0},{2,3},{3,2},{4,5},{5,4},{6,7},{7,6},{8,9},{9,8},{10,11... | collective-permute-start | bytes 1572872 | tf_op jit(solution)/shard_map/ppermute | solution.py:26
  76.3 33.2 %all-to-all-start.2 = ((bf16[8,576,128]{2,1,0:T(8,128)(2,1)}), bf16[8,576,128]{2,1,0:T(8,128)(2,1)S(1)}, u32[]{:S(2)}, u32[]{:S(2)}) async-start(bf16[8,576,128]{2,1,0:T(8,128)(2,1)} %backward_spectral.1), calls=%async_computation.2 | async-start | bytes 2359296 | tf_op jit(solution)/shard_map/all_to_all | solution.py:584
  85.1 3.9 %collective-permute-start.4 = (bf16[128,2048]{1,0:T(8,128)(2,1)S(1)}, bf16[128,2048]{1,0:T(8,128)(2,1)S(1)}, u32[]{:S(2)}, u32[]{:S(2)}) collective-permute-start(bf16[128,2048]{1,0:T(8,128)(2,1)S(1)} %get-tuple-element.32), channel_id=1, source_target_pairs={{0,1},{1,0},{2,3},{3,2},{4,5},{5,4},{6,7},{7,6},{8,9},{9,8},{10,11... | collective-permute-start | bytes 1572872 | tf_op jit(solution)/shard_map/ppermute | solution.py:26
  86.8 14.0 %collective-permute-start.6 = (bf16[128,2048]{1,0:T(8,128)(2,1)S(1)}, bf16[128,2048]{1,0:T(8,128)(2,1)S(1)}, u32[]{:S(2)}, u32[]{:S(2)}) collective-permute-start(bf16[128,2048]{1,0:T(8,128)(2,1)S(1)} %add_convert_fusion.2), channel_id=1, source_target_pairs={{0,2},{1,3},{2,0},{3,1},{4,6},{5,7},{6,4},{7,5},{8,10},{9,11},{10,... | collective-permute-start | bytes 1572872 | tf_op jit(solution)/shard_map/ppermute | solution.py:26
  87.7 14.0 %collective-permute-start.7 = (bf16[8,1024]{1,0:T(8,128)(2,1)S(1)}, bf16[8,1024]{1,0:T(8,128)(2,1)S(1)}, u32[]{:S(2)}, u32[]{:S(2)}) collective-permute-start(bf16[8,1024]{1,0:T(8,128)(2,1)S(1)} %get-tuple-element.36), channel_id=1, source_target_pairs={{4,0},{8,4},{12,8},{16,12},{20,16},{24,20},{28,24},{5,1},{9,5},{13... | collective-permute-start | bytes 49160 | tf_op jit(solution)/shard_map/ppermute | solution.py:32
  109.4 1.0 copy-start.2

commit v4 on v3

v4 whole, which is shorter than its diff:
```python
import math
from functools import partial

import jax
import jax.numpy as jnp
from jax import lax
from jax.experimental import pallas as pl
from jax.experimental.pallas import tpu as pltpu
from jax.sharding import PartitionSpec as P


F32 = jnp.float32
BF16 = jnp.bfloat16
HALO = 8
GROUP = 32
LANES = 128
CHUNK = 512
TABLE_LIMIT = 1 << 22


def dot(a, b):
    return lax.dot_general(a, b, (((1,), (0,)), ((), ())), preferred_element_type=F32)


def exchange(value, axis, flip):
    count = lax.axis_size(axis)
    return lax.ppermute(value, axis, [(source, source ^ flip) for source in range(count)])


def shift(value, axis, steps):
    count = lax.axis_size(axis)
    pairs = [(s, s + steps) for s in range(count) if 0 <= s + steps < count]
    return lax.ppermute(value, axis, pairs)


def whole(shape):
    return pl.BlockSpec(shape, lambda *_: (0,) * len(shape))


def spectral_sizes(tokens, medium_reach):
    need = tokens + -(-(medium_reach - 2) // 2)
    freqs = -(-need // 384) * 384
    return freqs, 384


def dft_tables(freqs):
    period = 8 * freqs
    unit = 2.0 * math.pi / period
    odd = 2 * jnp.arange(freqs, dtype=jnp.int32) + 1
    start = 2 * GROUP * jnp.arange(freqs // GROUP, dtype=jnp.int32)
    inner = 2 * jnp.arange(GROUP, dtype=jnp.int32) + 1
    first = (start[:, None] * odd[None, :] % period).astype(F32) * unit
    second = (inner[:, None] * odd[None, :] % period).astype(F32) * unit
    fc, fs = jnp.cos(first)[:, None], jnp.sin(first)[:, None]
    sc, ss = jnp.cos(second)[None], jnp.sin(second)[None]
    cosine = (fc * sc - fs * ss).astype(BF16).reshape(freqs, freqs)
    sine = (fs * sc + fc * ss).astype(BF16).reshape(freqs, freqs)
    return cosine, sine


def in_hbm(value):
    return pltpu.with_memory_space_constraint(value, pltpu.HBM)


def limit(mebibytes):
    return pltpu.CompilerParams(vmem_limit_bytes=mebibytes << 20)


def pack_kernel(x_ref, filter_ref, out_ref, streams, taps, rounded, sems):
    parts, rows, width = out_ref.shape
    length = rows // 3
    read_filter = pltpu.make_async_copy(filter_ref, taps, sems.at[0])
    read_streams = pltpu.make_async_copy(x_ref.at[pl.ds(1, 2)], streams, sems.at[1])
    read_filter.start()
    read_streams.start()
    read_filter.wait()
    for j in range(parts):
        rounded[j, 2 * length :, :] = taps[:, j * width : (j + 1) * width].astype(BF16)
    read_streams.wait()
    writes = []
    for j in range(parts):
        lanes = slice(j * width, (j + 1) * width)
        rounded[j, 0:length, :] = streams[0, :, lanes]
        rounded[j, length : 2 * length, :] = streams[1, :, lanes]
        writes.append(pltpu.make_async_copy(rounded.at[j], out_ref.at[j], sems.at[2 + j]))
        writes[j].start()
    for write in writes:
        write.wait()


def weight_chunks(place_ref, weight_ref, buffer, sems, flips, features):
    deep = buffer.shape[1]
    per = features // deep
    copies = []
    for i, flip in enumerate(flips):
        for k in range(per):
            start = jnp.bitwise_xor(place_ref[0], flip) * features + k * deep
            slot = i * per + k
            copies.append(
                pltpu.make_async_copy(
                    weight_ref.at[pl.ds(pl.multiple_of(start, deep), deep), :], buffer.at[slot], sems.at[slot]
                )
            )
    return copies


def chunk_scratch(weight, features, shards):
    deep = math.gcd(features, CHUNK)
    count = shards * (features // deep)
    return [pltpu.VMEM((count, deep, weight.shape[1]), weight.dtype), pltpu.SemaphoreType.DMA((count,))]


def summed(x_refs, copies, buffer, total):
    deep = buffer.shape[1]
    per = len(copies) // len(x_refs)
    for slot, copy in enumerate(copies):
        copy.wait()
        lanes = slice(slot % per * deep, (slot % per + 1) * deep)
        part = dot(x_refs[slot // per][:, lanes], buffer[slot])
        total = part if total is None else total + part
    return total


def product_grad_kernel(place_ref, w_ref, *refs, flips, last):
    x_refs = refs[: len(flips)]
    copies_in = []
    if last:
        acc_ref, x_ref, taps_ref, out_ref, query_ref, sent_ref, buffer, sems, ext, held, in_sems = refs[len(flips) :]
    else:
        out_ref, buffer, sems, held, in_sems = refs[len(flips) :]
    for i, ref in enumerate(x_refs):
        copies_in.append(pltpu.make_async_copy(ref, held.at[i], in_sems.at[i]))
        copies_in[i].start()
    copies = weight_chunks(place_ref, w_ref, buffer, sems, flips, held.shape[2])
    for copy in copies:
        copy.start()
    if last:
        length = x_ref.shape[1]
        ext[0:HALO, :] = jnp.zeros((HALO, ext.shape[1]), F32)
        ext[HALO:, :] = x_ref[0].astype(F32)
        query = taps_ref[0, 0:1, :] * ext[HALO : HALO + length, :]
        for i in range(1, taps_ref.shape[1]):
            query = query + taps_ref[0, i : i + 1, :] * ext[HALO - i : HALO - i + length, :]
        query_ref[...] = query
    for copy in copies_in:
        copy.wait()
    total = summed([held.at[i] for i in range(len(flips))], copies, buffer, acc_ref[...] if last else None)
    out_ref[...] = total
    if last:
        parts, _, width = sent_ref.shape
        for j in range(parts):
            lanes = slice(j * width, (j + 1) * width)
            sent_ref[j] = (total[:, lanes] * query_ref[:, lanes]).astype(BF16)


def grad_scratch(shards, weight, length, features):
    return chunk_scratch(weight, features, shards), [
        pltpu.VMEM((shards, length, features), BF16),
        pltpu.SemaphoreType.DMA((shards,)),
    ]


def product_grad_first(shards, weight, place, flips):
    length, features = shards[0].shape
    channels = weight.shape[1]
    hbm = pl.BlockSpec(memory_space=pltpu.HBM)
    chunks, inputs = grad_scratch(len(flips), weight, length, features)
    return pl.pallas_call(
        partial(product_grad_kernel, flips=flips, last=False),
        in_specs=[pl.BlockSpec(memory_space=pltpu.SMEM), hbm] + [pl.BlockSpec(memory_space=pl.ANY)] * len(shards),
        out_specs=pl.BlockSpec(memory_space=pltpu.VMEM),
        out_shape=jax.ShapeDtypeStruct((length, channels), F32),
        scratch_shapes=chunks + inputs,
        compiler_params=limit(16),
        name="grad_first",
    )(place, weight, in_hbm(shards[0]), *shards[1:])


def product_grad_last(shards, weight, place, flips, acc, streams, taps, parts):
    length, features = shards[0].shape
    channels = weight.shape[1]
    hbm = pl.BlockSpec(memory_space=pltpu.HBM)
    vmem = pl.BlockSpec(memory_space=pltpu.VMEM)
    full = whole((length, channels))
    chunks, inputs = grad_scratch(len(flips), weight, length, features)
    return pl.pallas_call(
        partial(product_grad_kernel, flips=flips, last=True),
        grid=(1,),
        in_specs=[pl.BlockSpec(memory_space=pltpu.SMEM)]
        + [hbm]
        + [pl.BlockSpec(memory_space=pl.ANY)] * len(shards)
        + [full, whole((1, length, channels)), whole(taps.shape)],
        out_specs=[full, full, whole((parts, length, channels // parts))],
        out_shape=[
            pltpu.HBM((length, channels), F32),
            pltpu.HBM((length, channels), F32),
            pltpu.HBM((parts, length, channels // parts), BF16),
        ],
        scratch_shapes=chunks + [pltpu.VMEM((length + HALO, channels), F32)] + inputs,
        compiler_params=limit(24),
        name="grad_last",
    )(place, weight, *shards, acc, streams, taps)


def edge_kernel(x_ref, edge_ref, taps_ref, grad_ref, _, __, query_ref, sent_ref, ext, query, sent, sems):
    parts, _, width = sent.shape
    ext[0:HALO, :] = edge_ref[0].astype(F32)
    ext[HALO:, :] = x_ref[0].astype(F32)[0:HALO]
    total = taps_ref[0, 0:1, :] * ext[HALO : 2 * HALO, :]
    for i in range(1, taps_ref.shape[1]):
        total = total + taps_ref[0, i : i + 1, :] * ext[HALO - i : 2 * HALO - i, :]
    query[...] = total
    for j in range(parts):
        lanes = slice(j * width, (j + 1) * width)
        sent[j] = (grad_ref[:, lanes] * total[:, lanes]).astype(BF16)
    copies = [
        pltpu.make_async_copy(query, query_ref.at[pl.ds(0, HALO), :], sems.at[0]),
        pltpu.make_async_copy(sent, sent_ref.at[:, pl.ds(0, HALO), :], sems.at[1]),
    ]
    for copy in copies:
        copy.start()
    for copy in copies:
        copy.wait()


def with_edge(streams, edge, taps, grad, query, sent):
    channels = streams.shape[2]
    parts, _, width = sent.shape
    hbm = pl.BlockSpec(memory_space=pltpu.HBM)
    return pl.pallas_call(
        edge_kernel,
        grid=(1,),
        in_specs=[
            whole((1, 2 * HALO, channels)),
            whole((1, HALO, channels)),
            whole(taps.shape),
            whole((HALO, channels)),
            hbm,
            hbm,
        ],
        out_specs=[hbm, hbm],
        out_shape=[pltpu.HBM(query.shape, F32), pltpu.HBM(sent.shape, BF16)],
        scratch_shapes=[
            pltpu.VMEM((2 * HALO, channels), F32),
            pltpu.VMEM((HALO, channels), F32),
            pltpu.VMEM((parts, HALO, width), BF16),
            pltpu.SemaphoreType.DMA((2,)),
        ],
        input_output_aliases={4: 0, 5: 1},
        compiler_params=limit(4),
        name="edge_rows",
    )(streams, edge, taps, in_hbm(grad), in_hbm(query), in_hbm(sent))


def filtered(taps_ref, stream, ext, begin, length):
    total = taps_ref[stream + 1, 0:1, :] * ext[stream, HALO + begin : HALO + begin + length, :]
    for i in range(1, taps_ref.shape[1]):
        first = HALO + begin - i
        total = total + taps_ref[stream + 1, i : i + 1, :] * ext[stream, first : first + length, :]
    return total


def extend(got_ref, ext):
    parts, _, width = got_ref.shape
    length = (ext.shape[1] - HALO) // parts
    ext[:, 0:HALO, :] = jnp.zeros((2, HALO, width), F32)
    for s in range(parts):
        here = slice(HALO + s * length, HALO + (s + 1) * length)
        ext[0, here, :] = got_ref[s, 0:length, :].astype(F32)
        ext[1, here, :] = got_ref[s, length : 2 * length, :].astype(F32)


def forward_begin(got_ref, taps_ref, medium_ref, kept, ext, signals, medium):
    parts, rows, width = got_ref.shape
    length = rows // 3
    extend(got_ref, ext)
    for s in range(parts):
        here = slice(s * length, (s + 1) * length)
        key = filtered(taps_ref, 0, ext, s * length, length)
        value = filtered(taps_ref, 1, ext, s * length, length)
        kept[0, here, :] = key
        kept[1, here, :] = value
        signals[here, 0:width] = (key * value).astype(BF16)
        signals[here, width : 2 * width] = got_ref[s, 2 * length : 3 * length, :]
    medium[...] = jnp.zeros_like(medium)
    medium[0 : medium_ref.shape[0], :] = medium_ref[...].astype(BF16)


def forward_spectra(cosine, sine, signals, medium):
    tokens, double = signals.shape
    width = double // 2
    kept = medium.shape[0]
    both_c = dot(cosine[:, 0:tokens], signals[...])
    both_s = dot(sine[:, 0:tokens], signals[...])
    mc = dot(cosine[:, 0:kept], medium[...])
    ms = dot(sine[:, 0:kept], medium[...])
    ac, hc, as_, hs = (both_c[:, :width], both_c[:, width:], both_s[:, :width], both_s[:, width:])
    xc = ac * mc - as_ * ms
    xs = ac * ms + as_ * mc
    saved = (ac, as_, mc, ms, hc, hs)
    return saved, (xc * hc - xs * hs).astype(BF16), (xc * hs + xs * hc).astype(BF16)


def forward_end(out_ref, acc, freqs):
    parts, length, _ = out_ref.shape
    for s in range(parts):
        first = s * length + 1
        out_ref[s] = (acc[first : first + length, :] * (1.0 / freqs)).astype(BF16)


def block_copies(tables, held, spectra, spectra_held, sems, blocks):
    size = held.shape[1] // blocks
    groups = []
    for b in range(blocks):
        here = pl.ds(b * size, size)
        group = [pltpu.make_async_copy(t.at[here, :], held.at[i, here, :], sems.at[i, b]) for i, t in enumerate(tables)]
        if spectra is not None:
            group.append(pltpu.make_async_copy(spectra.at[:, here, :], spectra_held.at[:, here, :], sems.at[2, b]))
        groups.append(group)
    return groups


def start_all(copies):
    for copy in copies:
        copy.start()


def wait_all(copies):
    for copy in copies:
        copy.wait()


def forward_kernel(got_ref, taps_ref, medium_ref, cos_ref, sin_ref, *refs, freqs, block, resident):
    if not resident:
        cos_across_ref, sin_across_ref, *refs = refs
    out_ref, kept_ref, spectra_ref, ext, signals, medium, acc, kept, kept_sem, *refs = refs
    rows = acc.shape[0]
    step = pl.program_id(0)
    keep = pltpu.make_async_copy(kept, kept_ref, kept_sem)

    if resident:
        held, yc_all, ys_all, spectra_held, sems, out_sems = refs
        blocks = freqs // block
        groups = block_copies((cos_ref, sin_ref), held, None, None, sems, blocks)
        for group in groups:
            start_all(group)
        forward_begin(got_ref, taps_ref, medium_ref, kept, ext, signals, medium)
        keep.start()
        writes = []
        for b, group in enumerate(groups):
            wait_all(group)
            here = slice(b * block, (b + 1) * block)
            saved, yc, ys = forward_spectra(held[0, here, :], held[1, here, :], signals, medium)
            for i, spectrum in enumerate(saved):
                spectra_held[i, here, :] = spectrum
            there = pl.ds(b * block, block)
            writes.append(
                pltpu.make_async_copy(spectra_held.at[:, there, :], spectra_ref.at[:, there, :], out_sems.at[b])
            )
            writes[b].start()
            yc_all[here, :] = yc
            ys_all[here, :] = ys
        acc[...] = dot(held[0, 0:rows, :], yc_all[...]) + dot(held[1, 0:rows, :], ys_all[...])
        forward_end(out_ref, acc, freqs)
        wait_all(writes)
        keep.wait()
        return

    @pl.when(step == 0)
    def _():
        forward_begin(got_ref, taps_ref, medium_ref, kept, ext, signals, medium)
        keep.start()
        keep.wait()
        acc[...] = jnp.zeros_like(acc)

    saved, yc, ys = forward_spectra(cos_ref[...], sin_ref[...], signals, medium)
    for i, spectrum in enumerate(saved):
        spectra_ref[i] = spectrum
    acc[...] += dot(cos_across_ref[0:rows, :], yc) + dot(sin_across_ref[0:rows, :], ys)

    @pl.when(step == pl.num_programs(0) - 1)
    def _():
        forward_end(out_ref, acc, freqs)


def backward_begin(grads_ref, delayed, signal):
    parts, length, _ = grads_ref.shape
    delayed[...] = jnp.zeros_like(delayed)
    for s in range(parts):
        delayed[s * length + 1 : (s + 1) * length + 1, :] = grads_ref[s].astype(F32)
    signal[...] = delayed[...].astype(BF16)


def backward_spectra(cosine, sine, signal, spectra):
    gc = dot(cosine, signal[...])
    gs = dot(sine, signal[...])
    ac, as_, mc, ms, hc, hs = spectra
    uc = hc * gc + hs * gs
    us = hc * gs - hs * gc
    xc = ac * mc - as_ * ms
    xs = ac * ms + as_ * mc
    both_c = jnp.concatenate([xc * gc + xs * gs, mc * uc + ms * us], 1).astype(BF16)
    both_s = jnp.concatenate([xc * gs - xs * gc, mc * us - ms * uc], 1).astype(BF16)
    return both_c, both_s, (ac * uc + as_ * us).astype(BF16), (ac * us - as_ * uc).astype(BF16)


def backward_end(
    streams, taps_ref, kept, out_ref, small_ref, ext, after, acc, tap_acc, freqs, scale, medium_reach
):
    parts, _, width = out_ref.shape
    extend(streams, ext)
    length = (ext.shape[1] - HALO) // parts
    tokens = parts * length
    reach = taps_ref.shape[1]
    inverse = 1.0 / freqs
    small_ref[...] = jnp.zeros_like(small_ref)
    small_ref[0:medium_reach, :] = tap_acc[0:medium_reach, :] * (inverse * scale)
    after[:, tokens : tokens + HALO, :] = jnp.zeros((2, HALO, width), F32)
    first = length + 2 * HALO
    for s in range(parts):
        here = slice(s * length, (s + 1) * length)
        out_ref[s, first : first + length, :] = (acc[here, 0:width] * (inverse * scale)).astype(BF16)
        gated = acc[here, width : 2 * width] * inverse
        out_ref[s, 0:length, :] = gated.astype(BF16)
        after[0, here, :] = gated * kept[1, here, :]
        after[1, here, :] = gated * kept[0, here, :]
    for j in range(2):
        sums = [jnp.zeros((8, width), F32) for _ in range(reach)]
        for s in range(parts):
            begin = s * length
            own = after[j, begin : begin + length, :]
            for i in range(reach):
                moved = ext[j, HALO + begin - i : HALO + begin - i + length, :]
                sums[i] = sums[i] + jnp.sum((moved * own).reshape(length // 8, 8, width), 0)
        for i in range(reach):
            row = medium_reach + j * reach + i
            small_ref[row : row + 1, :] = jnp.sum(sums[i], 0, keepdims=True) * scale
    small = small_ref[...].astype(BF16)
    first = 2 * length + 2 * HALO
    for s in range(parts):
        end = (s + 1) * length
        for j in range(2):
            rows = slice(length + j * HALO, length + (j + 1) * HALO)
            out_ref[s, rows, :] = after[j, end : end + HALO, :].astype(BF16)
        out_ref[s, first : first + small.shape[0], :] = small


def backward_kernel(
    grads_ref, taps_ref, got_ref, kept_ref, spectra_ref, cos_ref, sin_ref, *refs,
    freqs, block, scale, medium_reach, resident,
):
    if not resident:
        cos_across_ref, sin_across_ref, *refs = refs
    out_ref, small, delayed, signal, ext, after, acc, tap_acc, streams, kept, late_sems, *refs = refs
    step = pl.program_id(0)
    size = signal.shape[0]
    rows, taps_kept = (acc.shape[0], tap_acc.shape[0])
    late = [
        pltpu.make_async_copy(kept_ref, kept, late_sems.at[0]),
        pltpu.make_async_copy(got_ref.at[:, pl.ds(0, streams.shape[1]), :], streams, late_sems.at[1]),
    ]

    def end():
        wait_all(late)
        backward_end(
            streams, taps_ref, kept, out_ref, small, ext, after, acc, tap_acc, freqs, scale, medium_reach
        )

    if resident:
        held, both_c_all, both_s_all, taps_c_all, taps_s_all, spectra_held, sems = refs
        groups = block_copies((cos_ref, sin_ref), held, spectra_ref, spectra_held, sems, freqs // block)
        for group in groups:
            start_all(group)
        start_all(late)
        backward_begin(grads_ref, delayed, signal)
        for b, group in enumerate(groups):
            wait_all(group)
            here = slice(b * block, (b + 1) * block)
            spectra = [spectra_held[i, here, :] for i in range(spectra_held.shape[0])]
            both_c_all[here, :], both_s_all[here, :], taps_c_all[here, :], taps_s_all[here, :] = backward_spectra(
                held[0, here, 0:size], held[1, here, 0:size], signal, spectra
            )
        acc[...] = dot(held[0, 0:rows, :], both_c_all[...]) + dot(held[1, 0:rows, :], both_s_all[...])
        tap_acc[...] = dot(held[0, 0:taps_kept, :], taps_c_all[...]) + dot(held[1, 0:taps_kept, :], taps_s_all[...])
        end()
        return

    @pl.when(step == 0)
    def _():
        backward_begin(grads_ref, delayed, signal)
        acc[...] = jnp.zeros_like(acc)
        tap_acc[...] = jnp.zeros_like(tap_acc)

    spectra = [spectra_ref[i] for i in range(spectra_ref.shape[0])]
    both_c, both_s, taps_c, taps_s = backward_spectra(cos_ref[:, 0:size], sin_ref[:, 0:size], signal, spectra)
    acc[...] += dot(cos_across_ref[0:rows, :], both_c) + dot(sin_across_ref[0:rows, :], both_s)
    tap_acc[...] += dot(cos_across_ref[0:taps_kept, :], taps_c) + dot(sin_across_ref[0:taps_kept, :], taps_s)

    @pl.when(step == pl.num_programs(0) - 1)
    def _():
        start_all(late)
        end()


def spectral_plan(freqs, block, tables):
    if freqs * freqs <= TABLE_LIMIT:
        hbm = pl.BlockSpec(memory_space=pltpu.HBM)
        return True, 1, [hbm, hbm], [in_hbm(t) for t in tables]
    rows = pl.BlockSpec((block, freqs), lambda j: (j, 0))
    columns = pl.BlockSpec((freqs, block), lambda j: (0, j))
    return False, freqs // block, [rows, rows, columns, columns], [*tables, *tables]


def held_scratch(freqs, block, width, widths, kinds):
    blocks = freqs // block
    return (
        [pltpu.VMEM((2, freqs, freqs), BF16)]
        + [pltpu.VMEM((freqs, w), BF16) for w in widths]
        + [pltpu.VMEM((6, freqs, width), F32), pltpu.SemaphoreType.DMA((kinds, blocks))]
    )


def forward_call(got, taps, medium_taps, tables, freqs, block):
    parts, tall, width = got.shape
    length = tall // 3
    tokens = parts * length
    padded = -(-medium_taps.shape[0] // 128) * 128
    resident, steps, specs, operands = spectral_plan(freqs, block, tables)
    per = freqs // steps
    hbm = pl.BlockSpec(memory_space=pltpu.HBM)
    return pl.pallas_call(
        partial(forward_kernel, freqs=freqs, block=block, resident=resident),
        grid=(steps,),
        in_specs=[whole(got.shape), whole(taps.shape), whole(medium_taps.shape)] + specs,
        out_specs=[
            whole((parts, length, width)),
            hbm,
            hbm if resident else pl.BlockSpec((6, per, width), lambda j: (0, j, 0)),
        ],
        out_shape=[
            pltpu.HBM((parts, length, width), BF16),
            pltpu.HBM((2, tokens, width), F32),
            pltpu.HBM((6, freqs, width), F32),
        ],
        scratch_shapes=[
            pltpu.VMEM((2, tokens + HALO, width), F32),
            pltpu.VMEM((tokens, 2 * width), BF16),
            pltpu.VMEM((padded, width), BF16),
            pltpu.VMEM((tokens + HALO, width), F32),
            pltpu.VMEM((2, tokens, width), F32),
            pltpu.SemaphoreType.DMA,
        ]
        + (
            held_scratch(freqs, block, width, (width, width), 2) + [pltpu.SemaphoreType.DMA((freqs // block,))]
            if resident
            else []
        ),
        compiler_params=limit(32 if resident else 60),
        name="forward_spectral",
    )(in_hbm(got), taps, medium_taps, *operands)


def backward_call(got, grads, taps, kept, spectra, tables, freqs, block, scale, medium_reach, rows, small, extra):
    parts, tall, width = got.shape
    length = tall // 3
    tokens = parts * length
    padded = -(-medium_reach // 128) * 128
    late = -(-(tokens + 1) // 128) * 128
    resident, steps, specs, operands = spectral_plan(freqs, block, tables)
    per = freqs // steps
    hbm = pl.BlockSpec(memory_space=pltpu.HBM)
    return pl.pallas_call(
        partial(
            backward_kernel, freqs=freqs, block=block, scale=scale, medium_reach=medium_reach, resident=resident
        ),
        grid=(steps,),
        in_specs=[
            whole((parts, length, width)),
            whole(taps.shape),
            hbm,
            hbm,
            hbm if resident else pl.BlockSpec((6, per, width), lambda j: (0, j, 0)),
        ]
        + specs,
        out_specs=whole((parts, rows + small + extra, width)),
        out_shape=pltpu.HBM((parts, rows + small + extra, width), BF16),
        scratch_shapes=[
            pltpu.VMEM((small, width), F32),
            pltpu.VMEM((late, width), F32),
            pltpu.VMEM((late, width), BF16),
            pltpu.VMEM((2, tokens + HALO, width), F32),
            pltpu.VMEM((2, tokens + HALO, width), F32),
            pltpu.VMEM((tokens, 2 * width), F32),
            pltpu.VMEM((padded, width), F32),
            pltpu.VMEM((parts, 2 * length, width), BF16),
            pltpu.VMEM((2, tokens, width), F32),
            pltpu.SemaphoreType.DMA((2,)),
        ]
        + (held_scratch(freqs, block, width, (2 * width, 2 * width, width, width), 3) if resident else []),
        compiler_params=limit(40 if resident else 60),
        name="backward_spectral",
    )(in_hbm(grads), taps, in_hbm(got), in_hbm(kept), in_hbm(spectra), *operands)


def product_kernel(
    got_ref, query_ref, grad_ref, x_ref, edge_ref, _, product_ref, query_grad_ref, first_ref, back_ref,
    ext, taps, rounded, sem, *, reach, begin,
):
    parts, length, width = got_ref.shape
    ext[0:HALO, :] = edge_ref[0].astype(F32)
    ext[HALO:, :] = x_ref[0].astype(F32)
    taps[...] = jnp.zeros_like(taps)
    for j in range(parts):
        lanes = slice(j * width, (j + 1) * width)
        convolved = got_ref[j].astype(F32)
        product_ref[:, lanes] = (query_ref[:, lanes] * convolved).astype(BF16)
        own = grad_ref[:, lanes] * convolved
        query_grad_ref[:, lanes] = own
        first_ref[:, lanes] = own[0:HALO].astype(BF16)
        for i in range(reach):
            moved = ext[HALO - i : HALO - i + length, lanes]
            taps[j * reach + i : j * reach + i + 1, :] = jnp.sum(moved * own, 0, keepdims=True)
    for s in range(parts):
        rounded[s] = taps[...].astype(BF16)
    write = pltpu.make_async_copy(rounded, back_ref.at[:, pl.ds(begin, taps.shape[0]), :], sem)
    write.start()
    write.wait()


def product_call(convolved, query, grad, streams, edge, back, reach, begin):
    parts, length, width = convolved.shape
    channels = parts * width
    extra = back.shape[1] - begin
    hbm = pl.BlockSpec(memory_space=pltpu.HBM)
    full = whole((length, channels))
    return pl.pallas_call(
        partial(product_kernel, reach=reach, begin=begin),
        grid=(1,),
        in_specs=[
            whole((parts, length, width)),
            full,
            full,
            whole((1, length, channels)),
            whole((1, HALO, channels)),
            hbm,
        ],
        out_specs=[full, full, whole((HALO, channels)), hbm],
        out_shape=[
            pltpu.HBM((length, channels), BF16),
            pltpu.HBM((length, channels), F32),
            pltpu.HBM((HALO, channels), BF16),
            pltpu.HBM(back.shape, BF16),
        ],
        scratch_shapes=[
            pltpu.VMEM((length + HALO, channels), F32),
            pltpu.VMEM((extra, width), F32),
            pltpu.VMEM((parts, extra, width), BF16),
            pltpu.SemaphoreType.DMA,
        ],
        input_output_aliases={5: 3},
        compiler_params=limit(16),
        name="product",
    )(convolved, in_hbm(query), in_hbm(grad), streams, edge, in_hbm(back))


def project_kernel(place_ref, product_ref, w_ref, *refs, flips):
    out_refs = refs[: len(flips)]
    buffer, sems = refs[len(flips) :]
    copies = weight_chunks(place_ref, w_ref, buffer, sems, flips, out_refs[0].shape[1])
    start_all(copies)
    deep = buffer.shape[1]
    per = len(copies) // len(flips)
    for slot, copy in enumerate(copies):
        copy.wait()
        part = lax.dot_general(
            product_ref[...], buffer[slot], (((1,), (1,)), ((), ())), preferred_element_type=F32
        )
        lanes = slice(slot % per * deep, (slot % per + 1) * deep)
        out = out_refs[slot // per]
        out[:, lanes] = part.astype(out.dtype)


def project(product, weight, place, flips, features, dtypes):
    length = product.shape[0]
    vmem = pl.BlockSpec(memory_space=pltpu.VMEM)
    return pl.pallas_call(
        partial(project_kernel, flips=flips),
        in_specs=[pl.BlockSpec(memory_space=pltpu.SMEM), vmem, pl.BlockSpec(memory_space=pltpu.HBM)],
        out_specs=[vmem] * len(flips),
        out_shape=[jax.ShapeDtypeStruct((length, features), dtype) for dtype in dtypes],
        scratch_shapes=chunk_scratch(weight, features, len(flips)),
        compiler_params=limit(16),
        name="project",
    )(place, product, weight)


def local_kernel(x_ref, edge_ref, taps_ref, out_ref, ext):
    _, length, channels = out_ref.shape
    for j in range(2):
        ext[0:HALO, :] = edge_ref[j + 1].astype(F32)
        ext[HALO:, :] = x_ref[j + 1].astype(F32)
        for begin in range(0, channels, LANES):
            lanes = slice(begin, min(begin + LANES, channels))
            total = taps_ref[j + 1, 0:1, lanes] * ext[HALO : HALO + length, lanes]
            for i in range(1, taps_ref.shape[1]):
                total = total + taps_ref[j + 1, i : i + 1, lanes] * ext[HALO - i : HALO - i + length, lanes]
            out_ref[j, :, lanes] = total


def finish_kernel(
    got_ref, query_grad_ref, next_ref, taps_ref, local_ref,
    input_grad_ref, filter_ref, medium_ref, short_ref, ext, sums, *, scale, own_rows,
):
    parts, _, width = got_ref.shape
    length = filter_ref.shape[0]
    reach = taps_ref.shape[1]
    medium_reach = medium_ref.shape[0]
    ext[0, 0:length, :] = query_grad_ref[...]
    ext[0, length:, :] = next_ref[...].astype(F32)
    after = length + 2 * HALO
    for j in range(parts):
        lanes = slice(j * width, (j + 1) * width)
        gated = got_ref[j, 0:length, :].astype(F32)
        ext[1, 0:length, lanes] = gated * local_ref[1, :, lanes]
        ext[2, 0:length, lanes] = gated * local_ref[0, :, lanes]
        ext[1, length:, lanes] = got_ref[j, length : length + HALO, :].astype(F32)
        ext[2, length:, lanes] = got_ref[j, length + HALO : after, :].astype(F32)
        filter_ref[:, lanes] = got_ref[j, after : after + length, :].astype(F32)
        small = got_ref[j, after + length : after + length + own_rows, :].astype(F32)
        medium_ref[:, lanes] = small[0:medium_reach, :]
        first = medium_reach + reach
        short_ref[1, :, lanes] = small[medium_reach:first, :]
        short_ref[2, :, lanes] = small[first : first + reach, :]
        for k in range(3):
            total = taps_ref[k, 0:1, lanes] * ext[k, 0:length, lanes]
            for i in range(1, reach):
                total = total + taps_ref[k, i : i + 1, lanes] * ext[k, i : i + length, lanes]
            input_grad_ref[k, :, lanes] = total.astype(BF16)
    first = after + length + own_rows
    total = got_ref[0, first:, :].astype(F32)
    for j in range(1, parts):
        total = total + got_ref[j, first:, :].astype(F32)
    sums[...] = total
    for j in range(parts):
        short_ref[0, :, j * width : (j + 1) * width] = sums[j * reach : (j + 1) * reach, :] * scale


def reshard(value):
    return lax.all_to_all(value, "seq", split_axis=0, concat_axis=0, tiled=True)


def local(inputs, short_taps, medium_taps, long_filter, out_weight, out_cotangent):
    length, groups, channels = inputs.shape
    reach = short_taps.shape[0]
    medium_reach = medium_taps.shape[0]
    parts = lax.axis_size("seq")
    position = lax.axis_index("seq")
    place = lax.axis_index("tensor").astype(jnp.int32)[None]
    features = out_cotangent.shape[1]
    width = channels // parts
    tokens = length * parts
    scale = 1.0 / math.sqrt(tokens)
    freqs, block = spectral_sizes(tokens, medium_reach)
    vmem = pl.BlockSpec(memory_space=pltpu.VMEM)

    weight = pltpu.with_memory_space_constraint(out_weight, pltpu.HBM)
    streams = inputs.transpose(1, 0, 2)
    taps = short_taps.transpose(1, 0, 2)
    hbm = pl.BlockSpec(memory_space=pltpu.HBM)
    packed = pl.pallas_call(
        pack_kernel,
        in_specs=[hbm, hbm],
        out_specs=hbm,
        out_shape=pltpu.HBM((parts, 3 * length, width), BF16),
        scratch_shapes=[
            pltpu.VMEM((2, length, channels), BF16),
            pltpu.VMEM((length, channels), F32),
            pltpu.VMEM((parts, 3 * length, width), BF16),
            pltpu.SemaphoreType.DMA((2 + parts,)),
        ],
        compiler_params=limit(8),
        name="pack",
    )(
        pltpu.with_memory_space_constraint(streams, pltpu.HBM),
        pltpu.with_memory_space_constraint(long_filter, pltpu.HBM),
    )
    got = reshard(packed)
    edge = shift(streams[:, length - HALO :], "seq", 1)
    cot_x = exchange(out_cotangent, "tensor", 2)
    cot_core = exchange(out_cotangent, "tensor", 1)

    tables = dft_tables(freqs)
    own_taps = lax.dynamic_slice_in_dim(taps, position * width, width, 2)
    own_medium = lax.dynamic_slice_in_dim(medium_taps, position * width, width, 1)

    acc = product_grad_first((out_cotangent, cot_core), weight, place, (0, 1))
    cot_far = exchange(cot_x, "tensor", 1)
    product_grad, query, sent = product_grad_last((cot_x, cot_far), weight, place, (2, 3), acc, streams, taps, parts)
    query, sent = with_edge(streams, edge, taps, product_grad, query, sent)
    grads = reshard(sent)

    convolved, kept, spectra = forward_call(got, own_taps, own_medium, tables, freqs, block)
    convolved = reshard(convolved)

    rows = 2 * length + 2 * HALO
    small = -(-(medium_reach + 2 * reach) // 16) * 16
    extra = -(-parts * reach // 16) * 16
    back = backward_call(
        got, grads, own_taps, kept, spectra, tables, freqs, block, scale, medium_reach, rows, small, extra
    )
    product, query_grad, first_rows, back = product_call(
        convolved, query, product_grad, streams, edge, back, reach, rows + small
    )
    returned = reshard(back)

    (far,) = project(product, weight, place, (3,), features, (BF16,))
    far_core = exchange(far, "tensor", 1)
    (across,) = project(product, weight, place, (2,), features, (F32,))
    across_sum = exchange((across + far_core.astype(F32)).astype(BF16), "tensor", 2)
    near, own = project(product, weight, place, (1, 0), features, (BF16, F32))
    near_core = exchange(near, "tensor", 1)
    next_grad = shift(first_rows, "seq", -1)

    local_features = pl.pallas_call(
        local_kernel,
        in_specs=[vmem] * 3,
        out_specs=vmem,
        out_shape=pltpu.HBM((2, length, channels), F32),
        scratch_shapes=[pltpu.VMEM((length + HALO, channels), F32)],
        compiler_params=limit(8),
        name="local",
    )(in_hbm(streams), edge, taps)
    input_grad, filter_grad, medium_grad, short_grad = pl.pallas_call(
        partial(finish_kernel, scale=scale, own_rows=small),
        grid=(1,),
        in_specs=[
            whole((parts, rows + small + extra, width)),
            whole((length, channels)),
            whole((HALO, channels)),
            whole(taps.shape),
            whole((2, length, channels)),
        ],
        out_specs=[
            whole((groups, length, channels)),
            whole((length, channels)),
            whole((medium_reach, channels)),
            whole((groups, reach, channels)),
        ],
        out_shape=[
            jax.ShapeDtypeStruct((groups, length, channels), BF16),
            jax.ShapeDtypeStruct((length, channels), F32),
            jax.ShapeDtypeStruct((medium_reach, channels), F32),
            jax.ShapeDtypeStruct((groups, reach, channels), F32),
        ],
        scratch_shapes=[
            pltpu.VMEM((groups, length + HALO, channels), F32),
            pltpu.VMEM((extra, width), F32),
        ],
        compiler_params=limit(16),
        name="finish",
    )(returned, query_grad, next_grad, taps, in_hbm(local_features))

    output = (own + near_core.astype(F32) + across_sum.astype(F32)).astype(BF16)
    return (
        output,
        input_grad.transpose(1, 0, 2),
        filter_grad,
        medium_grad,
        short_grad.transpose(1, 0, 2),
    )


def solution(mesh):
    return jax.shard_map(
        local,
        mesh=mesh,
        in_specs=(
            P("seq", None, "tensor"),
            P(None, None, "tensor"),
            P(None, "tensor"),
            P("seq", "tensor"),
            P(None, "tensor"),
            P("seq", "tensor"),
        ),
        out_specs=(
            P("seq", "tensor"),
            P("seq", None, "tensor"),
            P("seq", "tensor"),
            P(None, "tensor"),
            P(None, None, "tensor"),
        ),
        check_vma=False,
    )
```

time: 113 us -> 109 us (0.965)
  blocking collectives: 18.7 us -> 0 us
  starting transfers between devices: 17.9 us -> 29.2 us
  Pallas kernels: 42 us -> 50.8 us
  waiting for transfers between devices: 21.7 us -> 17.3 us
    all_to_all x1 -> x0, blocking collectives: 18.7 us -> none  [reshard(): return lax.all_to_all(value, 'seq', split_axis=0, concat_axis=0, tiled=True)]
    all_to_all x2 -> x4, starting transfers between devices: 8.56 us -> 20.5 us  [reshard(): return lax.all_to_all(value, 'seq', split_axis=0, concat_axis=0, tiled=True)]
    pallas_call x5 -> x6, Pallas kernels: 15.3 us -> 21 us  [the longest x1 4.81 us: product_grad_last(): pl.pallas_call(partial(product_grad_kernel, flips=flips, last=True), grid...]
    all_to_all x2 -> x4, waiting for transfers between devices: 9.91 us -> 7.54 us  [reshard(): return lax.all_to_all(value, 'seq', split_axis=0, concat_axis=0, tiled=True)]
    ppermute x6, waiting for transfers between devices: 11.8 us -> 9.73 us  [exchange(): lax.ppermute(value, axis, [(source, source ^ flip) for source in range(co...]
    unnamed x14 -> x20, local copies, waits for them, and re-layouts: 2.9 us -> 1 us
    pallas_call x2 -> x3, Pallas kernels: 10.7 us -> 11.7 us  [project(): pl.pallas_call(partial(project_kernel, flips=flips), in_specs=[pl.BlockSp...]
  transfers between devices with their start and end apart: 10 -> 12, of which waited for: 3 -> 4; matrix products, arithmetic and copies ran while one was open for 7% -> 8% of each run, Pallas kernels for 16% -> 37%
where the time goes in v4:
time: 109 us; the launch traced here: 108 us
  Pallas kernels  50.8 us (47%)
  starting transfers between devices  29.2 us (27%)
  waiting for transfers between devices  17.3 us (16%)
  other arithmetic  7.31 us (7%)
  local copies, waits for them, and re-layouts  2.54 us (2%)
    all_to_all x4, starting transfers between devices, reshard(): return lax.all_to_all(value, 'seq', split_axis=0, concat_axis=0, tiled=True)  20.5 us
    pallas_call x3, Pallas kernels, project(): pl.pallas_call(partial(project_kernel, flips=flips), in_specs=[pl.BlockSp...  11.7 us
    ppermute x6, waiting for transfers between devices, exchange(): lax.ppermute(value, axis, [(source, source ^ flip) for source in range(co...  9.73 us
    pallas_call x1, Pallas kernels, backward_call(): pl.pallas_call(partial(backward_kernel, freqs=freqs, block=block, scale=s...  8.92 us
    all_to_all x4, waiting for transfers between devices, reshard(): return lax.all_to_all(value, 'seq', split_axis=0, concat_axis=0, tiled=True)  7.54 us
    pallas_call x1, Pallas kernels, forward_call(): pl.pallas_call(partial(forward_kernel, freqs=freqs, block=block, resident...  7.05 us
    pallas_call x1, Pallas kernels, product_grad_last(): pl.pallas_call(partial(product_grad_kernel, flips=flips, last=True), grid...  4.81 us
    ppermute x2, starting transfers between devices, shift(): return lax.ppermute(value, axis, pairs)  4.69 us
  transfers between devices with their start and end apart: 12, of which 4 were waited for; matrix products, arithmetic and copies ran while one was open for 8% of the time, Pallas kernels for 37%

profile of v4, /device:TPU:0, one launch (start us, length us, event | category | flops | bytes accessed | tf_op | source)
XLA Modules:
  0.0 108.1 jit_solution(13032138754190255562)
XLA Ops:
  0.6 0.6 collective-permute-start.3
  1.2 2.6 %collective-permute-start.1 = (bf16[128,2048]{1,0:T(8,128)(2,1)}, bf16[128,2048]{1,0:T(8,128)(2,1)S(1)}, u32[]{:S(2)}, u32[]{:S(2)}) collective-permute-start(bf16[128,2048]{1,0:T(8,128)(2,1)} %refs_0_.1), channel_id=1, source_target_pairs={{0,2},{1,3},{2,0},{3,1},{4,6},{5,7},{6,4},{7,5},{8,10},{9,11},{10,... | collective-permute-start | bytes 1572872 | tf_op jit(solution)/shard_map/ppermute | solution.py:27
  3.8 0.8 slice.4
  4.6 3.4 %collective-permute-start = (bf16[3,8,1024]{2,1,0:T(8,128)(2,1)S(1)}, bf16[3,8,1024]{2,1,0:T(8,128)(2,1)S(1)}, u32[]{:S(2)}, u32[]{:S(2)}) collective-permute-start(bf16[3,8,1024]{2,1,0:T(8,128)(2,1)S(1)} %slice.4), channel_id=1, source_target_pairs={{0,4},{4,8},{8,12},{12,16},{16,20},{20,24},{24,28},{1,5},{5,9},{9,... | collective-permute-start | bytes 147464 | tf_op jit(solution)/shard_map/ppermute | solution.py:33
  8.0 2.2 %pack.1 = bf16[8,384,128]{2,1,0:T(8,128)(2,1)} custom-call(bf16[3,128,1024]{2,1,0:T(8,128)(2,1)} %bitcast.10, f32[128,1024]{1,0:T(8,128)} %filter_ref.1), custom_call_target="tpu_custom_call" | custom-call | tf_op jit(solution)/shard_map/pack/pallas_call | solution.py:770
  10.2 4.9 %all-to-all-start = ((bf16[8,384,128]{2,1,0:T(8,128)(2,1)}), bf16[8,384,128]{2,1,0:T(8,128)(2,1)}, u32[]{:S(2)}, u32[]{:S(2)}) async-start(bf16[8,384,128]{2,1,0:T(8,128)(2,1)} %pack.1), calls=%async_computation | async-start | bytes 1572864 | tf_op jit(solution)/shard_map/all_to_all | solution.py:749
  15.1 0.8 fusion.5
  15.9 0.5 collective-permute-done.1.refs_0_
  16.5 1.4 %fusion.12 = (f32[32,1152]{1,0:T(8,128)}, f32[32,1152]{1,0:T(8,128)}) fusion(s32[1152]{0:T(1024)S(1)} %multiply_add_fusion, s32[32]{0:T(128)S(1)} %multiply_add_fusion.1), kind=kLoop, calls=%fused_computation.20 | loop fusion | flops 331776 | bytes 299648 | tf_op jit(solution)/shard_map/cos | solution.py:55
  17.9 0.7 dynamic-slice_bitcast_fusion.taps_ref
  18.6 4.0 %grad_first.1.refs_2_ = f32[128,1024]{1,0:T(8,128)S(1)} custom-call(s32[1]{0:T(128)} %bitcast.place_ref, bf16[8192,1024]{1,0:T(8,128)(2,1)} %w_ref.9, bf16[128,2048]{1,0:T(8,128)(2,1)} %refs_0_.1, bf16[128,2048]{1,0:T(8,128)(2,1)S(1)} %collective-permute-done.3.refs_1_), custom_call_target="tpu_custom_call" | custom-call | tf_op jit(solution)/shard_map/grad_first/pallas_call | solution.py:168
  22.7 4.8 %grad_last.1 = (f32[128,1024]{1,0:T(8,128)}, f32[128,1024]{1,0:T(8,128)}, bf16[8,128,128]{2,1,0:T(8,128)(2,1)}) custom-call(s32[1]{0:T(128)} %bitcast.place_ref, bf16[8192,1024]{1,0:T(8,128)(2,1)} %w_ref.9, bf16[128,2048]{1,0:T(8,128)(2,1)S(1)} %collective-permute-done.1.refs_0_, bf16[128,2048]{1,0:T(8,128)(2,1)S(1)} %collective-permute-done.2.refs_1_, ...), custom_call_target="tpu_custom_call" | custom-call | tf_op jit(solution)/shard_map/grad_last/pallas_call | solution.py:186
  27.5 1.5 %edge_rows.1 = (f32[128,1024]{1,0:T(8,128)}, bf16[8,128,128]{2,1,0:T(8,128)(2,1)}) custom-call(bf16[3,128,1024]{2,1,0:T(8,128)(2,1)S(1)} %bitcast.13, bf16[3,8,1024]{2,1,0:T(8,128)(2,1)S(1)} %collective-permute-done.edge_ref, f32[3,7,1024]{2,1,0:T(8,128)S(1)} %bitcast.16, ...), custom_call_target="tpu_custom_call", output_to_operand_aliasing={{0}: (4, {}), {1}: (5, {})} | custom-call | tf_op jit(solution)/shard_map/edge_rows/pallas_call | solution.py:230
  29.0 6.4 %all-to-all-done.got_ref = bf16[8,384,128]{2,1,0:T(8,128)(2,1)} async-done(((bf16[8,384,128]{2,1,0:T(8,128)(2,1)}), bf16[8,384,128]{2,1,0:T(8,128)(2,1)}, u32[]{:S(2)}, u32[]{:S(2)}) %all-to-all-start) | async-done | bytes 786464 | tf_op jit(solution)/shard_map/all_to_all | solution.py:749
  35.4 3.6 %all-to-all-start.2 = ((bf16[8,128,128]{2,1,0:T(8,128)(2,1)}), bf16[8,128,128]{2,1,0:T(8,128)(2,1)S(1)}, u32[]{:S(2)}, u32[]{:S(2)}) async-start(bf16[8,128,128]{2,1,0:T(8,128)(2,1)} %get-tuple-element.28), calls=%async_computation.2 | async-start | bytes 524288 | tf_op jit(solution)/shard_map/all_to_all | solution.py:749
  39.0 4.0 %add_convert_fusion = (bf16[36,32,1152]{2,1,0:T(8,128)(2,1)}, bf16[36,32,1152]{2,1,0:T(8,128)(2,1)}) fusion(f32[32,1152]{1,0:T(8,128)S(1)} %copy-done.8, f32[36,1152]{1,0:T(8,128)S(1)} %get-tuple-element.44, f32[32,1152]{1,0:T(8,128)S(1)} %copy-done.7, f32[36,1152]{1,0:T(8,128)S(1)} %get-tuple-element.43), kind=kLoop, calls=%fused_computation | loop fusion | flops 10616832 | bytes 5935104 | tf_op jit(solution)/shard_map/convert_element_type | solution.py:57
  43.0 7.1 %forward_spectral.1 = (bf16[8,128,128]{2,1,0:T(8,128)(2,1)}, f32[2,1024,128]{2,1,0:T(8,128)}, f32[6,1152,128]{2,1,0:T(8,128)}) custom-call(bf16[8,384,128]{2,1,0:T(8,128)(2,1)} %all-to-all-done.got_ref, f32[3,7,128]{2,1,0:T(8,128)S(1)} %dynamic-slice_bitcast_fusion.taps_ref, f32[120,128]{1,0:T(8,128)S(1)} %constant_dynamic-slice_fusion.medium_ref, ...), custom_call_target="tpu_custom_call" | custom-call | tf_op jit(solution)/shard_map/forward_spectral/pallas_call | solution.py:531
  50.0 6.0 %all-to-all-start.1 = ((bf16[8,128,128]{2,1,0:T(8,128)(2,1)}), bf16[8,128,128]{2,1,0:T(8,128)(2,1)S(1)}, u32[]{:S(2)}, u32[]{:S(2)}) async-start(bf16[8,128,128]{2,1,0:T(8,128)(2,1)} %get-tuple-element.23), calls=%async_computation.1 | async-start | bytes 524288 | tf_op jit(solution)/shard_map/all_to_all | solution.py:749
  56.1 8.9 %backward_spectral.1._ = bf16[8,480,128]{2,1,0:T(8,128)(2,1)} custom-call(bf16[8,128,128]{2,1,0:T(8,128)(2,1)} %copy-done.6, f32[3,7,128]{2,1,0:T(8,128)S(1)} %dynamic-slice_bitcast_fusion.taps_ref, bf16[8,384,128]{2,1,0:T(8,128)(2,1)} %all-to-all-done.got_ref, f32[2,1024,128]{2,1,0:T(8,128)} %get-tuple-element.29.kept_ref, ...), custom_call_target="tpu_custom_call" | custom-call | tf_op jit(solution)/shard_map/backward_spectral/pallas_call | solution.py:572
  65.0 3.6 %product.1 = (bf16[128,1024]{1,0:T(8,128)(2,1)}, f32[128,1024]{1,0:T(8,128)}, bf16[8,1024]{1,0:T(8,128)(2,1)}, bf16[8,480,128]{2,1,0:T(8,128)(2,1)}) custom-call(bf16[8,128,128]{2,1,0:T(8,128)(2,1)S(1)} %all-to-all-done.1.got_ref, f32[128,1024]{1,0:T(8,128)} %get-tuple-element.27.query_ref, ...), custom_call_target="tpu_custom_call", output_to_operand_aliasing={{3}: (5, {})} | custom-call | tf_op jit(solution)/shard_map/product/pallas_call | solution.py:636
  68.7 0.9 copy-done.2
  69.6 3.3 %project.5 = bf16[128,2048]{1,0:T(8,128)(2,1)S(1)} custom-call(s32[1]{0:T(128)} %bitcast.place_ref, bf16[128,1024]{1,0:T(8,128)(2,1)S(1)} %copy-done.2, bf16[8192,1024]{1,0:T(8,128)(2,1)} %w_ref.9), custom_call_target="tpu_custom_call" | custom-call | tf_op jit(solution)/shard_map/project/pallas_call | solution.py:686
  72.9 6.0 %all-to-all-start.3 = ((bf16[8,480,128]{2,1,0:T(8,128)(2,1)}), bf16[8,480,128]{2,1,0:T(8,128)(2,1)S(1)}, u32[]{:S(2)}, u32[]{:S(2)}) async-start(bf16[8,480,128]{2,1,0:T(8,128)(2,1)} %get-tuple-element.34), calls=%async_computation.3 | async-start | bytes 1966080 | tf_op jit(solution)/shard_map/all_to_all | solution.py:749
  78.9 3.2 %project.4 = f32[128,2048]{1,0:T(8,128)S(1)} custom-call(s32[1]{0:T(128)} %bitcast.place_ref, bf16[128,1024]{1,0:T(8,128)(2,1)S(1)} %copy-done.3, bf16[8192,1024]{1,0:T(8,128)(2,1)} %w_ref.9), custom_call_target="tpu_custom_call" | custom-call | tf_op jit(solution)/shard_map/project/pallas_call | solution.py:686
  82.2 5.2 %project.3 = (bf16[128,2048]{1,0:T(8,128)(2,1)S(1)}, f32[128,2048]{1,0:T(8,128)S(1)}) custom-call(s32[1]{0:T(128)} %bitcast.place_ref, bf16[128,1024]{1,0:T(8,128)(2,1)S(1)} %copy-done.3, bf16[8192,1024]{1,0:T(8,128)(2,1)} %w_ref.9), custom_call_target="tpu_custom_call" | custom-call | tf_op jit(solution)/shard_map/project/pallas_call | solution.py:686
  87.8 0.6 collective-permute-start.6
  88.4 3.1 %local.1.local_ref = f32[2,128,1024]{2,1,0:T(8,128)} custom-call(bf16[3,128,1024]{2,1,0:T(8,128)(2,1)} %bitcast.11, bf16[3,8,1024]{2,1,0:T(8,128)(2,1)S(1)} %collective-permute-done.edge_ref, f32[3,7,1024]{2,1,0:T(8,128)S(1)} %bitcast.17), custom_call_target="tpu_custom_call" | custom-call | tf_op jit(solution)/shard_map/local/pallas_call | solution.py:824
  91.5 1.3 %collective-permute-start.7 = (bf16[8,1024]{1,0:T(8,128)(2,1)S(1)}, bf16[8,1024]{1,0:T(8,128)(2,1)S(1)}, u32[]{:S(2)}, u32[]{:S(2)}) collective-permute-start(bf16[8,1024]{1,0:T(8,128)(2,1)S(1)} %copy-done.9), channel_id=1, source_target_pairs={{4,0},{8,4},{12,8},{16,12},{20,16},{24,20},{28,24},{5,1},{9,5},{13... | collective-permute-start | bytes 49160 | tf_op jit(solution)/shard_map/ppermute | solution.py:33
  92.8 9.2 %collective-permute-done.6 = bf16[128,2048]{1,0:T(8,128)(2,1)S(1)} collective-permute-done((bf16[128,2048]{1,0:T(8,128)(2,1)S(1)}, bf16[128,2048]{1,0:T(8,128)(2,1)S(1)}, u32[]{:S(2)}, u32[]{:S(2)}) %collective-permute-start.6) | collective-permute-done | bytes 524320 | tf_op jit(solution)/shard_map/ppermute | solution.py:27
  102.0 1.0 add_convert_fusion.1
  103.0 1.2 %all-to-all-done.3.got_ref = bf16[8,480,128]{2,1,0:T(8,128)(2,1)S(1)} async-done(((bf16[8,480,128]{2,1,0:T(8,128)(2,1)}), bf16[8,480,128]{2,1,0:T(8,128)(2,1)S(1)}, u32[]{:S(2)}, u32[]{:S(2)}) %all-to-all-start.3) | async-done | bytes 983072 | tf_op jit(solution)/shard_map/all_to_all | solution.py:749
  104.1 4.0 %finish.1 = (bf16[3,128,1024]{2,1,0:T(8,128)(2,1)}, f32[128,1024]{1,0:T(8,128)}, f32[120,1024]{1,0:T(8,128)}, f32[3,7,1024]{2,1,0:T(8,128)}) custom-call(bf16[8,480,128]{2,1,0:T(8,128)(2,1)S(1)} %all-to-all-done.3.got_ref, f32[128,1024]{1,0:T(8,128)S(1)} %copy-done.5, bf16[8,1024]{1,0:T(8,128)(2,1)S(1)} %collective-permute-done.7.next_ref, ...), custom_call_target="tpu_custom_call" | custom-call | tf_op jit(solution)/shard_map/finish/pallas_call | solution.py:833
  (35 shorter events, 0.6 us)
Async XLA Ops:
  0.6 14.4 %copy-start = (f32[120,1024]{1,0:T(8,128)S(1)}, f32[120,1024]{1,0:T(8,128)}, u32[]{:S(2)}) copy-start(f32[120,1024]{1,0:T(8,128)} %param.8) | copy-start | bytes 1474564
  0.6 18.0 %collective-permute-start.3 = (bf16[128,2048]{1,0:T(8,128)(2,1)}, bf16[128,2048]{1,0:T(8,128)(2,1)S(1)}, u32[]{:S(2)}, u32[]{:S(2)}) collective-permute-start(bf16[128,2048]{1,0:T(8,128)(2,1)} %refs_0_.1), channel_id=1, source_target_pairs={{0,1},{1,0},{2,3},{3,2},{4,5},{5,4},{6,7},{7,6},{8,9},{9,8},{10,11... | collective-permute-start | bytes 1572872 | tf_op jit(solution)/shard_map/ppermute | solution.py:27
  1.2 15.3 %collective-permute-start.1 = (bf16[128,2048]{1,0:T(8,128)(2,1)}, bf16[128,2048]{1,0:T(8,128)(2,1)S(1)}, u32[]{:S(2)}, u32[]{:S(2)}) collective-permute-start(bf16[128,2048]{1,0:T(8,128)(2,1)} %refs_0_.1), channel_id=1, source_target_pairs={{0,2},{1,3},{2,0},{3,1},{4,6},{5,7},{6,4},{7,5},{8,10},{9,11},{10,... | collective-permute-start | bytes 1572872 | tf_op jit(solution)/shard_map/ppermute | solution.py:27
  4.6 23.0 %collective-permute-start = (bf16[3,8,1024]{2,1,0:T(8,128)(2,1)S(1)}, bf16[3,8,1024]{2,1,0:T(8,128)(2,1)S(1)}, u32[]{:S(2)}, u32[]{:S(2)}) collective-permute-start(bf16[3,8,1024]{2,1,0:T(8,128)(2,1)S(1)} %slice.4), channel_id=1, source_target_pairs={{0,4},{4,8},{8,12},{12,16},{16,20},{20,24},{24,28},{1,5},{5,9},{9,... | collective-permute-start | bytes 147464 | tf_op jit(solution)/shard_map/ppermute | solution.py:33
  10.2 25.2 %all-to-all-start = ((bf16[8,384,128]{2,1,0:T(8,128)(2,1)}), bf16[8,384,128]{2,1,0:T(8,128)(2,1)}, u32[]{:S(2)}, u32[]{:S(2)}) async-start(bf16[8,384,128]{2,1,0:T(8,128)(2,1)} %pack.1), calls=%async_computation | async-start | bytes 1572864 | tf_op jit(solution)/shard_map/all_to_all | solution.py:749
  16.5 6.2 %collective-permute-start.2 = (bf16[128,2048]{1,0:T(8,128)(2,1)S(1)}, bf16[128,2048]{1,0:T(8,128)(2,1)S(1)}, u32[]{:S(2)}, u32[]{:S(2)}) collective-permute-start(bf16[128,2048]{1,0:T(8,128)(2,1)S(1)} %collective-permute-done.1.refs_0_), channel_id=1, source_target_pairs={{0,1},{1,0},{2,3},{3,2},{4,5},{5,4},{6,7},{7,6},{8,9},{9,8},{10,11... | collective-permute-start | bytes 1572872 | tf_op jit(solution)/shard_map/ppermute | solution.py:27
  18.6 4.1 %copy-start.1 = (bf16[128,3,1024]{2,0,1:T(8,128)(2,1)S(1)}, bf16[128,3,1024]{2,0,1:T(8,128)(2,1)}, u32[]{:S(2)}) copy-start(bf16[128,3,1024]{2,0,1:T(8,128)(2,1)} %param.6) | copy-start | bytes 2359300
  18.6 4.1 %copy-start.4 = (f32[7,3,1024]{2,0,1:T(8,128)S(1)}, f32[7,3,1024]{2,0,1:T(8,128)}, u32[]{:S(2)}) copy-start(f32[7,3,1024]{2,0,1:T(8,128)} %param.7) | copy-start | bytes 258052
  22.7 16.3 %copy-start.7 = (f32[32,1152]{1,0:T(8,128)S(1)}, f32[32,1152]{1,0:T(8,128)}, u32[]{:S(2)}) copy-start(f32[32,1152]{1,0:T(8,128)} %get-tuple-element.45) | copy-start | bytes 442372
  22.7 16.3 %copy-start.8 = (f32[32,1152]{1,0:T(8,128)S(1)}, f32[32,1152]{1,0:T(8,128)}, u32[]{:S(2)}) copy-start(f32[32,1152]{1,0:T(8,128)} %get-tuple-element.46) | copy-start | bytes 442372
  35.4 14.7 %all-to-all-start.2 = ((bf16[8,128,128]{2,1,0:T(8,128)(2,1)}), bf16[8,128,128]{2,1,0:T(8,128)(2,1)S(1)}, u32[]{:S(2)}, u32[]{:S(2)}) async-start(bf16[8,128,128]{2,1,0:T(8,128)(2,1)} %get-tuple-element.28), calls=%async_computation.2 | async-start | bytes 524288 | tf_op jit(solution)/shard_map/all_to_all | solution.py:749
  50.0 6.0 %copy-start.6 = (bf16[8,128,128]{2,1,0:T(8,128)(2,1)}, bf16[8,128,128]{2,1,0:T(8,128)(2,1)S(1)}, u32[]{:S(2)}) copy-start(bf16[8,128,128]{2,1,0:T(8,128)(2,1)S(1)} %all-to-all-done.2.grads_ref) | copy-start | bytes 786436
  50.0 14.9 %all-to-all-start.1 = ((bf16[8,128,128]{2,1,0:T(8,128)(2,1)}), bf16[8,128,128]{2,1,0:T(8,128)(2,1)S(1)}, u32[]{:S(2)}, u32[]{:S(2)}) async-start(bf16[8,128,128]{2,1,0:T(8,128)(2,1)} %get-tuple-element.23), calls=%async_computation.1 | async-start | bytes 524288 | tf_op jit(solution)/shard_map/all_to_all | solution.py:749
  68.6 1.0 copy-start.2
  69.6 9.3 %copy-start.3 = (bf16[128,1024]{1,0:T(8,128)(2,1)S(1)}, bf16[128,1024]{1,0:T(8,128)(2,1)}, u32[]{:S(2)}) copy-start(bf16[128,1024]{1,0:T(8,128)(2,1)} %get-tuple-element.31.product_ref) | copy-start | bytes 786436
  72.9 14.8 %collective-permute-start.5 = (bf16[128,2048]{1,0:T(8,128)(2,1)S(1)}, bf16[128,2048]{1,0:T(8,128)(2,1)S(1)}, u32[]{:S(2)}, u32[]{:S(2)}) collective-permute-start(bf16[128,2048]{1,0:T(8,128)(2,1)S(1)} %project.5), channel_id=1, source_target_pairs={{0,1},{1,0},{2,3},{3,2},{4,5},{5,4},{6,7},{7,6},{8,9},{9,8},{10,11... | collective-permute-start | bytes 1572872 | tf_op jit(solution)/shard_map/ppermute | solution.py:27
  72.9 31.2 %all-to-all-start.3 = ((bf16[8,480,128]{2,1,0:T(8,128)(2,1)}), bf16[8,480,128]{2,1,0:T(8,128)(2,1)S(1)}, u32[]{:S(2)}, u32[]{:S(2)}) async-start(bf16[8,480,128]{2,1,0:T(8,128)(2,1)} %get-tuple-element.34), calls=%async_computation.3 | async-start | bytes 1966080 | tf_op jit(solution)/shard_map/all_to_all | solution.py:749
  82.2 9.3 %copy-start.9 = (bf16[8,1024]{1,0:T(8,128)(2,1)S(1)}, bf16[8,1024]{1,0:T(8,128)(2,1)}, u32[]{:S(2)}) copy-start(bf16[8,1024]{1,0:T(8,128)(2,1)} %get-tuple-element.36) | copy-start | bytes 49156
  87.4 16.8 %copy-start.5 = (f32[128,1024]{1,0:T(8,128)S(1)}, f32[128,1024]{1,0:T(8,128)}, u32[]{:S(2)}) copy-start(f32[128,1024]{1,0:T(8,128)} %get-tuple-element.35.query_grad_ref) | copy-start | bytes 1572868
  87.4 5.4 %collective-permute-start.4 = (bf16[128,2048]{1,0:T(8,128)(2,1)S(1)}, bf16[128,2048]{1,0:T(8,128)(2,1)S(1)}, u32[]{:S(2)}, u32[]{:S(2)}) collective-permute-start(bf16[128,2048]{1,0:T(8,128)(2,1)S(1)} %get-tuple-element.33), channel_id=1, source_target_pairs={{0,1},{1,0},{2,3},{3,2},{4,5},{5,4},{6,7},{7,6},{8,9},{9,8},{10,11... | collective-permute-start | bytes 1572872 | tf_op jit(solution)/shard_map/ppermute | solution.py:27
  87.8 14.2 %collective-permute-start.6 = (bf16[128,2048]{1,0:T(8,128)(2,1)S(1)}, bf16[128,2048]{1,0:T(8,128)(2,1)S(1)}, u32[]{:S(2)}, u32[]{:S(2)}) collective-permute-start(bf16[128,2048]{1,0:T(8,128)(2,1)S(1)} %add_convert_fusion.2), channel_id=1, source_target_pairs={{0,2},{1,3},{2,0},{3,1},{4,6},{5,7},{6,4},{7,5},{8,10},{9,11},{10,... | collective-permute-start | bytes 1572872 | tf_op jit(solution)/shard_map/ppermute | solution.py:27
  91.5 11.5 %collective-permute-start.7 = (bf16[8,1024]{1,0:T(8,128)(2,1)S(1)}, bf16[8,1024]{1,0:T(8,128)(2,1)S(1)}, u32[]{:S(2)}, u32[]{:S(2)}) collective-permute-start(bf16[8,1024]{1,0:T(8,128)(2,1)S(1)} %copy-done.9), channel_id=1, source_target_pairs={{4,0},{8,4},{12,8},{16,12},{20,16},{24,20},{28,24},{5,1},{9,5},{13... | collective-permute-start | bytes 49160 | tf_op jit(solution)/shard_map/ppermute | solution.py:33

commit v5 on v4

--- a/solution.py
+++ b/solution.py
@@ -297,7 +297,7 @@
     ac, hc, as_, hs = (both_c[:, :width], both_c[:, width:], both_s[:, :width], both_s[:, width:])
     xc = ac * mc - as_ * ms
     xs = ac * ms + as_ * mc
-    saved = (ac, as_, mc, ms, hc, hs)
+    saved = (ac, as_, hc, hs)
     return saved, (xc * hc - xs * hs).astype(BF16), (xc * hs + xs * hc).astype(BF16)
 
 
@@ -383,18 +383,23 @@
         forward_end(out_ref, acc, freqs)
 
 
-def backward_begin(grads_ref, delayed, signal):
-    parts, length, _ = grads_ref.shape
+def backward_begin(grads, medium_ref, delayed, signal, medium):
+    parts, length, _ = grads.shape
+    medium[...] = jnp.zeros_like(medium)
+    medium[0 : medium_ref.shape[0], :] = medium_ref[...].astype(BF16)
     delayed[...] = jnp.zeros_like(delayed)
     for s in range(parts):
-        delayed[s * length + 1 : (s + 1) * length + 1, :] = grads_ref[s].astype(F32)
+        delayed[s * length + 1 : (s + 1) * length + 1, :] = grads[s].astype(F32)
     signal[...] = delayed[...].astype(BF16)
 
 
-def backward_spectra(cosine, sine, signal, spectra):
+def backward_spectra(cosine, sine, signal, medium, spectra):
     gc = dot(cosine, signal[...])
     gs = dot(sine, signal[...])
-    ac, as_, mc, ms, hc, hs = spectra
+    ac, as_, hc, hs = spectra
+    kept = medium.shape[0]
+    mc = dot(cosine[:, 0:kept], medium[...])
+    ms = dot(sine[:, 0:kept], medium[...])
     uc = hc * gc + hs * gs
     us = hc * gs - hs * gc
     xc = ac * mc - as_ * ms
@@ -405,25 +410,38 @@
 
 
 def backward_end(
-    streams, taps_ref, kept, out_ref, small_ref, ext, after, acc, tap_acc, freqs, scale, medium_reach
+    streams, taps_ref, kept, out_ref, packed, small_ref, ext, after, acc, tap_acc, sems, freqs, scale, medium_reach
 ):
-    parts, _, width = out_ref.shape
-    extend(streams, ext)
+    parts, rows, width = packed.shape
     length = (ext.shape[1] - HALO) // parts
     tokens = parts * length
     reach = taps_ref.shape[1]
     inverse = 1.0 / freqs
+    first = length + 2 * HALO
+    head = first + length
+    after[:, tokens : tokens + HALO, :] = jnp.zeros((2, HALO, width), F32)
+    for s in range(parts):
+        here = slice(s * length, (s + 1) * length)
+        packed[s, first:head, :] = (acc[here, 0:width] * (inverse * scale)).astype(BF16)
+        gated = acc[here, width : 2 * width] * inverse
+        packed[s, 0:length, :] = gated.astype(BF16)
+        after[0, here, :] = gated * kept[1, here, :]
+        after[1, here, :] = gated * kept[0, here, :]
+    for s in range(parts):
+        end = (s + 1) * length
+        for j in range(2):
+            begin = length + j * HALO
+            packed[s, begin : begin + HALO, :] = after[j, end : end + HALO, :].astype(BF16)
+    writes = [
+        pltpu.make_async_copy(packed.at[:, pl.ds(0, head), :], out_ref.at[:, pl.ds(0, head), :], sems.at[0]),
+        pltpu.make_async_copy(
+            packed.at[:, pl.ds(head, rows - head), :], out_ref.at[:, pl.ds(head, rows - head), :], sems.at[1]
+        ),
+    ]
+    writes[0].start()
+    extend(streams, ext)
     small_ref[...] = jnp.zeros_like(small_ref)
     small_ref[0:medium_reach, :] = tap_acc[0:medium_reach, :] * (inverse * scale)
-    after[:, tokens : tokens + HALO, :] = jnp.zeros((2, HALO, width), F32)
-    first = length + 2 * HALO
-    for s in range(parts):
-        here = slice(s * length, (s + 1) * length)
-        out_ref[s, first : first + length, :] = (acc[here, 0:width] * (inverse * scale)).astype(BF16)
-        gated = acc[here, width : 2 * width] * inverse
-        out_ref[s, 0:length, :] = gated.astype(BF16)
-        after[0, here, :] = gated * kept[1, here, :]
-        after[1, here, :] = gated * kept[0, here, :]
     for j in range(2):
         sums = [jnp.zeros((8, width), F32) for _ in range(reach)]
         for s in range(parts):
@@ -436,22 +454,20 @@
             row = medium_reach + j * reach + i
             small_ref[row : row + 1, :] = jnp.sum(sums[i], 0, keepdims=True) * scale
     small = small_ref[...].astype(BF16)
-    first = 2 * length + 2 * HALO
     for s in range(parts):
-        end = (s + 1) * length
-        for j in range(2):
-            rows = slice(length + j * HALO, length + (j + 1) * HALO)
-            out_ref[s, rows, :] = after[j, end : end + HALO, :].astype(BF16)
-        out_ref[s, first : first + small.shape[0], :] = small
+        packed[s, head:, :] = small
+    writes[1].start()
+    wait_all(writes)
 
 
 def backward_kernel(
-    grads_ref, taps_ref, got_ref, kept_ref, spectra_ref, cos_ref, sin_ref, *refs,
+    taps_ref, medium_ref, grads_ref, got_ref, kept_ref, spectra_ref, cos_ref, sin_ref, *refs,
     freqs, block, scale, medium_reach, resident,
 ):
     if not resident:
         cos_across_ref, sin_across_ref, *refs = refs
-    out_ref, small, delayed, signal, ext, after, acc, tap_acc, streams, kept, late_sems, *refs = refs
+    out_ref, packed, small, delayed, signal, ext, after, acc, tap_acc, streams, kept, grads, medium, *refs = refs
+    late_sems, write_sems, *refs = refs
     step = pl.program_id(0)
     size = signal.shape[0]
     rows, taps_kept = (acc.shape[0], tap_acc.shape[0])
@@ -459,26 +475,30 @@
         pltpu.make_async_copy(kept_ref, kept, late_sems.at[0]),
         pltpu.make_async_copy(got_ref.at[:, pl.ds(0, streams.shape[1]), :], streams, late_sems.at[1]),
     ]
+    early = pltpu.make_async_copy(grads_ref, grads, late_sems.at[2])
 
     def end():
         wait_all(late)
         backward_end(
-            streams, taps_ref, kept, out_ref, small, ext, after, acc, tap_acc, freqs, scale, medium_reach
+            streams, taps_ref, kept, out_ref, packed, small, ext, after, acc, tap_acc, write_sems,
+            freqs, scale, medium_reach,
         )
 
     if resident:
         held, both_c_all, both_s_all, taps_c_all, taps_s_all, spectra_held, sems = refs
         groups = block_copies((cos_ref, sin_ref), held, spectra_ref, spectra_held, sems, freqs // block)
+        early.start()
         for group in groups:
             start_all(group)
         start_all(late)
-        backward_begin(grads_ref, delayed, signal)
+        early.wait()
+        backward_begin(grads, medium_ref, delayed, signal, medium)
         for b, group in enumerate(groups):
             wait_all(group)
             here = slice(b * block, (b + 1) * block)
             spectra = [spectra_held[i, here, :] for i in range(spectra_held.shape[0])]
             both_c_all[here, :], both_s_all[here, :], taps_c_all[here, :], taps_s_all[here, :] = backward_spectra(
-                held[0, here, 0:size], held[1, here, 0:size], signal, spectra
+                held[0, here, 0:size], held[1, here, 0:size], signal, medium, spectra
             )
         acc[...] = dot(held[0, 0:rows, :], both_c_all[...]) + dot(held[1, 0:rows, :], both_s_all[...])
         tap_acc[...] = dot(held[0, 0:taps_kept, :], taps_c_all[...]) + dot(held[1, 0:taps_kept, :], taps_s_all[...])
@@ -487,12 +507,14 @@
 
     @pl.when(step == 0)
     def _():
-        backward_begin(grads_ref, delayed, signal)
+        early.start()
+        early.wait()
+        backward_begin(grads, medium_ref, delayed, signal, medium)
         acc[...] = jnp.zeros_like(acc)
         tap_acc[...] = jnp.zeros_like(tap_acc)
 
     spectra = [spectra_ref[i] for i in range(spectra_ref.shape[0])]
-    both_c, both_s, taps_c, taps_s = backward_spectra(cos_ref[:, 0:size], sin_ref[:, 0:size], signal, spectra)
+    both_c, both_s, taps_c, taps_s = backward_spectra(cos_ref[:, 0:size], sin_ref[:, 0:size], signal, medium, spectra)
     acc[...] += dot(cos_across_ref[0:rows, :], both_c) + dot(sin_across_ref[0:rows, :], both_s)
     tap_acc[...] += dot(cos_across_ref[0:taps_kept, :], taps_c) + dot(sin_across_ref[0:taps_kept, :], taps_s)
 
@@ -516,7 +538,7 @@
     return (
         [pltpu.VMEM((2, freqs, freqs), BF16)]
         + [pltpu.VMEM((freqs, w), BF16) for w in widths]
-        + [pltpu.VMEM((6, freqs, width), F32), pltpu.SemaphoreType.DMA((kinds, blocks))]
+        + [pltpu.VMEM((4, freqs, width), F32), pltpu.SemaphoreType.DMA((kinds, blocks))]
     )
 
 
@@ -535,12 +557,12 @@
         out_specs=[
             whole((parts, length, width)),
             hbm,
-            hbm if resident else pl.BlockSpec((6, per, width), lambda j: (0, j, 0)),
+            hbm if resident else pl.BlockSpec((4, per, width), lambda j: (0, j, 0)),
         ],
         out_shape=[
             pltpu.HBM((parts, length, width), BF16),
             pltpu.HBM((2, tokens, width), F32),
-            pltpu.HBM((6, freqs, width), F32),
+            pltpu.HBM((4, freqs, width), F32),
         ],
         scratch_shapes=[
             pltpu.VMEM((2, tokens + HALO, width), F32),
@@ -560,7 +582,7 @@
     )(in_hbm(got), taps, medium_taps, *operands)
 
 
-def backward_call(got, grads, taps, kept, spectra, tables, freqs, block, scale, medium_reach, rows, small, extra):
+def backward_call(got, grads, taps, medium_taps, kept, spectra, tables, freqs, block, scale, medium_reach, rows, small, extra):
     parts, tall, width = got.shape
     length = tall // 3
     tokens = parts * length
@@ -575,16 +597,18 @@
         ),
         grid=(steps,),
         in_specs=[
-            whole((parts, length, width)),
             whole(taps.shape),
+            whole(medium_taps.shape),
+            pl.BlockSpec(memory_space=pl.ANY),
             hbm,
             hbm,
-            hbm if resident else pl.BlockSpec((6, per, width), lambda j: (0, j, 0)),
+            hbm if resident else pl.BlockSpec((4, per, width), lambda j: (0, j, 0)),
         ]
         + specs,
-        out_specs=whole((parts, rows + small + extra, width)),
+        out_specs=hbm,
         out_shape=pltpu.HBM((parts, rows + small + extra, width), BF16),
         scratch_shapes=[
+            pltpu.VMEM((parts, rows + small, width), BF16),
             pltpu.VMEM((small, width), F32),
             pltpu.VMEM((late, width), F32),
             pltpu.VMEM((late, width), BF16),
@@ -594,37 +618,55 @@
             pltpu.VMEM((padded, width), F32),
             pltpu.VMEM((parts, 2 * length, width), BF16),
             pltpu.VMEM((2, tokens, width), F32),
+            pltpu.VMEM((parts, length, width), BF16),
+            pltpu.VMEM((padded, width), BF16),
+            pltpu.SemaphoreType.DMA((3,)),
             pltpu.SemaphoreType.DMA((2,)),
         ]
         + (held_scratch(freqs, block, width, (2 * width, 2 * width, width, width), 3) if resident else []),
         compiler_params=limit(40 if resident else 60),
         name="backward_spectral",
-    )(in_hbm(grads), taps, in_hbm(got), in_hbm(kept), in_hbm(spectra), *operands)
+    )(taps, medium_taps, grads, in_hbm(got), in_hbm(kept), in_hbm(spectra), *operands)
 
 
 def product_kernel(
     got_ref, query_ref, grad_ref, x_ref, edge_ref, _, product_ref, query_grad_ref, first_ref, back_ref,
-    ext, taps, rounded, sem, *, reach, begin,
+    got, query, grad, x, product, query_grad, first, ext, taps, rounded, sems, *, reach, begin,
 ):
-    parts, length, width = got_ref.shape
+    parts, length, width = got.shape
+    reads = [
+        pltpu.make_async_copy(source, held, sems.at[i])
+        for i, (source, held) in enumerate(((x_ref.at[0], x), (got_ref, got), (grad_ref, grad), (query_ref, query)))
+    ]
+    start_all(reads)
     ext[0:HALO, :] = edge_ref[0].astype(F32)
-    ext[HALO:, :] = x_ref[0].astype(F32)
     taps[...] = jnp.zeros_like(taps)
+    reads[0].wait()
+    ext[HALO:, :] = x[...].astype(F32)
+    wait_all(reads[1:3])
     for j in range(parts):
         lanes = slice(j * width, (j + 1) * width)
-        convolved = got_ref[j].astype(F32)
-        product_ref[:, lanes] = (query_ref[:, lanes] * convolved).astype(BF16)
-        own = grad_ref[:, lanes] * convolved
-        query_grad_ref[:, lanes] = own
-        first_ref[:, lanes] = own[0:HALO].astype(BF16)
+        own = grad[:, lanes] * got[j].astype(F32)
+        query_grad[:, lanes] = own
+        first[:, lanes] = own[0:HALO].astype(BF16)
         for i in range(reach):
             moved = ext[HALO - i : HALO - i + length, lanes]
             taps[j * reach + i : j * reach + i + 1, :] = jnp.sum(moved * own, 0, keepdims=True)
     for s in range(parts):
         rounded[s] = taps[...].astype(BF16)
-    write = pltpu.make_async_copy(rounded, back_ref.at[:, pl.ds(begin, taps.shape[0]), :], sem)
-    write.start()
-    write.wait()
+    writes = [
+        pltpu.make_async_copy(rounded, back_ref.at[:, pl.ds(begin, taps.shape[0]), :], sems.at[4]),
+        pltpu.make_async_copy(query_grad, query_grad_ref, sems.at[5]),
+        pltpu.make_async_copy(first, first_ref, sems.at[6]),
+        pltpu.make_async_copy(product, product_ref, sems.at[7]),
+    ]
+    start_all(writes[0:3])
+    reads[3].wait()
+    for j in range(parts):
+        lanes = slice(j * width, (j + 1) * width)
+        product[:, lanes] = (query[:, lanes] * got[j].astype(F32)).astype(BF16)
+    writes[3].start()
+    wait_all(writes)
 
 
 def product_call(convolved, query, grad, streams, edge, back, reach, begin):
@@ -632,19 +674,11 @@
     channels = parts * width
     extra = back.shape[1] - begin
     hbm = pl.BlockSpec(memory_space=pltpu.HBM)
-    full = whole((length, channels))
     return pl.pallas_call(
         partial(product_kernel, reach=reach, begin=begin),
         grid=(1,),
-        in_specs=[
-            whole((parts, length, width)),
-            full,
-            full,
-            whole((1, length, channels)),
-            whole((1, HALO, channels)),
-            hbm,
-        ],
-        out_specs=[full, full, whole((HALO, channels)), hbm],
+        in_specs=[pl.BlockSpec(memory_space=pl.ANY), hbm, hbm, hbm, whole((1, HALO, channels)), hbm],
+        out_specs=[hbm] * 4,
         out_shape=[
             pltpu.HBM((length, channels), BF16),
             pltpu.HBM((length, channels), F32),
@@ -652,15 +686,22 @@
             pltpu.HBM(back.shape, BF16),
         ],
         scratch_shapes=[
+            pltpu.VMEM((parts, length, width), BF16),
+            pltpu.VMEM((length, channels), F32),
+            pltpu.VMEM((length, channels), F32),
+            pltpu.VMEM((length, channels), BF16),
+            pltpu.VMEM((length, channels), BF16),
+            pltpu.VMEM((length, channels), F32),
+            pltpu.VMEM((HALO, channels), BF16),
             pltpu.VMEM((length + HALO, channels), F32),
             pltpu.VMEM((extra, width), F32),
             pltpu.VMEM((parts, extra, width), BF16),
-            pltpu.SemaphoreType.DMA,
+            pltpu.SemaphoreType.DMA((8,)),
         ],
         input_output_aliases={5: 3},
         compiler_params=limit(16),
         name="product",
-    )(convolved, in_hbm(query), in_hbm(grad), streams, edge, in_hbm(back))
+    )(convolved, in_hbm(query), in_hbm(grad), in_hbm(streams), edge, in_hbm(back))
 
 
 def project_kernel(place_ref, product_ref, w_ref, *refs, flips):
@@ -709,40 +750,98 @@
 
 def finish_kernel(
     got_ref, query_grad_ref, next_ref, taps_ref, local_ref,
-    input_grad_ref, filter_ref, medium_ref, short_ref, ext, sums, *, scale, own_rows,
+    input_grad_ref, filter_ref, medium_ref, short_ref,
+    got, local, ext, input_grad, filtering, medium, sums, sems, *, own_rows, scale,
 ):
-    parts, _, width = got_ref.shape
-    length = filter_ref.shape[0]
+    parts, _, width = got.shape
+    length = filtering.shape[0]
     reach = taps_ref.shape[1]
-    medium_reach = medium_ref.shape[0]
-    ext[0, 0:length, :] = query_grad_ref[...]
-    ext[0, length:, :] = next_ref[...].astype(F32)
-    after = length + 2 * HALO
-    for j in range(parts):
-        lanes = slice(j * width, (j + 1) * width)
-        gated = got_ref[j, 0:length, :].astype(F32)
-        ext[1, 0:length, lanes] = gated * local_ref[1, :, lanes]
-        ext[2, 0:length, lanes] = gated * local_ref[0, :, lanes]
-        ext[1, length:, lanes] = got_ref[j, length : length + HALO, :].astype(F32)
-        ext[2, length:, lanes] = got_ref[j, length + HALO : after, :].astype(F32)
-        filter_ref[:, lanes] = got_ref[j, after : after + length, :].astype(F32)
-        small = got_ref[j, after + length : after + length + own_rows, :].astype(F32)
-        medium_ref[:, lanes] = small[0:medium_reach, :]
-        first = medium_reach + reach
-        short_ref[1, :, lanes] = small[medium_reach:first, :]
-        short_ref[2, :, lanes] = small[first : first + reach, :]
-        for k in range(3):
+    medium_reach = medium.shape[0]
+    reads = [
+        pltpu.make_async_copy(query_grad_ref, ext.at[0, pl.ds(0, length), :], sems.at[0]),
+        pltpu.make_async_copy(got_ref, got, sems.at[1]),
+        pltpu.make_async_copy(local_ref, local, sems.at[2]),
+    ]
+    start_all(reads)
+
+    def convolve(k):
+        for j in range(parts):
+            lanes = slice(j * width, (j + 1) * width)
             total = taps_ref[k, 0:1, lanes] * ext[k, 0:length, lanes]
             for i in range(1, reach):
                 total = total + taps_ref[k, i : i + 1, lanes] * ext[k, i : i + length, lanes]
-            input_grad_ref[k, :, lanes] = total.astype(BF16)
-    first = after + length + own_rows
-    total = got_ref[0, first:, :].astype(F32)
+            input_grad[k, :, lanes] = total.astype(BF16)
+
+    writes = [
+        pltpu.make_async_copy(input_grad.at[k], input_grad_ref.at[k], sems.at[3 + k]) for k in range(3)
+    ]
+    more = [
+        pltpu.make_async_copy(filtering, filter_ref, sems.at[6]),
+        pltpu.make_async_copy(medium, medium_ref, sems.at[7]),
+    ]
+    ext[0, length:, :] = next_ref[...].astype(F32)
+    reads[0].wait()
+    convolve(0)
+    writes[0].start()
+    reads[1].wait()
+    after = length + 2 * HALO
+    first = after + length
+    taps = first + own_rows
+    total = got[0, taps:, :].astype(F32)
     for j in range(1, parts):
-        total = total + got_ref[j, first:, :].astype(F32)
+        total = total + got[j, taps:, :].astype(F32)
     sums[...] = total
     for j in range(parts):
-        short_ref[0, :, j * width : (j + 1) * width] = sums[j * reach : (j + 1) * reach, :] * scale
+        lanes = slice(j * width, (j + 1) * width)
+        filtering[:, lanes] = got[j, after:first, :].astype(F32)
+        small = got[j, first:taps, :].astype(F32)
+        medium[:, lanes] = small[0:medium_reach, :]
+        second = medium_reach + reach
+        short_ref[0, :, lanes] = sums[j * reach : (j + 1) * reach, :] * scale
+        short_ref[1, :, lanes] = small[medium_reach:second, :]
+        short_ref[2, :, lanes] = small[second : second + reach, :]
+    start_all(more)
+    reads[2].wait()
+    for k in range(1, 3):
+        for j in range(parts):
+            lanes = slice(j * width, (j + 1) * width)
+            ext[k, 0:length, lanes] = got[j, 0:length, :].astype(F32) * local[2 - k, :, lanes]
+            begin = length + (k - 1) * HALO
+            ext[k, length:, lanes] = got[j, begin : begin + HALO, :].astype(F32)
+        convolve(k)
+        writes[k].start()
+    wait_all(writes + more)
+
+
+def finish_call(returned, query_grad, next_grad, taps, features, medium_reach, own_rows, scale):
+    parts, _, width = returned.shape
+    groups, reach, channels = taps.shape
+    length = query_grad.shape[0]
+    hbm = pl.BlockSpec(memory_space=pltpu.HBM)
+    return pl.pallas_call(
+        partial(finish_kernel, own_rows=own_rows, scale=scale),
+        grid=(1,),
+        in_specs=[pl.BlockSpec(memory_space=pl.ANY), hbm, whole((HALO, channels)), whole(taps.shape), hbm],
+        out_specs=[hbm, hbm, hbm, whole((groups, reach, channels))],
+        out_shape=[
+            pltpu.HBM((groups, length, channels), BF16),
+            pltpu.HBM((length, channels), F32),
+            pltpu.HBM((medium_reach, channels), F32),
+            jax.ShapeDtypeStruct((groups, reach, channels), F32),
+        ],
+        scratch_shapes=[
+            pltpu.VMEM(returned.shape, BF16),
+            pltpu.VMEM((2, length, channels), F32),
+            pltpu.VMEM((groups, length + HALO, channels), F32),
+            pltpu.VMEM((groups, length, channels), BF16),
+            pltpu.VMEM((length, channels), F32),
+            pltpu.VMEM((medium_reach, channels), F32),
+            pltpu.VMEM((-(-parts * reach // 16) * 16, width), F32),
+            pltpu.SemaphoreType.DMA((8,)),
+        ],
+        compiler_params=limit(16),
+        name="finish",
+    )(returned, in_hbm(query_grad), next_grad, taps, in_hbm(features))
 
 
 def reshard(value):
@@ -750,7 +849,7 @@
 
 
 def local(inputs, short_taps, medium_taps, long_filter, out_weight, out_cotangent):
-    length, groups, channels = inputs.shape
+    length, _, channels = inputs.shape
     reach = short_taps.shape[0]
     medium_reach = medium_taps.shape[0]
     parts = lax.axis_size("seq")
@@ -806,7 +905,7 @@
     small = -(-(medium_reach + 2 * reach) // 16) * 16
     extra = -(-parts * reach // 16) * 16
     back = backward_call(
-        got, grads, own_taps, kept, spectra, tables, freqs, block, scale, medium_reach, rows, small, extra
+        got, grads, own_taps, own_medium, kept, spectra, tables, freqs, block, scale, medium_reach, rows, small, extra
     )
     product, query_grad, first_rows, back = product_call(
         convolved, query, product_grad, streams, edge, back, reach, rows + small
@@ -830,35 +929,9 @@
         compiler_params=limit(8),
         name="local",
     )(in_hbm(streams), edge, taps)
-    input_grad, filter_grad, medium_grad, short_grad = pl.pallas_call(
-        partial(finish_kernel, scale=scale, own_rows=small),
-        grid=(1,),
-        in_specs=[
-            whole((parts, rows + small + extra, width)),
-            whole((length, channels)),
-            whole((HALO, channels)),
-            whole(taps.shape),
-            whole((2, length, channels)),
-        ],
-        out_specs=[
-            whole((groups, length, channels)),
-            whole((length, channels)),
-            whole((medium_reach, channels)),
-            whole((groups, reach, channels)),
-        ],
-        out_shape=[
-            jax.ShapeDtypeStruct((groups, length, channels), BF16),
-            jax.ShapeDtypeStruct((length, channels), F32),
-            jax.ShapeDtypeStruct((medium_reach, channels), F32),
-            jax.ShapeDtypeStruct((groups, reach, channels), F32),
-        ],
-        scratch_shapes=[
-            pltpu.VMEM((groups, length + HALO, channels), F32),
-            pltpu.VMEM((extra, width), F32),
-        ],
-        compiler_params=limit(16),
-        name="finish",
-    )(returned, query_grad, next_grad, taps, in_hbm(local_features))
+    input_grad, filter_grad, medium_grad, short_grad = finish_call(
+        returned, query_grad, next_grad, taps, local_features, medium_reach, small, scale
+    )
 
     output = (own + near_core.astype(F32) + across_sum.astype(F32)).astype(BF16)
     return (

time: 109 us -> 107 us (0.982)
  Pallas kernels: 50.8 us -> 48.8 us
  waiting for transfers between devices: 17.3 us -> 19.1 us
    all_to_all x4, waiting for transfers between devices: 7.54 us -> 9.35 us  [reshard(): return lax.all_to_all(value, 'seq', split_axis=0, concat_axis=0, tiled=True)]
    pallas_call x1, Pallas kernels: 8.92 us -> 7.46 us  [backward_call(): pl.pallas_call(partial(backward_kernel, freqs=freqs, block=block, scale=s...]
  transfers between devices with their start and end apart: 12 -> 12, of which waited for: 4 -> 5; matrix products, arithmetic and copies ran while one was open for 8% -> 8% of each run, Pallas kernels for 37% -> 36%
where the time goes in v5:
time: 107 us; the launch traced here: 106 us
  Pallas kernels  48.8 us (46%)
  starting transfers between devices  28.2 us (26%)
  waiting for transfers between devices  19.1 us (18%)
  other arithmetic  6.6 us (6%)
  local copies, waits for them, and re-layouts  2.52 us (2%)
    all_to_all x4, starting transfers between devices, reshard(): return lax.all_to_all(value, 'seq', split_axis=0, concat_axis=0, tiled=True)  19.4 us
    pallas_call x3, Pallas kernels, project(): pl.pallas_call(partial(project_kernel, flips=flips), in_specs=[pl.BlockSp...  11.7 us
    ppermute x6, waiting for transfers between devices, exchange(): lax.ppermute(value, axis, [(source, source ^ flip) for source in range(co...  9.73 us
    all_to_all x4, waiting for transfers between devices, reshard(): return lax.all_to_all(value, 'seq', split_axis=0, concat_axis=0, tiled=True)  9.35 us
    pallas_call x1, Pallas kernels, backward_call(): pl.pallas_call(partial(backward_kernel, freqs=freqs, block=block, scale=s...  7.46 us
    pallas_call x1, Pallas kernels, forward_call(): pl.pallas_call(partial(forward_kernel, freqs=freqs, block=block, resident...  7.05 us
    pallas_call x1, Pallas kernels, product_grad_last(): pl.pallas_call(partial(product_grad_kernel, flips=flips, last=True), grid...  4.79 us
    ppermute x2, starting transfers between devices, shift(): return lax.ppermute(value, axis, pairs)  4.69 us
  transfers between devices with their start and end apart: 12, of which 5 were waited for; matrix products, arithmetic and copies ran while one was open for 8% of the time, Pallas kernels for 36%

profile of v5, /device:TPU:0, one launch (start us, length us, event | category | flops | bytes accessed | tf_op | source)
XLA Modules:
  0.0 106.2 jit_solution(17656052573665289290)
XLA Ops:
  0.6 0.6 collective-permute-start.3
  1.2 2.6 %collective-permute-start.1 = (bf16[128,2048]{1,0:T(8,128)(2,1)}, bf16[128,2048]{1,0:T(8,128)(2,1)S(1)}, u32[]{:S(2)}, u32[]{:S(2)}) collective-permute-start(bf16[128,2048]{1,0:T(8,128)(2,1)} %refs_0_.1), channel_id=1, source_target_pairs={{0,2},{1,3},{2,0},{3,1},{4,6},{5,7},{6,4},{7,5},{8,10},{9,11},{10,... | collective-permute-start | bytes 1572872 | tf_op jit(solution)/shard_map/ppermute | solution.py:27
  3.8 0.8 slice.4
  4.6 3.4 %collective-permute-start = (bf16[3,8,1024]{2,1,0:T(8,128)(2,1)S(1)}, bf16[3,8,1024]{2,1,0:T(8,128)(2,1)S(1)}, u32[]{:S(2)}, u32[]{:S(2)}) collective-permute-start(bf16[3,8,1024]{2,1,0:T(8,128)(2,1)S(1)} %slice.4), channel_id=1, source_target_pairs={{0,4},{4,8},{8,12},{12,16},{16,20},{20,24},{24,28},{1,5},{5,9},{9,... | collective-permute-start | bytes 147464 | tf_op jit(solution)/shard_map/ppermute | solution.py:33
  8.0 2.2 %pack.1 = bf16[8,384,128]{2,1,0:T(8,128)(2,1)} custom-call(bf16[3,128,1024]{2,1,0:T(8,128)(2,1)} %bitcast.10, f32[128,1024]{1,0:T(8,128)} %filter_ref.1), custom_call_target="tpu_custom_call" | custom-call | tf_op jit(solution)/shard_map/pack/pallas_call | solution.py:869
  10.2 4.9 %all-to-all-start = ((bf16[8,384,128]{2,1,0:T(8,128)(2,1)}), bf16[8,384,128]{2,1,0:T(8,128)(2,1)}, u32[]{:S(2)}, u32[]{:S(2)}) async-start(bf16[8,384,128]{2,1,0:T(8,128)(2,1)} %pack.1), calls=%async_computation | async-start | bytes 1572864 | tf_op jit(solution)/shard_map/all_to_all | solution.py:848
  15.1 0.8 fusion.5
  16.5 0.7 fusion.12
  17.2 0.7 dynamic-slice_bitcast_fusion.taps_ref
  17.9 4.0 %grad_first.1.refs_2_ = f32[128,1024]{1,0:T(8,128)S(1)} custom-call(s32[1]{0:T(128)} %bitcast.place_ref, bf16[8192,1024]{1,0:T(8,128)(2,1)} %w_ref.9, bf16[128,2048]{1,0:T(8,128)(2,1)} %refs_0_.1, bf16[128,2048]{1,0:T(8,128)(2,1)S(1)} %collective-permute-done.3.refs_1_), custom_call_target="tpu_custom_call" | custom-call | tf_op jit(solution)/shard_map/grad_first/pallas_call | solution.py:168
  22.0 4.8 %grad_last.1 = (f32[128,1024]{1,0:T(8,128)}, f32[128,1024]{1,0:T(8,128)}, bf16[8,128,128]{2,1,0:T(8,128)(2,1)}) custom-call(s32[1]{0:T(128)} %bitcast.place_ref, bf16[8192,1024]{1,0:T(8,128)(2,1)} %w_ref.9, bf16[128,2048]{1,0:T(8,128)(2,1)S(1)} %collective-permute-done.1.refs_0_, bf16[128,2048]{1,0:T(8,128)(2,1)S(1)} %collective-permute-done.2.refs_1_, ...), custom_call_target="tpu_custom_call" | custom-call | tf_op jit(solution)/shard_map/grad_last/pallas_call | solution.py:186
  26.8 1.5 %edge_rows.1 = (f32[128,1024]{1,0:T(8,128)}, bf16[8,128,128]{2,1,0:T(8,128)(2,1)}) custom-call(bf16[3,128,1024]{2,1,0:T(8,128)(2,1)S(1)} %bitcast.14, bf16[3,8,1024]{2,1,0:T(8,128)(2,1)S(1)} %collective-permute-done.edge_ref, f32[3,7,1024]{2,1,0:T(8,128)S(1)} %bitcast.16, ...), custom_call_target="tpu_custom_call", output_to_operand_aliasing={{0}: (4, {}), {1}: (5, {})} | custom-call | tf_op jit(solution)/shard_map/edge_rows/pallas_call | solution.py:230
  28.3 7.1 %all-to-all-done.got_ref = bf16[8,384,128]{2,1,0:T(8,128)(2,1)} async-done(((bf16[8,384,128]{2,1,0:T(8,128)(2,1)}), bf16[8,384,128]{2,1,0:T(8,128)(2,1)}, u32[]{:S(2)}, u32[]{:S(2)}) %all-to-all-start) | async-done | bytes 786464 | tf_op jit(solution)/shard_map/all_to_all | solution.py:848
  35.4 3.6 %all-to-all-start.2 = ((bf16[8,128,128]{2,1,0:T(8,128)(2,1)}), bf16[8,128,128]{2,1,0:T(8,128)(2,1)S(1)}, u32[]{:S(2)}, u32[]{:S(2)}) async-start(bf16[8,128,128]{2,1,0:T(8,128)(2,1)} %get-tuple-element.28), calls=%async_computation.2 | async-start | bytes 524288 | tf_op jit(solution)/shard_map/all_to_all | solution.py:848
  38.9 4.0 %add_convert_fusion = (bf16[36,32,1152]{2,1,0:T(8,128)(2,1)}, bf16[36,32,1152]{2,1,0:T(8,128)(2,1)}) fusion(f32[32,1152]{1,0:T(8,128)S(1)} %get-tuple-element.46, f32[36,1152]{1,0:T(8,128)S(1)} %get-tuple-element.44, f32[32,1152]{1,0:T(8,128)S(1)} %get-tuple-element.45, f32[36,1152]{1,0:T(8,128)S(1)} %get-tuple-element.43), kind=kLoop, calls=%fused_computation | loop fusion | flops 10616832 | bytes 5935104 | tf_op jit(solution)/shard_map/convert_element_type | solution.py:57
  42.9 7.0 %forward_spectral.1 = (bf16[8,128,128]{2,1,0:T(8,128)(2,1)}, f32[2,1024,128]{2,1,0:T(8,128)}, f32[4,1152,128]{2,1,0:T(8,128)}) custom-call(bf16[8,384,128]{2,1,0:T(8,128)(2,1)} %all-to-all-done.got_ref, f32[3,7,128]{2,1,0:T(8,128)S(1)} %dynamic-slice_bitcast_fusion.taps_ref, f32[120,128]{1,0:T(8,128)S(1)} %constant_dynamic-slice_fusion.medium_ref, ...), custom_call_target="tpu_custom_call" | custom-call | tf_op jit(solution)/shard_map/forward_spectral/pallas_call | solution.py:553
  50.0 6.0 %all-to-all-start.1 = ((bf16[8,128,128]{2,1,0:T(8,128)(2,1)}), bf16[8,128,128]{2,1,0:T(8,128)(2,1)S(1)}, u32[]{:S(2)}, u32[]{:S(2)}) async-start(bf16[8,128,128]{2,1,0:T(8,128)(2,1)} %get-tuple-element.23), calls=%async_computation.1 | async-start | bytes 524288 | tf_op jit(solution)/shard_map/all_to_all | solution.py:848
  56.0 7.5 %backward_spectral.1._ = bf16[8,480,128]{2,1,0:T(8,128)(2,1)} custom-call(f32[3,7,128]{2,1,0:T(8,128)S(1)} %dynamic-slice_bitcast_fusion.taps_ref, f32[120,128]{1,0:T(8,128)S(1)} %constant_dynamic-slice_fusion.medium_ref, bf16[8,128,128]{2,1,0:T(8,128)(2,1)S(1)} %all-to-all-done.2.grads_ref, bf16[8,384,128]{2,1,0:T(8,128)(2,1)} %all-to-all-done.got_ref, ...), custom_call_target="tpu_custom_call" | custom-call | tf_op jit(solution)/shard_map/backward_spectral/pallas_call | solution.py:594
  63.5 1.1 %all-to-all-done.1.got_ref = bf16[8,128,128]{2,1,0:T(8,128)(2,1)S(1)} async-done(((bf16[8,128,128]{2,1,0:T(8,128)(2,1)}), bf16[8,128,128]{2,1,0:T(8,128)(2,1)S(1)}, u32[]{:S(2)}, u32[]{:S(2)}) %all-to-all-start.1) | async-done | bytes 262176 | tf_op jit(solution)/shard_map/all_to_all | solution.py:848
  64.6 2.9 %product.1 = (bf16[128,1024]{1,0:T(8,128)(2,1)}, f32[128,1024]{1,0:T(8,128)}, bf16[8,1024]{1,0:T(8,128)(2,1)}, bf16[8,480,128]{2,1,0:T(8,128)(2,1)}) custom-call(bf16[8,128,128]{2,1,0:T(8,128)(2,1)S(1)} %all-to-all-done.1.got_ref, f32[128,1024]{1,0:T(8,128)} %get-tuple-element.27.query_ref, ...), custom_call_target="tpu_custom_call", output_to_operand_aliasing={{3}: (5, {})} | custom-call | tf_op jit(solution)/shard_map/product/pallas_call | solution.py:677
  67.5 0.9 copy-done.2
  68.4 3.3 %project.5 = bf16[128,2048]{1,0:T(8,128)(2,1)S(1)} custom-call(s32[1]{0:T(128)} %bitcast.place_ref, bf16[128,1024]{1,0:T(8,128)(2,1)S(1)} %copy-done.2, bf16[8192,1024]{1,0:T(8,128)(2,1)} %w_ref.9), custom_call_target="tpu_custom_call" | custom-call | tf_op jit(solution)/shard_map/project/pallas_call | solution.py:727
  71.8 5.0 %all-to-all-start.3 = ((bf16[8,480,128]{2,1,0:T(8,128)(2,1)}), bf16[8,480,128]{2,1,0:T(8,128)(2,1)S(1)}, u32[]{:S(2)}, u32[]{:S(2)}) async-start(bf16[8,480,128]{2,1,0:T(8,128)(2,1)} %get-tuple-element.34), calls=%async_computation.3 | async-start | bytes 1966080 | tf_op jit(solution)/shard_map/all_to_all | solution.py:848
  76.7 3.2 %project.4 = f32[128,2048]{1,0:T(8,128)S(1)} custom-call(s32[1]{0:T(128)} %bitcast.place_ref, bf16[128,1024]{1,0:T(8,128)(2,1)S(1)} %copy-done.3, bf16[8192,1024]{1,0:T(8,128)(2,1)} %w_ref.9), custom_call_target="tpu_custom_call" | custom-call | tf_op jit(solution)/shard_map/project/pallas_call | solution.py:727
  79.9 5.2 %project.3 = (bf16[128,2048]{1,0:T(8,128)(2,1)S(1)}, f32[128,2048]{1,0:T(8,128)S(1)}) custom-call(s32[1]{0:T(128)} %bitcast.place_ref, bf16[128,1024]{1,0:T(8,128)(2,1)S(1)} %copy-done.3, bf16[8192,1024]{1,0:T(8,128)(2,1)} %w_ref.9), custom_call_target="tpu_custom_call" | custom-call | tf_op jit(solution)/shard_map/project/pallas_call | solution.py:727
  85.5 0.6 collective-permute-start.6
  86.1 3.1 %local.1.local_ref = f32[2,128,1024]{2,1,0:T(8,128)} custom-call(bf16[3,128,1024]{2,1,0:T(8,128)(2,1)} %bitcast.12, bf16[3,8,1024]{2,1,0:T(8,128)(2,1)S(1)} %collective-permute-done.edge_ref, f32[3,7,1024]{2,1,0:T(8,128)S(1)} %bitcast.17), custom_call_target="tpu_custom_call" | custom-call | tf_op jit(solution)/shard_map/local/pallas_call | solution.py:923
  89.2 1.3 %collective-permute-start.7 = (bf16[8,1024]{1,0:T(8,128)(2,1)S(1)}, bf16[8,1024]{1,0:T(8,128)(2,1)S(1)}, u32[]{:S(2)}, u32[]{:S(2)}) collective-permute-start(bf16[8,1024]{1,0:T(8,128)(2,1)S(1)} %copy-done.5), channel_id=1, source_target_pairs={{4,0},{8,4},{12,8},{16,12},{20,16},{24,20},{28,24},{5,1},{9,5},{13... | collective-permute-start | bytes 49160 | tf_op jit(solution)/shard_map/ppermute | solution.py:33
  90.5 9.2 %collective-permute-done.6 = bf16[128,2048]{1,0:T(8,128)(2,1)S(1)} collective-permute-done((bf16[128,2048]{1,0:T(8,128)(2,1)S(1)}, bf16[128,2048]{1,0:T(8,128)(2,1)S(1)}, u32[]{:S(2)}, u32[]{:S(2)}) %collective-permute-start.6) | collective-permute-done | bytes 524320 | tf_op jit(solution)/shard_map/ppermute | solution.py:27
  99.7 1.0 add_convert_fusion.1
  100.7 1.2 %all-to-all-done.3.got_ref = bf16[8,480,128]{2,1,0:T(8,128)(2,1)S(1)} async-done(((bf16[8,480,128]{2,1,0:T(8,128)(2,1)}), bf16[8,480,128]{2,1,0:T(8,128)(2,1)S(1)}, u32[]{:S(2)}, u32[]{:S(2)}) %all-to-all-start.3) | async-done | bytes 983072 | tf_op jit(solution)/shard_map/all_to_all | solution.py:848
  101.9 4.1 %finish.1 = (bf16[3,128,1024]{2,1,0:T(8,128)(2,1)}, f32[128,1024]{1,0:T(8,128)}, f32[120,1024]{1,0:T(8,128)}, f32[3,7,1024]{2,1,0:T(8,128)}) custom-call(bf16[8,480,128]{2,1,0:T(8,128)(2,1)S(1)} %all-to-all-done.3.got_ref, f32[128,1024]{1,0:T(8,128)} %get-tuple-element.35.query_grad_ref, bf16[8,1024]{1,0:T(8,128)(2,1)S(1)} %collective-permute-done.7.next_ref, ...), custom_call_target="tpu_custom_call" | custom-call | tf_op jit(solution)/shard_map/finish/pallas_call | solution.py:821
  (27 shorter events, 1.1 us)
Async XLA Ops:
  0.6 14.4 %copy-start = (f32[120,1024]{1,0:T(8,128)S(1)}, f32[120,1024]{1,0:T(8,128)}, u32[]{:S(2)}) copy-start(f32[120,1024]{1,0:T(8,128)} %param.8) | copy-start | bytes 1474564
  0.6 17.3 %collective-permute-start.3 = (bf16[128,2048]{1,0:T(8,128)(2,1)}, bf16[128,2048]{1,0:T(8,128)(2,1)S(1)}, u32[]{:S(2)}, u32[]{:S(2)}) collective-permute-start(bf16[128,2048]{1,0:T(8,128)(2,1)} %refs_0_.1), channel_id=1, source_target_pairs={{0,1},{1,0},{2,3},{3,2},{4,5},{5,4},{6,7},{7,6},{8,9},{9,8},{10,11... | collective-permute-start | bytes 1572872 | tf_op jit(solution)/shard_map/ppermute | solution.py:27
  1.2 15.3 %collective-permute-start.1 = (bf16[128,2048]{1,0:T(8,128)(2,1)}, bf16[128,2048]{1,0:T(8,128)(2,1)S(1)}, u32[]{:S(2)}, u32[]{:S(2)}) collective-permute-start(bf16[128,2048]{1,0:T(8,128)(2,1)} %refs_0_.1), channel_id=1, source_target_pairs={{0,2},{1,3},{2,0},{3,1},{4,6},{5,7},{6,4},{7,5},{8,10},{9,11},{10,... | collective-permute-start | bytes 1572872 | tf_op jit(solution)/shard_map/ppermute | solution.py:27
  4.6 22.2 %collective-permute-start = (bf16[3,8,1024]{2,1,0:T(8,128)(2,1)S(1)}, bf16[3,8,1024]{2,1,0:T(8,128)(2,1)S(1)}, u32[]{:S(2)}, u32[]{:S(2)}) collective-permute-start(bf16[3,8,1024]{2,1,0:T(8,128)(2,1)S(1)} %slice.4), channel_id=1, source_target_pairs={{0,4},{4,8},{8,12},{12,16},{16,20},{20,24},{24,28},{1,5},{5,9},{9,... | collective-permute-start | bytes 147464 | tf_op jit(solution)/shard_map/ppermute | solution.py:33
  10.2 25.2 %all-to-all-start = ((bf16[8,384,128]{2,1,0:T(8,128)(2,1)}), bf16[8,384,128]{2,1,0:T(8,128)(2,1)}, u32[]{:S(2)}, u32[]{:S(2)}) async-start(bf16[8,384,128]{2,1,0:T(8,128)(2,1)} %pack.1), calls=%async_computation | async-start | bytes 1572864 | tf_op jit(solution)/shard_map/all_to_all | solution.py:848
  16.5 5.5 %collective-permute-start.2 = (bf16[128,2048]{1,0:T(8,128)(2,1)S(1)}, bf16[128,2048]{1,0:T(8,128)(2,1)S(1)}, u32[]{:S(2)}, u32[]{:S(2)}) collective-permute-start(bf16[128,2048]{1,0:T(8,128)(2,1)S(1)} %collective-permute-done.1.refs_0_), channel_id=1, source_target_pairs={{0,1},{1,0},{2,3},{3,2},{4,5},{5,4},{6,7},{7,6},{8,9},{9,8},{10,11... | collective-permute-start | bytes 1572872 | tf_op jit(solution)/shard_map/ppermute | solution.py:27
  17.9 4.1 %copy-start.1 = (bf16[128,3,1024]{2,0,1:T(8,128)(2,1)S(1)}, bf16[128,3,1024]{2,0,1:T(8,128)(2,1)}, u32[]{:S(2)}) copy-start(bf16[128,3,1024]{2,0,1:T(8,128)(2,1)} %param.6) | copy-start | bytes 2359300
  17.9 4.1 %copy-start.4 = (f32[7,3,1024]{2,0,1:T(8,128)S(1)}, f32[7,3,1024]{2,0,1:T(8,128)}, u32[]{:S(2)}) copy-start(f32[7,3,1024]{2,0,1:T(8,128)} %param.7) | copy-start | bytes 258052
  35.4 14.7 %all-to-all-start.2 = ((bf16[8,128,128]{2,1,0:T(8,128)(2,1)}), bf16[8,128,128]{2,1,0:T(8,128)(2,1)S(1)}, u32[]{:S(2)}, u32[]{:S(2)}) async-start(bf16[8,128,128]{2,1,0:T(8,128)(2,1)} %get-tuple-element.28), calls=%async_computation.2 | async-start | bytes 524288 | tf_op jit(solution)/shard_map/all_to_all | solution.py:848
  50.0 14.5 %all-to-all-start.1 = ((bf16[8,128,128]{2,1,0:T(8,128)(2,1)}), bf16[8,128,128]{2,1,0:T(8,128)(2,1)S(1)}, u32[]{:S(2)}, u32[]{:S(2)}) async-start(bf16[8,128,128]{2,1,0:T(8,128)(2,1)} %get-tuple-element.23), calls=%async_computation.1 | async-start | bytes 524288 | tf_op jit(solution)/shard_map/all_to_all | solution.py:848
  67.5 1.0 copy-start.2
  68.4 8.3 %copy-start.3 = (bf16[128,1024]{1,0:T(8,128)(2,1)S(1)}, bf16[128,1024]{1,0:T(8,128)(2,1)}, u32[]{:S(2)}) copy-start(bf16[128,1024]{1,0:T(8,128)(2,1)} %get-tuple-element.31.product_ref) | copy-start | bytes 786436
  71.7 13.7 %collective-permute-start.5 = (bf16[128,2048]{1,0:T(8,128)(2,1)S(1)}, bf16[128,2048]{1,0:T(8,128)(2,1)S(1)}, u32[]{:S(2)}, u32[]{:S(2)}) collective-permute-start(bf16[128,2048]{1,0:T(8,128)(2,1)S(1)} %project.5), channel_id=1, source_target_pairs={{0,1},{1,0},{2,3},{3,2},{4,5},{5,4},{6,7},{7,6},{8,9},{9,8},{10,11... | collective-permute-start | bytes 1572872 | tf_op jit(solution)/shard_map/ppermute | solution.py:27
  71.8 30.1 %all-to-all-start.3 = ((bf16[8,480,128]{2,1,0:T(8,128)(2,1)}), bf16[8,480,128]{2,1,0:T(8,128)(2,1)S(1)}, u32[]{:S(2)}, u32[]{:S(2)}) async-start(bf16[8,480,128]{2,1,0:T(8,128)(2,1)} %get-tuple-element.34), calls=%async_computation.3 | async-start | bytes 1966080 | tf_op jit(solution)/shard_map/all_to_all | solution.py:848
  79.9 9.3 %copy-start.5 = (bf16[8,1024]{1,0:T(8,128)(2,1)S(1)}, bf16[8,1024]{1,0:T(8,128)(2,1)}, u32[]{:S(2)}) copy-start(bf16[8,1024]{1,0:T(8,128)(2,1)} %get-tuple-element.36) | copy-start | bytes 49156
  85.1 5.4 %collective-permute-start.4 = (bf16[128,2048]{1,0:T(8,128)(2,1)S(1)}, bf16[128,2048]{1,0:T(8,128)(2,1)S(1)}, u32[]{:S(2)}, u32[]{:S(2)}) collective-permute-start(bf16[128,2048]{1,0:T(8,128)(2,1)S(1)} %get-tuple-element.33), channel_id=1, source_target_pairs={{0,1},{1,0},{2,3},{3,2},{4,5},{5,4},{6,7},{7,6},{8,9},{9,8},{10,11... | collective-permute-start | bytes 1572872 | tf_op jit(solution)/shard_map/ppermute | solution.py:27
  85.5 14.2 %collective-permute-start.6 = (bf16[128,2048]{1,0:T(8,128)(2,1)S(1)}, bf16[128,2048]{1,0:T(8,128)(2,1)S(1)}, u32[]{:S(2)}, u32[]{:S(2)}) collective-permute-start(bf16[128,2048]{1,0:T(8,128)(2,1)S(1)} %add_convert_fusion.2), channel_id=1, source_target_pairs={{0,2},{1,3},{2,0},{3,1},{4,6},{5,7},{6,4},{7,5},{8,10},{9,11},{10,... | collective-permute-start | bytes 1572872 | tf_op jit(solution)/shard_map/ppermute | solution.py:27
  89.2 11.5 %collective-permute-start.7 = (bf16[8,1024]{1,0:T(8,128)(2,1)S(1)}, bf16[8,1024]{1,0:T(8,128)(2,1)S(1)}, u32[]{:S(2)}, u32[]{:S(2)}) collective-permute-start(bf16[8,1024]{1,0:T(8,128)(2,1)S(1)} %copy-done.5), channel_id=1, source_target_pairs={{4,0},{8,4},{12,8},{16,12},{20,16},{24,20},{28,24},{5,1},{9,5},{13... | collective-permute-start | bytes 49160 | tf_op jit(solution)/shard_map/ppermute | solution.py:33

commit v6 on v5

--- a/solution.py
+++ b/solution.py
@@ -13,7 +13,6 @@
 BF16 = jnp.bfloat16
 HALO = 8
 GROUP = 32
-LANES = 128
 CHUNK = 512
 TABLE_LIMIT = 1 << 22
 
@@ -136,12 +135,15 @@
         copy.start()
     if last:
         length = x_ref.shape[1]
-        ext[0:HALO, :] = jnp.zeros((HALO, ext.shape[1]), F32)
-        ext[HALO:, :] = x_ref[0].astype(F32)
-        query = taps_ref[0, 0:1, :] * ext[HALO : HALO + length, :]
-        for i in range(1, taps_ref.shape[1]):
-            query = query + taps_ref[0, i : i + 1, :] * ext[HALO - i : HALO - i + length, :]
-        query_ref[...] = query
+        parts, _, width = ext.shape
+        for j in range(parts):
+            lanes = slice(j * width, (j + 1) * width)
+            ext[j, 0:HALO, :] = jnp.zeros((HALO, width), F32)
+            ext[j, HALO:, :] = x_ref[0, :, lanes].astype(F32)
+            query = taps_ref[0, 0:1, lanes] * ext[j, HALO : HALO + length, :]
+            for i in range(1, taps_ref.shape[1]):
+                query = query + taps_ref[0, i : i + 1, lanes] * ext[j, HALO - i : HALO - i + length, :]
+            query_ref[:, lanes] = query
     for copy in copies_in:
         copy.wait()
     total = summed([held.at[i] for i in range(len(flips))], copies, buffer, acc_ref[...] if last else None)
@@ -196,7 +198,7 @@
             pltpu.HBM((length, channels), F32),
             pltpu.HBM((parts, length, channels // parts), BF16),
         ],
-        scratch_shapes=chunks + [pltpu.VMEM((length + HALO, channels), F32)] + inputs,
+        scratch_shapes=chunks + [pltpu.VMEM((parts, length + HALO, channels // parts), F32)] + inputs,
         compiler_params=limit(24),
         name="grad_last",
     )(place, weight, *shards, acc, streams, taps)
@@ -639,18 +641,20 @@
         for i, (source, held) in enumerate(((x_ref.at[0], x), (got_ref, got), (grad_ref, grad), (query_ref, query)))
     ]
     start_all(reads)
-    ext[0:HALO, :] = edge_ref[0].astype(F32)
     taps[...] = jnp.zeros_like(taps)
     reads[0].wait()
-    ext[HALO:, :] = x[...].astype(F32)
+    for j in range(parts):
+        lanes = slice(j * width, (j + 1) * width)
+        ext[j, 0:HALO, :] = edge_ref[0, :, lanes].astype(F32)
+        ext[j, HALO:, :] = x[:, lanes].astype(F32)
     wait_all(reads[1:3])
     for j in range(parts):
         lanes = slice(j * width, (j + 1) * width)
         own = grad[:, lanes] * got[j].astype(F32)
-        query_grad[:, lanes] = own
+        query_grad[j] = own
         first[:, lanes] = own[0:HALO].astype(BF16)
         for i in range(reach):
-            moved = ext[HALO - i : HALO - i + length, lanes]
+            moved = ext[j, HALO - i : HALO - i + length, :]
             taps[j * reach + i : j * reach + i + 1, :] = jnp.sum(moved * own, 0, keepdims=True)
     for s in range(parts):
         rounded[s] = taps[...].astype(BF16)
@@ -681,7 +685,7 @@
         out_specs=[hbm] * 4,
         out_shape=[
             pltpu.HBM((length, channels), BF16),
-            pltpu.HBM((length, channels), F32),
+            pltpu.HBM((parts, length, width), F32),
             pltpu.HBM((HALO, channels), BF16),
             pltpu.HBM(back.shape, BF16),
         ],
@@ -691,9 +695,9 @@
             pltpu.VMEM((length, channels), F32),
             pltpu.VMEM((length, channels), BF16),
             pltpu.VMEM((length, channels), BF16),
-            pltpu.VMEM((length, channels), F32),
+            pltpu.VMEM((parts, length, width), F32),
             pltpu.VMEM((HALO, channels), BF16),
-            pltpu.VMEM((length + HALO, channels), F32),
+            pltpu.VMEM((parts, length + HALO, width), F32),
             pltpu.VMEM((extra, width), F32),
             pltpu.VMEM((parts, extra, width), BF16),
             pltpu.SemaphoreType.DMA((8,)),
@@ -736,16 +740,16 @@
 
 
 def local_kernel(x_ref, edge_ref, taps_ref, out_ref, ext):
-    _, length, channels = out_ref.shape
+    _, parts, length, width = out_ref.shape
     for j in range(2):
-        ext[0:HALO, :] = edge_ref[j + 1].astype(F32)
-        ext[HALO:, :] = x_ref[j + 1].astype(F32)
-        for begin in range(0, channels, LANES):
-            lanes = slice(begin, min(begin + LANES, channels))
-            total = taps_ref[j + 1, 0:1, lanes] * ext[HALO : HALO + length, lanes]
+        for p in range(parts):
+            lanes = slice(p * width, (p + 1) * width)
+            ext[p, 0:HALO, :] = edge_ref[j + 1, :, lanes].astype(F32)
+            ext[p, HALO:, :] = x_ref[j + 1, :, lanes].astype(F32)
+            total = taps_ref[j + 1, 0:1, lanes] * ext[p, HALO : HALO + length, :]
             for i in range(1, taps_ref.shape[1]):
-                total = total + taps_ref[j + 1, i : i + 1, lanes] * ext[HALO - i : HALO - i + length, lanes]
-            out_ref[j, :, lanes] = total
+                total = total + taps_ref[j + 1, i : i + 1, lanes] * ext[p, HALO - i : HALO - i + length, :]
+            out_ref[j, p] = total
 
 
 def finish_kernel(
@@ -758,7 +762,7 @@
     reach = taps_ref.shape[1]
     medium_reach = medium.shape[0]
     reads = [
-        pltpu.make_async_copy(query_grad_ref, ext.at[0, pl.ds(0, length), :], sems.at[0]),
+        pltpu.make_async_copy(query_grad_ref, ext.at[0, :, pl.ds(0, length), :], sems.at[0]),
         pltpu.make_async_copy(got_ref, got, sems.at[1]),
         pltpu.make_async_copy(local_ref, local, sems.at[2]),
     ]
@@ -767,9 +771,9 @@
     def convolve(k):
         for j in range(parts):
             lanes = slice(j * width, (j + 1) * width)
-            total = taps_ref[k, 0:1, lanes] * ext[k, 0:length, lanes]
+            total = taps_ref[k, 0:1, lanes] * ext[k, j, 0:length, :]
             for i in range(1, reach):
-                total = total + taps_ref[k, i : i + 1, lanes] * ext[k, i : i + length, lanes]
+                total = total + taps_ref[k, i : i + 1, lanes] * ext[k, j, i : i + length, :]
             input_grad[k, :, lanes] = total.astype(BF16)
 
     writes = [
@@ -779,7 +783,8 @@
         pltpu.make_async_copy(filtering, filter_ref, sems.at[6]),
         pltpu.make_async_copy(medium, medium_ref, sems.at[7]),
     ]
-    ext[0, length:, :] = next_ref[...].astype(F32)
+    for j in range(parts):
+        ext[0, j, length:, :] = next_ref[:, j * width : (j + 1) * width].astype(F32)
     reads[0].wait()
     convolve(0)
     writes[0].start()
@@ -804,10 +809,9 @@
     reads[2].wait()
     for k in range(1, 3):
         for j in range(parts):
-            lanes = slice(j * width, (j + 1) * width)
-            ext[k, 0:length, lanes] = got[j, 0:length, :].astype(F32) * local[2 - k, :, lanes]
+            ext[k, j, 0:length, :] = got[j, 0:length, :].astype(F32) * local[2 - k, j]
             begin = length + (k - 1) * HALO
-            ext[k, length:, lanes] = got[j, begin : begin + HALO, :].astype(F32)
+            ext[k, j, length:, :] = got[j, begin : begin + HALO, :].astype(F32)
         convolve(k)
         writes[k].start()
     wait_all(writes + more)
@@ -816,7 +820,7 @@
 def finish_call(returned, query_grad, next_grad, taps, features, medium_reach, own_rows, scale):
     parts, _, width = returned.shape
     groups, reach, channels = taps.shape
-    length = query_grad.shape[0]
+    length = query_grad.shape[1]
     hbm = pl.BlockSpec(memory_space=pltpu.HBM)
     return pl.pallas_call(
         partial(finish_kernel, own_rows=own_rows, scale=scale),
@@ -831,15 +835,15 @@
         ],
         scratch_shapes=[
             pltpu.VMEM(returned.shape, BF16),
-            pltpu.VMEM((2, length, channels), F32),
-            pltpu.VMEM((groups, length + HALO, channels), F32),
+            pltpu.VMEM((2, parts, length, width), F32),
+            pltpu.VMEM((groups, parts, length + HALO, width), F32),
             pltpu.VMEM((groups, length, channels), BF16),
             pltpu.VMEM((length, channels), F32),
             pltpu.VMEM((medium_reach, channels), F32),
-            pltpu.VMEM((-(-parts * reach // 16) * 16, width), F32),
+            pltpu.VMEM((-(-parts * reach // 8) * 8, width), F32),
             pltpu.SemaphoreType.DMA((8,)),
         ],
-        compiler_params=limit(16),
+        compiler_params=limit(24),
         name="finish",
     )(returned, in_hbm(query_grad), next_grad, taps, in_hbm(features))
 
@@ -902,8 +906,8 @@
     convolved = reshard(convolved)
 
     rows = 2 * length + 2 * HALO
-    small = -(-(medium_reach + 2 * reach) // 16) * 16
-    extra = -(-parts * reach // 16) * 16
+    small = -(-(medium_reach + 2 * reach) // 8) * 8
+    extra = -(-parts * reach // 8) * 8
     back = backward_call(
         got, grads, own_taps, own_medium, kept, spectra, tables, freqs, block, scale, medium_reach, rows, small, extra
     )
@@ -924,8 +928,8 @@
         local_kernel,
         in_specs=[vmem] * 3,
         out_specs=vmem,
-        out_shape=pltpu.HBM((2, length, channels), F32),
-        scratch_shapes=[pltpu.VMEM((length + HALO, channels), F32)],
+        out_shape=pltpu.HBM((2, parts, length, width), F32),
+        scratch_shapes=[pltpu.VMEM((parts, length + HALO, width), F32)],
         compiler_params=limit(8),
         name="local",
     )(in_hbm(streams), edge, taps)

time: 107 us -> 105 us (0.981)
  Pallas kernels: 48.8 us -> 47.3 us
where the time goes in v6:
time: 105 us; the launch traced here: 104 us
  Pallas kernels  47.3 us (45%)
  starting transfers between devices  28.2 us (27%)
  waiting for transfers between devices  18.8 us (18%)
  other arithmetic  6.6 us (6%)
  local copies, waits for them, and re-layouts  2.52 us (2%)
    all_to_all x4, starting transfers between devices, reshard(): return lax.all_to_all(value, 'seq', split_axis=0, concat_axis=0, tiled=True)  19.4 us
    pallas_call x3, Pallas kernels, project(): pl.pallas_call(partial(project_kernel, flips=flips), in_specs=[pl.BlockSp...  11.6 us
    ppermute x6, waiting for transfers between devices, exchange(): lax.ppermute(value, axis, [(source, source ^ flip) for source in range(co...  10.2 us
    all_to_all x4, waiting for transfers between devices, reshard(): return lax.all_to_all(value, 'seq', split_axis=0, concat_axis=0, tiled=True)  8.66 us
    pallas_call x1, Pallas kernels, backward_call(): pl.pallas_call(partial(backward_kernel, freqs=freqs, block=block, scale=s...  7.45 us
    pallas_call x1, Pallas kernels, forward_call(): pl.pallas_call(partial(forward_kernel, freqs=freqs, block=block, resident...  7.05 us
    pallas_call x1, Pallas kernels, product_grad_last(): pl.pallas_call(partial(product_grad_kernel, flips=flips, last=True), grid...  4.79 us
    ppermute x2, starting transfers between devices, shift(): return lax.ppermute(value, axis, pairs)  4.69 us
  transfers between devices with their start and end apart: 12, of which 5 were waited for; matrix products, arithmetic and copies ran while one was open for 8% of the time, Pallas kernels for 36%

profile of v6, /device:TPU:0, one launch (start us, length us, event | category | flops | bytes accessed | tf_op | source)
XLA Modules:
  0.0 104.5 jit_solution(13439396603914414403)
XLA Ops:
  0.6 0.6 collective-permute-start.3
  1.2 2.6 %collective-permute-start.1 = (bf16[128,2048]{1,0:T(8,128)(2,1)}, bf16[128,2048]{1,0:T(8,128)(2,1)S(1)}, u32[]{:S(2)}, u32[]{:S(2)}) collective-permute-start(bf16[128,2048]{1,0:T(8,128)(2,1)} %refs_0_.1), channel_id=1, source_target_pairs={{0,2},{1,3},{2,0},{3,1},{4,6},{5,7},{6,4},{7,5},{8,10},{9,11},{10,... | collective-permute-start | bytes 1572872 | tf_op jit(solution)/shard_map/ppermute | solution.py:26
  3.8 0.8 slice.4
  4.6 3.4 %collective-permute-start = (bf16[3,8,1024]{2,1,0:T(8,128)(2,1)S(1)}, bf16[3,8,1024]{2,1,0:T(8,128)(2,1)S(1)}, u32[]{:S(2)}, u32[]{:S(2)}) collective-permute-start(bf16[3,8,1024]{2,1,0:T(8,128)(2,1)S(1)} %slice.4), channel_id=1, source_target_pairs={{0,4},{4,8},{8,12},{12,16},{16,20},{20,24},{24,28},{1,5},{5,9},{9,... | collective-permute-start | bytes 147464 | tf_op jit(solution)/shard_map/ppermute | solution.py:32
  8.0 2.2 %pack.1 = bf16[8,384,128]{2,1,0:T(8,128)(2,1)} custom-call(bf16[3,128,1024]{2,1,0:T(8,128)(2,1)} %bitcast.10, f32[128,1024]{1,0:T(8,128)} %filter_ref.1), custom_call_target="tpu_custom_call" | custom-call | tf_op jit(solution)/shard_map/pack/pallas_call | solution.py:873
  10.2 4.9 %all-to-all-start = ((bf16[8,384,128]{2,1,0:T(8,128)(2,1)}), bf16[8,384,128]{2,1,0:T(8,128)(2,1)}, u32[]{:S(2)}, u32[]{:S(2)}) async-start(bf16[8,384,128]{2,1,0:T(8,128)(2,1)} %pack.1), calls=%async_computation | async-start | bytes 1572864 | tf_op jit(solution)/shard_map/all_to_all | solution.py:852
  15.1 0.8 fusion.5
  15.9 0.5 collective-permute-done.1.refs_0_
  16.5 0.7 fusion.12
  17.2 0.7 dynamic-slice_bitcast_fusion.taps_ref
  17.9 4.0 %grad_first.1.refs_2_ = f32[128,1024]{1,0:T(8,128)S(1)} custom-call(s32[1]{0:T(128)} %bitcast.place_ref, bf16[8192,1024]{1,0:T(8,128)(2,1)} %w_ref.9, bf16[128,2048]{1,0:T(8,128)(2,1)} %refs_0_.1, bf16[128,2048]{1,0:T(8,128)(2,1)S(1)} %collective-permute-done.3.refs_1_), custom_call_target="tpu_custom_call" | custom-call | tf_op jit(solution)/shard_map/grad_first/pallas_call | solution.py:170
  22.0 4.8 %grad_last.1 = (f32[128,1024]{1,0:T(8,128)}, f32[128,1024]{1,0:T(8,128)}, bf16[8,128,128]{2,1,0:T(8,128)(2,1)}) custom-call(s32[1]{0:T(128)} %bitcast.place_ref, bf16[8192,1024]{1,0:T(8,128)(2,1)} %w_ref.9, bf16[128,2048]{1,0:T(8,128)(2,1)S(1)} %collective-permute-done.1.refs_0_, bf16[128,2048]{1,0:T(8,128)(2,1)S(1)} %collective-permute-done.2.refs_1_, ...), custom_call_target="tpu_custom_call" | custom-call | tf_op jit(solution)/shard_map/grad_last/pallas_call | solution.py:188
  26.8 1.5 %edge_rows.1 = (f32[128,1024]{1,0:T(8,128)}, bf16[8,128,128]{2,1,0:T(8,128)(2,1)}) custom-call(bf16[3,128,1024]{2,1,0:T(8,128)(2,1)S(1)} %bitcast.14, bf16[3,8,1024]{2,1,0:T(8,128)(2,1)S(1)} %collective-permute-done.edge_ref, f32[3,7,1024]{2,1,0:T(8,128)S(1)} %bitcast.16, ...), custom_call_target="tpu_custom_call", output_to_operand_aliasing={{0}: (4, {}), {1}: (5, {})} | custom-call | tf_op jit(solution)/shard_map/edge_rows/pallas_call | solution.py:232
  28.3 7.1 %all-to-all-done.got_ref = bf16[8,384,128]{2,1,0:T(8,128)(2,1)} async-done(((bf16[8,384,128]{2,1,0:T(8,128)(2,1)}), bf16[8,384,128]{2,1,0:T(8,128)(2,1)}, u32[]{:S(2)}, u32[]{:S(2)}) %all-to-all-start) | async-done | bytes 786464 | tf_op jit(solution)/shard_map/all_to_all | solution.py:852
  35.4 3.6 %all-to-all-start.2 = ((bf16[8,128,128]{2,1,0:T(8,128)(2,1)}), bf16[8,128,128]{2,1,0:T(8,128)(2,1)S(1)}, u32[]{:S(2)}, u32[]{:S(2)}) async-start(bf16[8,128,128]{2,1,0:T(8,128)(2,1)} %get-tuple-element.28), calls=%async_computation.2 | async-start | bytes 524288 | tf_op jit(solution)/shard_map/all_to_all | solution.py:852
  38.9 4.0 %add_convert_fusion = (bf16[36,32,1152]{2,1,0:T(8,128)(2,1)}, bf16[36,32,1152]{2,1,0:T(8,128)(2,1)}) fusion(f32[32,1152]{1,0:T(8,128)S(1)} %get-tuple-element.46, f32[36,1152]{1,0:T(8,128)S(1)} %get-tuple-element.44, f32[32,1152]{1,0:T(8,128)S(1)} %get-tuple-element.45, f32[36,1152]{1,0:T(8,128)S(1)} %get-tuple-element.43), kind=kLoop, calls=%fused_computation | loop fusion | flops 10616832 | bytes 5935104 | tf_op jit(solution)/shard_map/convert_element_type | solution.py:56
  42.9 7.0 %forward_spectral.1 = (bf16[8,128,128]{2,1,0:T(8,128)(2,1)}, f32[2,1024,128]{2,1,0:T(8,128)}, f32[4,1152,128]{2,1,0:T(8,128)}) custom-call(bf16[8,384,128]{2,1,0:T(8,128)(2,1)} %all-to-all-done.got_ref, f32[3,7,128]{2,1,0:T(8,128)S(1)} %dynamic-slice_bitcast_fusion.taps_ref, f32[120,128]{1,0:T(8,128)S(1)} %constant_dynamic-slice_fusion.medium_ref, ...), custom_call_target="tpu_custom_call" | custom-call | tf_op jit(solution)/shard_map/forward_spectral/pallas_call | solution.py:555
  50.0 6.0 %all-to-all-start.1 = ((bf16[8,128,128]{2,1,0:T(8,128)(2,1)}), bf16[8,128,128]{2,1,0:T(8,128)(2,1)S(1)}, u32[]{:S(2)}, u32[]{:S(2)}) async-start(bf16[8,128,128]{2,1,0:T(8,128)(2,1)} %get-tuple-element.23), calls=%async_computation.1 | async-start | bytes 524288 | tf_op jit(solution)/shard_map/all_to_all | solution.py:852
  56.0 7.4 %backward_spectral.1._ = bf16[8,464,128]{2,1,0:T(8,128)(2,1)} custom-call(f32[3,7,128]{2,1,0:T(8,128)S(1)} %dynamic-slice_bitcast_fusion.taps_ref, f32[120,128]{1,0:T(8,128)S(1)} %constant_dynamic-slice_fusion.medium_ref, bf16[8,128,128]{2,1,0:T(8,128)(2,1)S(1)} %all-to-all-done.2.grads_ref, bf16[8,384,128]{2,1,0:T(8,128)(2,1)} %all-to-all-done.got_ref, ...), custom_call_target="tpu_custom_call" | custom-call | tf_op jit(solution)/shard_map/backward_spectral/pallas_call | solution.py:596
  63.5 1.1 %all-to-all-done.1.got_ref = bf16[8,128,128]{2,1,0:T(8,128)(2,1)S(1)} async-done(((bf16[8,128,128]{2,1,0:T(8,128)(2,1)}), bf16[8,128,128]{2,1,0:T(8,128)(2,1)S(1)}, u32[]{:S(2)}, u32[]{:S(2)}) %all-to-all-start.1) | async-done | bytes 262176 | tf_op jit(solution)/shard_map/all_to_all | solution.py:852
  64.6 2.5 %product.1 = (bf16[128,1024]{1,0:T(8,128)(2,1)}, f32[8,128,128]{2,1,0:T(8,128)}, bf16[8,1024]{1,0:T(8,128)(2,1)}, bf16[8,464,128]{2,1,0:T(8,128)(2,1)}) custom-call(bf16[8,128,128]{2,1,0:T(8,128)(2,1)S(1)} %all-to-all-done.1.got_ref, f32[128,1024]{1,0:T(8,128)} %get-tuple-element.27.query_ref, ...), custom_call_target="tpu_custom_call", output_to_operand_aliasing={{3}: (5, {})} | custom-call | tf_op jit(solution)/shard_map/product/pallas_call | solution.py:681
  67.0 0.9 copy-done.2
  68.0 3.3 %project.5 = bf16[128,2048]{1,0:T(8,128)(2,1)S(1)} custom-call(s32[1]{0:T(128)} %bitcast.place_ref, bf16[128,1024]{1,0:T(8,128)(2,1)S(1)} %copy-done.2, bf16[8192,1024]{1,0:T(8,128)(2,1)} %w_ref.9), custom_call_target="tpu_custom_call" | custom-call | tf_op jit(solution)/shard_map/project/pallas_call | solution.py:731
  71.3 4.9 %all-to-all-start.3 = ((bf16[8,464,128]{2,1,0:T(8,128)(2,1)}), bf16[8,464,128]{2,1,0:T(8,128)(2,1)S(1)}, u32[]{:S(2)}, u32[]{:S(2)}) async-start(bf16[8,464,128]{2,1,0:T(8,128)(2,1)} %get-tuple-element.34), calls=%async_computation.3 | async-start | bytes 1900544 | tf_op jit(solution)/shard_map/all_to_all | solution.py:852
  76.3 3.2 %project.4 = f32[128,2048]{1,0:T(8,128)S(1)} custom-call(s32[1]{0:T(128)} %bitcast.place_ref, bf16[128,1024]{1,0:T(8,128)(2,1)S(1)} %copy-done.3, bf16[8192,1024]{1,0:T(8,128)(2,1)} %w_ref.9), custom_call_target="tpu_custom_call" | custom-call | tf_op jit(solution)/shard_map/project/pallas_call | solution.py:731
  79.5 5.2 %project.3 = (bf16[128,2048]{1,0:T(8,128)(2,1)S(1)}, f32[128,2048]{1,0:T(8,128)S(1)}) custom-call(s32[1]{0:T(128)} %bitcast.place_ref, bf16[128,1024]{1,0:T(8,128)(2,1)S(1)} %copy-done.3, bf16[8192,1024]{1,0:T(8,128)(2,1)} %w_ref.9), custom_call_target="tpu_custom_call" | custom-call | tf_op jit(solution)/shard_map/project/pallas_call | solution.py:731
  85.1 0.6 collective-permute-start.6
  85.7 2.7 %local.1.local_ref = f32[2,8,128,128]{3,2,1,0:T(8,128)} custom-call(bf16[3,128,1024]{2,1,0:T(8,128)(2,1)} %bitcast.12, bf16[3,8,1024]{2,1,0:T(8,128)(2,1)S(1)} %collective-permute-done.edge_ref, f32[3,7,1024]{2,1,0:T(8,128)S(1)} %bitcast.17), custom_call_target="tpu_custom_call" | custom-call | tf_op jit(solution)/shard_map/local/pallas_call | solution.py:927
  88.4 1.3 %collective-permute-start.7 = (bf16[8,1024]{1,0:T(8,128)(2,1)S(1)}, bf16[8,1024]{1,0:T(8,128)(2,1)S(1)}, u32[]{:S(2)}, u32[]{:S(2)}) collective-permute-start(bf16[8,1024]{1,0:T(8,128)(2,1)S(1)} %copy-done.5), channel_id=1, source_target_pairs={{4,0},{8,4},{12,8},{16,12},{20,16},{24,20},{28,24},{5,1},{9,5},{13... | collective-permute-start | bytes 49160 | tf_op jit(solution)/shard_map/ppermute | solution.py:32
  89.7 9.6 %collective-permute-done.6 = bf16[128,2048]{1,0:T(8,128)(2,1)S(1)} collective-permute-done((bf16[128,2048]{1,0:T(8,128)(2,1)S(1)}, bf16[128,2048]{1,0:T(8,128)(2,1)S(1)}, u32[]{:S(2)}, u32[]{:S(2)}) %collective-permute-start.6) | collective-permute-done | bytes 524320 | tf_op jit(solution)/shard_map/ppermute | solution.py:26
  99.3 1.0 add_convert_fusion.1
  100.8 3.6 %finish.1 = (bf16[3,128,1024]{2,1,0:T(8,128)(2,1)}, f32[128,1024]{1,0:T(8,128)}, f32[120,1024]{1,0:T(8,128)}, f32[3,7,1024]{2,1,0:T(8,128)}) custom-call(bf16[8,464,128]{2,1,0:T(8,128)(2,1)S(1)} %all-to-all-done.3.got_ref, f32[8,128,128]{2,1,0:T(8,128)} %get-tuple-element.35.query_grad_ref, bf16[8,1024]{1,0:T(8,128)(2,1)S(1)} %collective-permute-done.7.next_ref, ...), custom_call_target="tpu_custom_call" | custom-call | tf_op jit(solution)/shard_map/finish/pallas_call | solution.py:825
  (27 shorter events, 1.0 us)
Async XLA Ops:
  0.6 14.4 %copy-start = (f32[120,1024]{1,0:T(8,128)S(1)}, f32[120,1024]{1,0:T(8,128)}, u32[]{:S(2)}) copy-start(f32[120,1024]{1,0:T(8,128)} %param.8) | copy-start | bytes 1474564
  0.6 17.3 %collective-permute-start.3 = (bf16[128,2048]{1,0:T(8,128)(2,1)}, bf16[128,2048]{1,0:T(8,128)(2,1)S(1)}, u32[]{:S(2)}, u32[]{:S(2)}) collective-permute-start(bf16[128,2048]{1,0:T(8,128)(2,1)} %refs_0_.1), channel_id=1, source_target_pairs={{0,1},{1,0},{2,3},{3,2},{4,5},{5,4},{6,7},{7,6},{8,9},{9,8},{10,11... | collective-permute-start | bytes 1572872 | tf_op jit(solution)/shard_map/ppermute | solution.py:26
  1.2 15.3 %collective-permute-start.1 = (bf16[128,2048]{1,0:T(8,128)(2,1)}, bf16[128,2048]{1,0:T(8,128)(2,1)S(1)}, u32[]{:S(2)}, u32[]{:S(2)}) collective-permute-start(bf16[128,2048]{1,0:T(8,128)(2,1)} %refs_0_.1), channel_id=1, source_target_pairs={{0,2},{1,3},{2,0},{3,1},{4,6},{5,7},{6,4},{7,5},{8,10},{9,11},{10,... | collective-permute-start | bytes 1572872 | tf_op jit(solution)/shard_map/ppermute | solution.py:26
  4.6 22.2 %collective-permute-start = (bf16[3,8,1024]{2,1,0:T(8,128)(2,1)S(1)}, bf16[3,8,1024]{2,1,0:T(8,128)(2,1)S(1)}, u32[]{:S(2)}, u32[]{:S(2)}) collective-permute-start(bf16[3,8,1024]{2,1,0:T(8,128)(2,1)S(1)} %slice.4), channel_id=1, source_target_pairs={{0,4},{4,8},{8,12},{12,16},{16,20},{20,24},{24,28},{1,5},{5,9},{9,... | collective-permute-start | bytes 147464 | tf_op jit(solution)/shard_map/ppermute | solution.py:32
  10.2 25.2 %all-to-all-start = ((bf16[8,384,128]{2,1,0:T(8,128)(2,1)}), bf16[8,384,128]{2,1,0:T(8,128)(2,1)}, u32[]{:S(2)}, u32[]{:S(2)}) async-start(bf16[8,384,128]{2,1,0:T(8,128)(2,1)} %pack.1), calls=%async_computation | async-start | bytes 1572864 | tf_op jit(solution)/shard_map/all_to_all | solution.py:852
  16.5 5.5 %collective-permute-start.2 = (bf16[128,2048]{1,0:T(8,128)(2,1)S(1)}, bf16[128,2048]{1,0:T(8,128)(2,1)S(1)}, u32[]{:S(2)}, u32[]{:S(2)}) collective-permute-start(bf16[128,2048]{1,0:T(8,128)(2,1)S(1)} %collective-permute-done.1.refs_0_), channel_id=1, source_target_pairs={{0,1},{1,0},{2,3},{3,2},{4,5},{5,4},{6,7},{7,6},{8,9},{9,8},{10,11... | collective-permute-start | bytes 1572872 | tf_op jit(solution)/shard_map/ppermute | solution.py:26
  17.9 4.1 %copy-start.1 = (bf16[128,3,1024]{2,0,1:T(8,128)(2,1)S(1)}, bf16[128,3,1024]{2,0,1:T(8,128)(2,1)}, u32[]{:S(2)}) copy-start(bf16[128,3,1024]{2,0,1:T(8,128)(2,1)} %param.6) | copy-start | bytes 2359300
  17.9 4.1 %copy-start.4 = (f32[7,3,1024]{2,0,1:T(8,128)S(1)}, f32[7,3,1024]{2,0,1:T(8,128)}, u32[]{:S(2)}) copy-start(f32[7,3,1024]{2,0,1:T(8,128)} %param.7) | copy-start | bytes 258052
  35.4 14.7 %all-to-all-start.2 = ((bf16[8,128,128]{2,1,0:T(8,128)(2,1)}), bf16[8,128,128]{2,1,0:T(8,128)(2,1)S(1)}, u32[]{:S(2)}, u32[]{:S(2)}) async-start(bf16[8,128,128]{2,1,0:T(8,128)(2,1)} %get-tuple-element.28), calls=%async_computation.2 | async-start | bytes 524288 | tf_op jit(solution)/shard_map/all_to_all | solution.py:852
  50.0 14.5 %all-to-all-start.1 = ((bf16[8,128,128]{2,1,0:T(8,128)(2,1)}), bf16[8,128,128]{2,1,0:T(8,128)(2,1)S(1)}, u32[]{:S(2)}, u32[]{:S(2)}) async-start(bf16[8,128,128]{2,1,0:T(8,128)(2,1)} %get-tuple-element.23), calls=%async_computation.1 | async-start | bytes 524288 | tf_op jit(solution)/shard_map/all_to_all | solution.py:852
  67.0 1.0 copy-start.2
  68.0 8.3 %copy-start.3 = (bf16[128,1024]{1,0:T(8,128)(2,1)S(1)}, bf16[128,1024]{1,0:T(8,128)(2,1)}, u32[]{:S(2)}) copy-start(bf16[128,1024]{1,0:T(8,128)(2,1)} %get-tuple-element.31.product_ref) | copy-start | bytes 786436
  71.2 13.7 %collective-permute-start.5 = (bf16[128,2048]{1,0:T(8,128)(2,1)S(1)}, bf16[128,2048]{1,0:T(8,128)(2,1)S(1)}, u32[]{:S(2)}, u32[]{:S(2)}) collective-permute-start(bf16[128,2048]{1,0:T(8,128)(2,1)S(1)} %project.5), channel_id=1, source_target_pairs={{0,1},{1,0},{2,3},{3,2},{4,5},{5,4},{6,7},{7,6},{8,9},{9,8},{10,11... | collective-permute-start | bytes 1572872 | tf_op jit(solution)/shard_map/ppermute | solution.py:26
  71.3 29.4 %all-to-all-start.3 = ((bf16[8,464,128]{2,1,0:T(8,128)(2,1)}), bf16[8,464,128]{2,1,0:T(8,128)(2,1)S(1)}, u32[]{:S(2)}, u32[]{:S(2)}) async-start(bf16[8,464,128]{2,1,0:T(8,128)(2,1)} %get-tuple-element.34), calls=%async_computation.3 | async-start | bytes 1900544 | tf_op jit(solution)/shard_map/all_to_all | solution.py:852
  79.5 8.9 %copy-start.5 = (bf16[8,1024]{1,0:T(8,128)(2,1)S(1)}, bf16[8,1024]{1,0:T(8,128)(2,1)}, u32[]{:S(2)}) copy-start(bf16[8,1024]{1,0:T(8,128)(2,1)} %get-tuple-element.36) | copy-start | bytes 49156
  84.7 5.0 %collective-permute-start.4 = (bf16[128,2048]{1,0:T(8,128)(2,1)S(1)}, bf16[128,2048]{1,0:T(8,128)(2,1)S(1)}, u32[]{:S(2)}, u32[]{:S(2)}) collective-permute-start(bf16[128,2048]{1,0:T(8,128)(2,1)S(1)} %get-tuple-element.33), channel_id=1, source_target_pairs={{0,1},{1,0},{2,3},{3,2},{4,5},{5,4},{6,7},{7,6},{8,9},{9,8},{10,11... | collective-permute-start | bytes 1572872 | tf_op jit(solution)/shard_map/ppermute | solution.py:26
  85.1 14.2 %collective-permute-start.6 = (bf16[128,2048]{1,0:T(8,128)(2,1)S(1)}, bf16[128,2048]{1,0:T(8,128)(2,1)S(1)}, u32[]{:S(2)}, u32[]{:S(2)}) collective-permute-start(bf16[128,2048]{1,0:T(8,128)(2,1)S(1)} %add_convert_fusion.2), channel_id=1, source_target_pairs={{0,2},{1,3},{2,0},{3,1},{4,6},{5,7},{6,4},{7,5},{8,10},{9,11},{10,... | collective-permute-start | bytes 1572872 | tf_op jit(solution)/shard_map/ppermute | solution.py:26
  88.4 11.9 %collective-permute-start.7 = (bf16[8,1024]{1,0:T(8,128)(2,1)S(1)}, bf16[8,1024]{1,0:T(8,128)(2,1)S(1)}, u32[]{:S(2)}, u32[]{:S(2)}) collective-permute-start(bf16[8,1024]{1,0:T(8,128)(2,1)S(1)} %copy-done.5), channel_id=1, source_target_pairs={{4,0},{8,4},{12,8},{16,12},{20,16},{24,20},{28,24},{5,1},{9,5},{13... | collective-permute-start | bytes 49160 | tf_op jit(solution)/shard_map/ppermute | solution.py:32

commit v7 on v6

--- a/solution.py
+++ b/solution.py
@@ -755,7 +755,7 @@
 def finish_kernel(
     got_ref, query_grad_ref, next_ref, taps_ref, local_ref,
     input_grad_ref, filter_ref, medium_ref, short_ref,
-    got, local, ext, input_grad, filtering, medium, sums, sems, *, own_rows, scale,
+    got, local, ext, input_grad, filtering, medium, short, sums, sems, *, own_rows, scale,
 ):
     parts, _, width = got.shape
     length = filtering.shape[0]
@@ -782,6 +782,7 @@
     more = [
         pltpu.make_async_copy(filtering, filter_ref, sems.at[6]),
         pltpu.make_async_copy(medium, medium_ref, sems.at[7]),
+        pltpu.make_async_copy(short, short_ref, sems.at[8]),
     ]
     for j in range(parts):
         ext[0, j, length:, :] = next_ref[:, j * width : (j + 1) * width].astype(F32)
@@ -802,9 +803,9 @@
         small = got[j, first:taps, :].astype(F32)
         medium[:, lanes] = small[0:medium_reach, :]
         second = medium_reach + reach
-        short_ref[0, :, lanes] = sums[j * reach : (j + 1) * reach, :] * scale
-        short_ref[1, :, lanes] = small[medium_reach:second, :]
-        short_ref[2, :, lanes] = small[second : second + reach, :]
+        short[0, :, lanes] = sums[j * reach : (j + 1) * reach, :] * scale
+        short[1, :, lanes] = small[medium_reach:second, :]
+        short[2, :, lanes] = small[second : second + reach, :]
     start_all(more)
     reads[2].wait()
     for k in range(1, 3):
@@ -826,12 +827,12 @@
         partial(finish_kernel, own_rows=own_rows, scale=scale),
         grid=(1,),
         in_specs=[pl.BlockSpec(memory_space=pl.ANY), hbm, whole((HALO, channels)), whole(taps.shape), hbm],
-        out_specs=[hbm, hbm, hbm, whole((groups, reach, channels))],
+        out_specs=[hbm] * 4,
         out_shape=[
             pltpu.HBM((groups, length, channels), BF16),
             pltpu.HBM((length, channels), F32),
             pltpu.HBM((medium_reach, channels), F32),
-            jax.ShapeDtypeStruct((groups, reach, channels), F32),
+            pltpu.HBM((groups, reach, channels), F32),
         ],
         scratch_shapes=[
             pltpu.VMEM(returned.shape, BF16),
@@ -840,8 +841,9 @@
             pltpu.VMEM((groups, length, channels), BF16),
             pltpu.VMEM((length, channels), F32),
             pltpu.VMEM((medium_reach, channels), F32),
+            pltpu.VMEM((groups, reach, channels), F32),
             pltpu.VMEM((-(-parts * reach // 8) * 8, width), F32),
-            pltpu.SemaphoreType.DMA((8,)),
+            pltpu.SemaphoreType.DMA((9,)),
         ],
         compiler_params=limit(24),
         name="finish",

time: 105 us -> 105 us (level)
  transfers between devices with their start and end apart: 12 -> 12, of which waited for: 5 -> 5; matrix products, arithmetic and copies ran while one was open for 8% -> 8% of each run, Pallas kernels for 36% -> 37%
where the time goes in v7:
time: 105 us; the launch traced here: 104 us
  Pallas kernels  46.7 us (44%)
  starting transfers between devices  28.2 us (27%)
  waiting for transfers between devices  18.8 us (18%)
  other arithmetic  6.6 us (6%)
  local copies, waits for them, and re-layouts  2.52 us (2%)
    all_to_all x4, starting transfers between devices, reshard(): return lax.all_to_all(value, 'seq', split_axis=0, concat_axis=0, tiled=True)  19.4 us
    pallas_call x3, Pallas kernels, project(): pl.pallas_call(partial(project_kernel, flips=flips), in_specs=[pl.BlockSp...  11.6 us
    ppermute x6, waiting for transfers between devices, exchange(): lax.ppermute(value, axis, [(source, source ^ flip) for source in range(co...  10.2 us
    all_to_all x4, waiting for transfers between devices, reshard(): return lax.all_to_all(value, 'seq', split_axis=0, concat_axis=0, tiled=True)  8.66 us
    pallas_call x1, Pallas kernels, backward_call(): pl.pallas_call(partial(backward_kernel, freqs=freqs, block=block, scale=s...  7.45 us
    pallas_call x1, Pallas kernels, forward_call(): pl.pallas_call(partial(forward_kernel, freqs=freqs, block=block, resident...  7.05 us
    pallas_call x1, Pallas kernels, product_grad_last(): pl.pallas_call(partial(product_grad_kernel, flips=flips, last=True), grid...  4.79 us
    ppermute x2, starting transfers between devices, shift(): return lax.ppermute(value, axis, pairs)  4.69 us
  transfers between devices with their start and end apart: 12, of which 5 were waited for; matrix products, arithmetic and copies ran while one was open for 8% of the time, Pallas kernels for 37%

profile of v7, /device:TPU:0, one launch (start us, length us, event | category | flops | bytes accessed | tf_op | source)
XLA Modules:
  0.0 103.8 jit_solution(15998270661348834621)
XLA Ops:
  0.6 0.6 collective-permute-start.3
  1.2 2.6 %collective-permute-start.1 = (bf16[128,2048]{1,0:T(8,128)(2,1)}, bf16[128,2048]{1,0:T(8,128)(2,1)S(1)}, u32[]{:S(2)}, u32[]{:S(2)}) collective-permute-start(bf16[128,2048]{1,0:T(8,128)(2,1)} %refs_0_.1), channel_id=1, source_target_pairs={{0,2},{1,3},{2,0},{3,1},{4,6},{5,7},{6,4},{7,5},{8,10},{9,11},{10,... | collective-permute-start | bytes 1572872 | tf_op jit(solution)/shard_map/ppermute | solution.py:26
  3.8 0.8 slice.4
  4.6 3.4 %collective-permute-start = (bf16[3,8,1024]{2,1,0:T(8,128)(2,1)S(1)}, bf16[3,8,1024]{2,1,0:T(8,128)(2,1)S(1)}, u32[]{:S(2)}, u32[]{:S(2)}) collective-permute-start(bf16[3,8,1024]{2,1,0:T(8,128)(2,1)S(1)} %slice.4), channel_id=1, source_target_pairs={{0,4},{4,8},{8,12},{12,16},{16,20},{20,24},{24,28},{1,5},{5,9},{9,... | collective-permute-start | bytes 147464 | tf_op jit(solution)/shard_map/ppermute | solution.py:32
  8.0 2.2 %pack.1 = bf16[8,384,128]{2,1,0:T(8,128)(2,1)} custom-call(bf16[3,128,1024]{2,1,0:T(8,128)(2,1)} %bitcast.10, f32[128,1024]{1,0:T(8,128)} %filter_ref.1), custom_call_target="tpu_custom_call" | custom-call | tf_op jit(solution)/shard_map/pack/pallas_call | solution.py:875
  10.2 4.9 %all-to-all-start = ((bf16[8,384,128]{2,1,0:T(8,128)(2,1)}), bf16[8,384,128]{2,1,0:T(8,128)(2,1)}, u32[]{:S(2)}, u32[]{:S(2)}) async-start(bf16[8,384,128]{2,1,0:T(8,128)(2,1)} %pack.1), calls=%async_computation | async-start | bytes 1572864 | tf_op jit(solution)/shard_map/all_to_all | solution.py:854
  15.1 0.8 fusion.5
  15.9 0.5 collective-permute-done.1.refs_0_
  16.5 0.7 fusion.12
  17.2 0.7 dynamic-slice_bitcast_fusion.taps_ref
  17.9 4.0 %grad_first.1.refs_2_ = f32[128,1024]{1,0:T(8,128)S(1)} custom-call(s32[1]{0:T(128)} %bitcast.place_ref, bf16[8192,1024]{1,0:T(8,128)(2,1)} %w_ref.9, bf16[128,2048]{1,0:T(8,128)(2,1)} %refs_0_.1, bf16[128,2048]{1,0:T(8,128)(2,1)S(1)} %collective-permute-done.3.refs_1_), custom_call_target="tpu_custom_call" | custom-call | tf_op jit(solution)/shard_map/grad_first/pallas_call | solution.py:170
  22.0 4.8 %grad_last.1 = (f32[128,1024]{1,0:T(8,128)}, f32[128,1024]{1,0:T(8,128)}, bf16[8,128,128]{2,1,0:T(8,128)(2,1)}) custom-call(s32[1]{0:T(128)} %bitcast.place_ref, bf16[8192,1024]{1,0:T(8,128)(2,1)} %w_ref.9, bf16[128,2048]{1,0:T(8,128)(2,1)S(1)} %collective-permute-done.1.refs_0_, bf16[128,2048]{1,0:T(8,128)(2,1)S(1)} %collective-permute-done.2.refs_1_, ...), custom_call_target="tpu_custom_call" | custom-call | tf_op jit(solution)/shard_map/grad_last/pallas_call | solution.py:188
  26.8 1.5 %edge_rows.1 = (f32[128,1024]{1,0:T(8,128)}, bf16[8,128,128]{2,1,0:T(8,128)(2,1)}) custom-call(bf16[3,128,1024]{2,1,0:T(8,128)(2,1)S(1)} %bitcast.14, bf16[3,8,1024]{2,1,0:T(8,128)(2,1)S(1)} %collective-permute-done.edge_ref, f32[3,7,1024]{2,1,0:T(8,128)S(1)} %bitcast.16, ...), custom_call_target="tpu_custom_call", output_to_operand_aliasing={{0}: (4, {}), {1}: (5, {})} | custom-call | tf_op jit(solution)/shard_map/edge_rows/pallas_call | solution.py:232
  28.3 7.1 %all-to-all-done.got_ref = bf16[8,384,128]{2,1,0:T(8,128)(2,1)} async-done(((bf16[8,384,128]{2,1,0:T(8,128)(2,1)}), bf16[8,384,128]{2,1,0:T(8,128)(2,1)}, u32[]{:S(2)}, u32[]{:S(2)}) %all-to-all-start) | async-done | bytes 786464 | tf_op jit(solution)/shard_map/all_to_all | solution.py:854
  35.4 3.6 %all-to-all-start.2 = ((bf16[8,128,128]{2,1,0:T(8,128)(2,1)}), bf16[8,128,128]{2,1,0:T(8,128)(2,1)S(1)}, u32[]{:S(2)}, u32[]{:S(2)}) async-start(bf16[8,128,128]{2,1,0:T(8,128)(2,1)} %get-tuple-element.28), calls=%async_computation.2 | async-start | bytes 524288 | tf_op jit(solution)/shard_map/all_to_all | solution.py:854
  38.9 4.0 %add_convert_fusion = (bf16[36,32,1152]{2,1,0:T(8,128)(2,1)}, bf16[36,32,1152]{2,1,0:T(8,128)(2,1)}) fusion(f32[32,1152]{1,0:T(8,128)S(1)} %get-tuple-element.46, f32[36,1152]{1,0:T(8,128)S(1)} %get-tuple-element.44, f32[32,1152]{1,0:T(8,128)S(1)} %get-tuple-element.45, f32[36,1152]{1,0:T(8,128)S(1)} %get-tuple-element.43), kind=kLoop, calls=%fused_computation | loop fusion | flops 10616832 | bytes 5935104 | tf_op jit(solution)/shard_map/convert_element_type | solution.py:56
  42.9 7.0 %forward_spectral.1 = (bf16[8,128,128]{2,1,0:T(8,128)(2,1)}, f32[2,1024,128]{2,1,0:T(8,128)}, f32[4,1152,128]{2,1,0:T(8,128)}) custom-call(bf16[8,384,128]{2,1,0:T(8,128)(2,1)} %all-to-all-done.got_ref, f32[3,7,128]{2,1,0:T(8,128)S(1)} %dynamic-slice_bitcast_fusion.taps_ref, f32[120,128]{1,0:T(8,128)S(1)} %constant_dynamic-slice_fusion.medium_ref, ...), custom_call_target="tpu_custom_call" | custom-call | tf_op jit(solution)/shard_map/forward_spectral/pallas_call | solution.py:555
  50.0 6.0 %all-to-all-start.1 = ((bf16[8,128,128]{2,1,0:T(8,128)(2,1)}), bf16[8,128,128]{2,1,0:T(8,128)(2,1)S(1)}, u32[]{:S(2)}, u32[]{:S(2)}) async-start(bf16[8,128,128]{2,1,0:T(8,128)(2,1)} %get-tuple-element.23), calls=%async_computation.1 | async-start | bytes 524288 | tf_op jit(solution)/shard_map/all_to_all | solution.py:854
  56.0 7.4 %backward_spectral.1._ = bf16[8,464,128]{2,1,0:T(8,128)(2,1)} custom-call(f32[3,7,128]{2,1,0:T(8,128)S(1)} %dynamic-slice_bitcast_fusion.taps_ref, f32[120,128]{1,0:T(8,128)S(1)} %constant_dynamic-slice_fusion.medium_ref, bf16[8,128,128]{2,1,0:T(8,128)(2,1)S(1)} %all-to-all-done.2.grads_ref, bf16[8,384,128]{2,1,0:T(8,128)(2,1)} %all-to-all-done.got_ref, ...), custom_call_target="tpu_custom_call" | custom-call | tf_op jit(solution)/shard_map/backward_spectral/pallas_call | solution.py:596
  63.5 1.1 %all-to-all-done.1.got_ref = bf16[8,128,128]{2,1,0:T(8,128)(2,1)S(1)} async-done(((bf16[8,128,128]{2,1,0:T(8,128)(2,1)}), bf16[8,128,128]{2,1,0:T(8,128)(2,1)S(1)}, u32[]{:S(2)}, u32[]{:S(2)}) %all-to-all-start.1) | async-done | bytes 262176 | tf_op jit(solution)/shard_map/all_to_all | solution.py:854
  64.6 2.5 %product.1 = (bf16[128,1024]{1,0:T(8,128)(2,1)}, f32[8,128,128]{2,1,0:T(8,128)}, bf16[8,1024]{1,0:T(8,128)(2,1)}, bf16[8,464,128]{2,1,0:T(8,128)(2,1)}) custom-call(bf16[8,128,128]{2,1,0:T(8,128)(2,1)S(1)} %all-to-all-done.1.got_ref, f32[128,1024]{1,0:T(8,128)} %get-tuple-element.27.query_ref, ...), custom_call_target="tpu_custom_call", output_to_operand_aliasing={{3}: (5, {})} | custom-call | tf_op jit(solution)/shard_map/product/pallas_call | solution.py:681
  67.0 0.9 copy-done.2
  68.0 3.3 %project.5 = bf16[128,2048]{1,0:T(8,128)(2,1)S(1)} custom-call(s32[1]{0:T(128)} %bitcast.place_ref, bf16[128,1024]{1,0:T(8,128)(2,1)S(1)} %copy-done.2, bf16[8192,1024]{1,0:T(8,128)(2,1)} %w_ref.9), custom_call_target="tpu_custom_call" | custom-call | tf_op jit(solution)/shard_map/project/pallas_call | solution.py:731
  71.3 4.9 %all-to-all-start.3 = ((bf16[8,464,128]{2,1,0:T(8,128)(2,1)}), bf16[8,464,128]{2,1,0:T(8,128)(2,1)S(1)}, u32[]{:S(2)}, u32[]{:S(2)}) async-start(bf16[8,464,128]{2,1,0:T(8,128)(2,1)} %get-tuple-element.34), calls=%async_computation.3 | async-start | bytes 1900544 | tf_op jit(solution)/shard_map/all_to_all | solution.py:854
  76.3 3.2 %project.4 = f32[128,2048]{1,0:T(8,128)S(1)} custom-call(s32[1]{0:T(128)} %bitcast.place_ref, bf16[128,1024]{1,0:T(8,128)(2,1)S(1)} %copy-done.3, bf16[8192,1024]{1,0:T(8,128)(2,1)} %w_ref.9), custom_call_target="tpu_custom_call" | custom-call | tf_op jit(solution)/shard_map/project/pallas_call | solution.py:731
  79.5 5.2 %project.3 = (bf16[128,2048]{1,0:T(8,128)(2,1)S(1)}, f32[128,2048]{1,0:T(8,128)S(1)}) custom-call(s32[1]{0:T(128)} %bitcast.place_ref, bf16[128,1024]{1,0:T(8,128)(2,1)S(1)} %copy-done.3, bf16[8192,1024]{1,0:T(8,128)(2,1)} %w_ref.9), custom_call_target="tpu_custom_call" | custom-call | tf_op jit(solution)/shard_map/project/pallas_call | solution.py:731
  85.1 0.6 collective-permute-start.6
  85.7 2.7 %local.1.local_ref = f32[2,8,128,128]{3,2,1,0:T(8,128)} custom-call(bf16[3,128,1024]{2,1,0:T(8,128)(2,1)} %bitcast.12, bf16[3,8,1024]{2,1,0:T(8,128)(2,1)S(1)} %collective-permute-done.edge_ref, f32[3,7,1024]{2,1,0:T(8,128)S(1)} %bitcast.17), custom_call_target="tpu_custom_call" | custom-call | tf_op jit(solution)/shard_map/local/pallas_call | solution.py:929
  88.4 1.3 %collective-permute-start.7 = (bf16[8,1024]{1,0:T(8,128)(2,1)S(1)}, bf16[8,1024]{1,0:T(8,128)(2,1)S(1)}, u32[]{:S(2)}, u32[]{:S(2)}) collective-permute-start(bf16[8,1024]{1,0:T(8,128)(2,1)S(1)} %copy-done.5), channel_id=1, source_target_pairs={{4,0},{8,4},{12,8},{16,12},{20,16},{24,20},{28,24},{5,1},{9,5},{13... | collective-permute-start | bytes 49160 | tf_op jit(solution)/shard_map/ppermute | solution.py:32
  89.7 9.6 %collective-permute-done.6 = bf16[128,2048]{1,0:T(8,128)(2,1)S(1)} collective-permute-done((bf16[128,2048]{1,0:T(8,128)(2,1)S(1)}, bf16[128,2048]{1,0:T(8,128)(2,1)S(1)}, u32[]{:S(2)}, u32[]{:S(2)}) %collective-permute-start.6) | collective-permute-done | bytes 524320 | tf_op jit(solution)/shard_map/ppermute | solution.py:26
  99.3 1.0 add_convert_fusion.1
  100.8 2.9 %finish.1 = (bf16[3,128,1024]{2,1,0:T(8,128)(2,1)}, f32[128,1024]{1,0:T(8,128)}, f32[120,1024]{1,0:T(8,128)}, f32[3,7,1024]{2,1,0:T(8,128)}) custom-call(bf16[8,464,128]{2,1,0:T(8,128)(2,1)S(1)} %all-to-all-done.3.got_ref, f32[8,128,128]{2,1,0:T(8,128)} %get-tuple-element.35.query_grad_ref, bf16[8,1024]{1,0:T(8,128)(2,1)S(1)} %collective-permute-done.7.next_ref, ...), custom_call_target="tpu_custom_call" | custom-call | tf_op jit(solution)/shard_map/finish/pallas_call | solution.py:826
  (27 shorter events, 1.0 us)
Async XLA Ops:
  0.6 14.4 %copy-start = (f32[120,1024]{1,0:T(8,128)S(1)}, f32[120,1024]{1,0:T(8,128)}, u32[]{:S(2)}) copy-start(f32[120,1024]{1,0:T(8,128)} %param.8) | copy-start | bytes 1474564
  0.6 17.3 %collective-permute-start.3 = (bf16[128,2048]{1,0:T(8,128)(2,1)}, bf16[128,2048]{1,0:T(8,128)(2,1)S(1)}, u32[]{:S(2)}, u32[]{:S(2)}) collective-permute-start(bf16[128,2048]{1,0:T(8,128)(2,1)} %refs_0_.1), channel_id=1, source_target_pairs={{0,1},{1,0},{2,3},{3,2},{4,5},{5,4},{6,7},{7,6},{8,9},{9,8},{10,11... | collective-permute-start | bytes 1572872 | tf_op jit(solution)/shard_map/ppermute | solution.py:26
  1.2 15.3 %collective-permute-start.1 = (bf16[128,2048]{1,0:T(8,128)(2,1)}, bf16[128,2048]{1,0:T(8,128)(2,1)S(1)}, u32[]{:S(2)}, u32[]{:S(2)}) collective-permute-start(bf16[128,2048]{1,0:T(8,128)(2,1)} %refs_0_.1), channel_id=1, source_target_pairs={{0,2},{1,3},{2,0},{3,1},{4,6},{5,7},{6,4},{7,5},{8,10},{9,11},{10,... | collective-permute-start | bytes 1572872 | tf_op jit(solution)/shard_map/ppermute | solution.py:26
  4.6 22.2 %collective-permute-start = (bf16[3,8,1024]{2,1,0:T(8,128)(2,1)S(1)}, bf16[3,8,1024]{2,1,0:T(8,128)(2,1)S(1)}, u32[]{:S(2)}, u32[]{:S(2)}) collective-permute-start(bf16[3,8,1024]{2,1,0:T(8,128)(2,1)S(1)} %slice.4), channel_id=1, source_target_pairs={{0,4},{4,8},{8,12},{12,16},{16,20},{20,24},{24,28},{1,5},{5,9},{9,... | collective-permute-start | bytes 147464 | tf_op jit(solution)/shard_map/ppermute | solution.py:32
  10.2 25.2 %all-to-all-start = ((bf16[8,384,128]{2,1,0:T(8,128)(2,1)}), bf16[8,384,128]{2,1,0:T(8,128)(2,1)}, u32[]{:S(2)}, u32[]{:S(2)}) async-start(bf16[8,384,128]{2,1,0:T(8,128)(2,1)} %pack.1), calls=%async_computation | async-start | bytes 1572864 | tf_op jit(solution)/shard_map/all_to_all | solution.py:854
  16.5 5.5 %collective-permute-start.2 = (bf16[128,2048]{1,0:T(8,128)(2,1)S(1)}, bf16[128,2048]{1,0:T(8,128)(2,1)S(1)}, u32[]{:S(2)}, u32[]{:S(2)}) collective-permute-start(bf16[128,2048]{1,0:T(8,128)(2,1)S(1)} %collective-permute-done.1.refs_0_), channel_id=1, source_target_pairs={{0,1},{1,0},{2,3},{3,2},{4,5},{5,4},{6,7},{7,6},{8,9},{9,8},{10,11... | collective-permute-start | bytes 1572872 | tf_op jit(solution)/shard_map/ppermute | solution.py:26
  17.9 4.1 %copy-start.1 = (bf16[128,3,1024]{2,0,1:T(8,128)(2,1)S(1)}, bf16[128,3,1024]{2,0,1:T(8,128)(2,1)}, u32[]{:S(2)}) copy-start(bf16[128,3,1024]{2,0,1:T(8,128)(2,1)} %param.6) | copy-start | bytes 2359300
  17.9 4.1 %copy-start.4 = (f32[7,3,1024]{2,0,1:T(8,128)S(1)}, f32[7,3,1024]{2,0,1:T(8,128)}, u32[]{:S(2)}) copy-start(f32[7,3,1024]{2,0,1:T(8,128)} %param.7) | copy-start | bytes 258052
  35.4 14.7 %all-to-all-start.2 = ((bf16[8,128,128]{2,1,0:T(8,128)(2,1)}), bf16[8,128,128]{2,1,0:T(8,128)(2,1)S(1)}, u32[]{:S(2)}, u32[]{:S(2)}) async-start(bf16[8,128,128]{2,1,0:T(8,128)(2,1)} %get-tuple-element.28), calls=%async_computation.2 | async-start | bytes 524288 | tf_op jit(solution)/shard_map/all_to_all | solution.py:854
  50.0 14.5 %all-to-all-start.1 = ((bf16[8,128,128]{2,1,0:T(8,128)(2,1)}), bf16[8,128,128]{2,1,0:T(8,128)(2,1)S(1)}, u32[]{:S(2)}, u32[]{:S(2)}) async-start(bf16[8,128,128]{2,1,0:T(8,128)(2,1)} %get-tuple-element.23), calls=%async_computation.1 | async-start | bytes 524288 | tf_op jit(solution)/shard_map/all_to_all | solution.py:854
  67.0 1.0 copy-start.2
  68.0 8.3 %copy-start.3 = (bf16[128,1024]{1,0:T(8,128)(2,1)S(1)}, bf16[128,1024]{1,0:T(8,128)(2,1)}, u32[]{:S(2)}) copy-start(bf16[128,1024]{1,0:T(8,128)(2,1)} %get-tuple-element.31.product_ref) | copy-start | bytes 786436
  71.2 13.7 %collective-permute-start.5 = (bf16[128,2048]{1,0:T(8,128)(2,1)S(1)}, bf16[128,2048]{1,0:T(8,128)(2,1)S(1)}, u32[]{:S(2)}, u32[]{:S(2)}) collective-permute-start(bf16[128,2048]{1,0:T(8,128)(2,1)S(1)} %project.5), channel_id=1, source_target_pairs={{0,1},{1,0},{2,3},{3,2},{4,5},{5,4},{6,7},{7,6},{8,9},{9,8},{10,11... | collective-permute-start | bytes 1572872 | tf_op jit(solution)/shard_map/ppermute | solution.py:26
  71.3 29.4 %all-to-all-start.3 = ((bf16[8,464,128]{2,1,0:T(8,128)(2,1)}), bf16[8,464,128]{2,1,0:T(8,128)(2,1)S(1)}, u32[]{:S(2)}, u32[]{:S(2)}) async-start(bf16[8,464,128]{2,1,0:T(8,128)(2,1)} %get-tuple-element.34), calls=%async_computation.3 | async-start | bytes 1900544 | tf_op jit(solution)/shard_map/all_to_all | solution.py:854
  79.5 8.9 %copy-start.5 = (bf16[8,1024]{1,0:T(8,128)(2,1)S(1)}, bf16[8,1024]{1,0:T(8,128)(2,1)}, u32[]{:S(2)}) copy-start(bf16[8,1024]{1,0:T(8,128)(2,1)} %get-tuple-element.36) | copy-start | bytes 49156
  84.7 5.0 %collective-permute-start.4 = (bf16[128,2048]{1,0:T(8,128)(2,1)S(1)}, bf16[128,2048]{1,0:T(8,128)(2,1)S(1)}, u32[]{:S(2)}, u32[]{:S(2)}) collective-permute-start(bf16[128,2048]{1,0:T(8,128)(2,1)S(1)} %get-tuple-element.33), channel_id=1, source_target_pairs={{0,1},{1,0},{2,3},{3,2},{4,5},{5,4},{6,7},{7,6},{8,9},{9,8},{10,11... | collective-permute-start | bytes 1572872 | tf_op jit(solution)/shard_map/ppermute | solution.py:26
  85.1 14.2 %collective-permute-start.6 = (bf16[128,2048]{1,0:T(8,128)(2,1)S(1)}, bf16[128,2048]{1,0:T(8,128)(2,1)S(1)}, u32[]{:S(2)}, u32[]{:S(2)}) collective-permute-start(bf16[128,2048]{1,0:T(8,128)(2,1)S(1)} %add_convert_fusion.2), channel_id=1, source_target_pairs={{0,2},{1,3},{2,0},{3,1},{4,6},{5,7},{6,4},{7,5},{8,10},{9,11},{10,... | collective-permute-start | bytes 1572872 | tf_op jit(solution)/shard_map/ppermute | solution.py:26
  88.4 11.9 %collective-permute-start.7 = (bf16[8,1024]{1,0:T(8,128)(2,1)S(1)}, bf16[8,1024]{1,0:T(8,128)(2,1)S(1)}, u32[]{:S(2)}, u32[]{:S(2)}) collective-permute-start(bf16[8,1024]{1,0:T(8,128)(2,1)S(1)} %copy-done.5), channel_id=1, source_target_pairs={{4,0},{8,4},{12,8},{16,12},{20,16},{24,20},{28,24},{5,1},{9,5},{13... | collective-permute-start | bytes 49160 | tf_op jit(solution)/shard_map/ppermute | solution.py:32

commit v8 on v7

--- a/solution.py
+++ b/solution.py
@@ -65,9 +65,12 @@
     return pltpu.CompilerParams(vmem_limit_bytes=mebibytes << 20)
 
 
-def pack_kernel(x_ref, filter_ref, out_ref, streams, taps, rounded, sems):
+def pack_kernel(x_ref, filter_ref, out_ref, edge_ref, streams, taps, rounded, edge, sems, edge_sems):
     parts, rows, width = out_ref.shape
     length = rows // 3
+    read_edge = pltpu.make_async_copy(x_ref.at[:, pl.ds(length - HALO, HALO), :], edge, edge_sems.at[0])
+    write_edge = pltpu.make_async_copy(edge, edge_ref, edge_sems.at[1])
+    read_edge.start()
     read_filter = pltpu.make_async_copy(filter_ref, taps, sems.at[0])
     read_streams = pltpu.make_async_copy(x_ref.at[pl.ds(1, 2)], streams, sems.at[1])
     read_filter.start()
@@ -75,6 +78,8 @@
     read_filter.wait()
     for j in range(parts):
         rounded[j, 2 * length :, :] = taps[:, j * width : (j + 1) * width].astype(BF16)
+    read_edge.wait()
+    write_edge.start()
     read_streams.wait()
     writes = []
     for j in range(parts):
@@ -85,6 +90,7 @@
         writes[j].start()
     for write in writes:
         write.wait()
+    write_edge.wait()
 
 
 def weight_chunks(place_ref, weight_ref, buffer, sems, flips, features):
@@ -855,7 +861,7 @@
 
 
 def local(inputs, short_taps, medium_taps, long_filter, out_weight, out_cotangent):
-    length, _, channels = inputs.shape
+    length, groups, channels = inputs.shape
     reach = short_taps.shape[0]
     medium_reach = medium_taps.shape[0]
     parts = lax.axis_size("seq")
@@ -872,16 +878,21 @@
     streams = inputs.transpose(1, 0, 2)
     taps = short_taps.transpose(1, 0, 2)
     hbm = pl.BlockSpec(memory_space=pltpu.HBM)
-    packed = pl.pallas_call(
+    packed, last_rows = pl.pallas_call(
         pack_kernel,
         in_specs=[hbm, hbm],
-        out_specs=hbm,
-        out_shape=pltpu.HBM((parts, 3 * length, width), BF16),
+        out_specs=[hbm, hbm],
+        out_shape=[
+            pltpu.HBM((parts, 3 * length, width), BF16),
+            pltpu.HBM((groups, HALO, channels), BF16),
+        ],
         scratch_shapes=[
             pltpu.VMEM((2, length, channels), BF16),
             pltpu.VMEM((length, channels), F32),
             pltpu.VMEM((parts, 3 * length, width), BF16),
+            pltpu.VMEM((groups, HALO, channels), BF16),
             pltpu.SemaphoreType.DMA((2 + parts,)),
+            pltpu.SemaphoreType.DMA((2,)),
         ],
         compiler_params=limit(8),
         name="pack",
@@ -890,7 +901,7 @@
         pltpu.with_memory_space_constraint(long_filter, pltpu.HBM),
     )
     got = reshard(packed)
-    edge = shift(streams[:, length - HALO :], "seq", 1)
+    edge = shift(last_rows, "seq", 1)
     cot_x = exchange(out_cotangent, "tensor", 2)
     cot_core = exchange(out_cotangent, "tensor", 1)
 

time: 105 us -> 104 us (level)
  transfers between devices with their start and end apart: 12 -> 12, of which waited for: 5 -> 5; matrix products, arithmetic and copies ran while one was open for 8% -> 7% of each run, Pallas kernels for 37% -> 37%
where the time goes in v8:
time: 104 us; the launch traced here: 103 us
  Pallas kernels  46.7 us (45%)
  starting transfers between devices  28.2 us (27%)
  waiting for transfers between devices  18.8 us (18%)
  other arithmetic  6.6 us (6%)
  local copies, waits for them, and re-layouts  1.72 us (2%)
  between operations  1.04 us (1%)
    all_to_all x4, starting transfers between devices, reshard(): return lax.all_to_all(value, 'seq', split_axis=0, concat_axis=0, tiled=True)  19.4 us
    pallas_call x3, Pallas kernels, project(): pl.pallas_call(partial(project_kernel, flips=flips), in_specs=[pl.BlockSp...  11.6 us
    ppermute x6, waiting for transfers between devices, exchange(): lax.ppermute(value, axis, [(source, source ^ flip) for source in range(co...  10.9 us
    all_to_all x4, waiting for transfers between devices, reshard(): return lax.all_to_all(value, 'seq', split_axis=0, concat_axis=0, tiled=True)  7.9 us
    pallas_call x1, Pallas kernels, backward_call(): pl.pallas_call(partial(backward_kernel, freqs=freqs, block=block, scale=s...  7.45 us
    pallas_call x1, Pallas kernels, forward_call(): pl.pallas_call(partial(forward_kernel, freqs=freqs, block=block, resident...  7.05 us
    pallas_call x1, Pallas kernels, product_grad_last(): pl.pallas_call(partial(product_grad_kernel, flips=flips, last=True), grid...  4.79 us
    ppermute x2, starting transfers between devices, shift(): return lax.ppermute(value, axis, pairs)  4.71 us
  transfers between devices with their start and end apart: 12, of which 5 were waited for; matrix products, arithmetic and copies ran while one was open for 7% of the time, Pallas kernels for 37%

profile of v8, /device:TPU:0, one launch (start us, length us, event | category | flops | bytes accessed | tf_op | source)
XLA Modules:
  0.0 103.1 jit_solution(13235492305043946838)
XLA Ops:
  0.6 0.6 collective-permute-start.3
  1.2 2.6 %collective-permute-start.1 = (bf16[128,2048]{1,0:T(8,128)(2,1)}, bf16[128,2048]{1,0:T(8,128)(2,1)S(1)}, u32[]{:S(2)}, u32[]{:S(2)}) collective-permute-start(bf16[128,2048]{1,0:T(8,128)(2,1)} %refs_0_.1), channel_id=1, source_target_pairs={{0,2},{1,3},{2,0},{3,1},{4,6},{5,7},{6,4},{7,5},{8,10},{9,11},{10,... | collective-permute-start | bytes 1572872 | tf_op jit(solution)/shard_map/ppermute | solution.py:26
  3.8 2.2 %pack.1 = (bf16[8,384,128]{2,1,0:T(8,128)(2,1)}, bf16[3,8,1024]{2,1,0:T(8,128)(2,1)}) custom-call(bf16[3,128,1024]{2,1,0:T(8,128)(2,1)} %bitcast.9, f32[128,1024]{1,0:T(8,128)} %filter_ref.1), custom_call_target="tpu_custom_call" | custom-call | tf_op jit(solution)/shard_map/pack/pallas_call | solution.py:881
  6.0 3.4 %collective-permute-start = (bf16[3,8,1024]{2,1,0:T(8,128)(2,1)}, bf16[3,8,1024]{2,1,0:T(8,128)(2,1)S(1)}, u32[]{:S(2)}, u32[]{:S(2)}) collective-permute-start(bf16[3,8,1024]{2,1,0:T(8,128)(2,1)} %get-tuple-element.27), channel_id=1, source_target_pairs={{0,4},{4,8},{8,12},{12,16},{16,20},{20,24},{24,28},{1,5},{5,9},{9,... | collective-permute-start | bytes 147464 | tf_op jit(solution)/shard_map/ppermute | solution.py:32
  9.4 4.9 %all-to-all-start = ((bf16[8,384,128]{2,1,0:T(8,128)(2,1)}), bf16[8,384,128]{2,1,0:T(8,128)(2,1)}, u32[]{:S(2)}, u32[]{:S(2)}) async-start(bf16[8,384,128]{2,1,0:T(8,128)(2,1)} %get-tuple-element.25), calls=%async_computation | async-start | bytes 1572864 | tf_op jit(solution)/shard_map/all_to_all | solution.py:860
  14.4 0.8 fusion.5
  15.2 1.3 %collective-permute-done.1.refs_0_ = bf16[128,2048]{1,0:T(8,128)(2,1)S(1)} collective-permute-done((bf16[128,2048]{1,0:T(8,128)(2,1)}, bf16[128,2048]{1,0:T(8,128)(2,1)S(1)}, u32[]{:S(2)}, u32[]{:S(2)}) %collective-permute-start.1) | collective-permute-done | bytes 524320 | tf_op jit(solution)/shard_map/ppermute | solution.py:26
  16.5 0.7 fusion.12
  17.2 0.7 dynamic-slice_bitcast_fusion.taps_ref
  17.9 4.0 %grad_first.1.refs_2_ = f32[128,1024]{1,0:T(8,128)S(1)} custom-call(s32[1]{0:T(128)} %bitcast.place_ref, bf16[8192,1024]{1,0:T(8,128)(2,1)} %w_ref.9, bf16[128,2048]{1,0:T(8,128)(2,1)} %refs_0_.1, bf16[128,2048]{1,0:T(8,128)(2,1)S(1)} %collective-permute-done.3.refs_1_), custom_call_target="tpu_custom_call" | custom-call | tf_op jit(solution)/shard_map/grad_first/pallas_call | solution.py:176
  22.0 4.8 %grad_last.1 = (f32[128,1024]{1,0:T(8,128)}, f32[128,1024]{1,0:T(8,128)}, bf16[8,128,128]{2,1,0:T(8,128)(2,1)}) custom-call(s32[1]{0:T(128)} %bitcast.place_ref, bf16[8192,1024]{1,0:T(8,128)(2,1)} %w_ref.9, bf16[128,2048]{1,0:T(8,128)(2,1)S(1)} %collective-permute-done.1.refs_0_, bf16[128,2048]{1,0:T(8,128)(2,1)S(1)} %collective-permute-done.2.refs_1_, ...), custom_call_target="tpu_custom_call" | custom-call | tf_op jit(solution)/shard_map/grad_last/pallas_call | solution.py:194
  26.8 1.5 %edge_rows.1 = (f32[128,1024]{1,0:T(8,128)}, bf16[8,128,128]{2,1,0:T(8,128)(2,1)}) custom-call(bf16[3,128,1024]{2,1,0:T(8,128)(2,1)S(1)} %bitcast.13, bf16[3,8,1024]{2,1,0:T(8,128)(2,1)S(1)} %collective-permute-done.edge_ref, f32[3,7,1024]{2,1,0:T(8,128)S(1)} %bitcast.15, ...), custom_call_target="tpu_custom_call", output_to_operand_aliasing={{0}: (4, {}), {1}: (5, {})} | custom-call | tf_op jit(solution)/shard_map/edge_rows/pallas_call | solution.py:238
  28.3 6.3 %all-to-all-done.got_ref = bf16[8,384,128]{2,1,0:T(8,128)(2,1)} async-done(((bf16[8,384,128]{2,1,0:T(8,128)(2,1)}), bf16[8,384,128]{2,1,0:T(8,128)(2,1)}, u32[]{:S(2)}, u32[]{:S(2)}) %all-to-all-start) | async-done | bytes 786464 | tf_op jit(solution)/shard_map/all_to_all | solution.py:860
  34.6 3.6 %all-to-all-start.2 = ((bf16[8,128,128]{2,1,0:T(8,128)(2,1)}), bf16[8,128,128]{2,1,0:T(8,128)(2,1)S(1)}, u32[]{:S(2)}, u32[]{:S(2)}) async-start(bf16[8,128,128]{2,1,0:T(8,128)(2,1)} %get-tuple-element.32), calls=%async_computation.2 | async-start | bytes 524288 | tf_op jit(solution)/shard_map/all_to_all | solution.py:860
  38.2 4.0 %add_convert_fusion = (bf16[36,32,1152]{2,1,0:T(8,128)(2,1)}, bf16[36,32,1152]{2,1,0:T(8,128)(2,1)}) fusion(f32[32,1152]{1,0:T(8,128)S(1)} %get-tuple-element.50, f32[36,1152]{1,0:T(8,128)S(1)} %get-tuple-element.48, f32[32,1152]{1,0:T(8,128)S(1)} %get-tuple-element.49, f32[36,1152]{1,0:T(8,128)S(1)} %get-tuple-element.47), kind=kLoop, calls=%fused_computation | loop fusion | flops 10616832 | bytes 5935104 | tf_op jit(solution)/shard_map/convert_element_type | solution.py:56
  42.2 7.0 %forward_spectral.1 = (bf16[8,128,128]{2,1,0:T(8,128)(2,1)}, f32[2,1024,128]{2,1,0:T(8,128)}, f32[4,1152,128]{2,1,0:T(8,128)}) custom-call(bf16[8,384,128]{2,1,0:T(8,128)(2,1)} %all-to-all-done.got_ref, f32[3,7,128]{2,1,0:T(8,128)S(1)} %dynamic-slice_bitcast_fusion.taps_ref, f32[120,128]{1,0:T(8,128)S(1)} %constant_dynamic-slice_fusion.medium_ref, ...), custom_call_target="tpu_custom_call" | custom-call | tf_op jit(solution)/shard_map/forward_spectral/pallas_call | solution.py:561
  49.2 6.0 %all-to-all-start.1 = ((bf16[8,128,128]{2,1,0:T(8,128)(2,1)}), bf16[8,128,128]{2,1,0:T(8,128)(2,1)S(1)}, u32[]{:S(2)}, u32[]{:S(2)}) async-start(bf16[8,128,128]{2,1,0:T(8,128)(2,1)} %get-tuple-element.26), calls=%async_computation.1 | async-start | bytes 524288 | tf_op jit(solution)/shard_map/all_to_all | solution.py:860
  55.3 7.5 %backward_spectral.1._ = bf16[8,464,128]{2,1,0:T(8,128)(2,1)} custom-call(f32[3,7,128]{2,1,0:T(8,128)S(1)} %dynamic-slice_bitcast_fusion.taps_ref, f32[120,128]{1,0:T(8,128)S(1)} %constant_dynamic-slice_fusion.medium_ref, bf16[8,128,128]{2,1,0:T(8,128)(2,1)S(1)} %all-to-all-done.2.grads_ref, bf16[8,384,128]{2,1,0:T(8,128)(2,1)} %all-to-all-done.got_ref, ...), custom_call_target="tpu_custom_call" | custom-call | tf_op jit(solution)/shard_map/backward_spectral/pallas_call | solution.py:602
  62.7 1.1 %all-to-all-done.1.got_ref = bf16[8,128,128]{2,1,0:T(8,128)(2,1)S(1)} async-done(((bf16[8,128,128]{2,1,0:T(8,128)(2,1)}), bf16[8,128,128]{2,1,0:T(8,128)(2,1)S(1)}, u32[]{:S(2)}, u32[]{:S(2)}) %all-to-all-start.1) | async-done | bytes 262176 | tf_op jit(solution)/shard_map/all_to_all | solution.py:860
  63.8 2.5 %product.1 = (bf16[128,1024]{1,0:T(8,128)(2,1)}, f32[8,128,128]{2,1,0:T(8,128)}, bf16[8,1024]{1,0:T(8,128)(2,1)}, bf16[8,464,128]{2,1,0:T(8,128)(2,1)}) custom-call(bf16[8,128,128]{2,1,0:T(8,128)(2,1)S(1)} %all-to-all-done.1.got_ref, f32[128,1024]{1,0:T(8,128)} %get-tuple-element.31.query_ref, ...), custom_call_target="tpu_custom_call", output_to_operand_aliasing={{3}: (5, {})} | custom-call | tf_op jit(solution)/shard_map/product/pallas_call | solution.py:687
  66.3 0.9 copy-done.2
  67.2 3.2 %project.5 = bf16[128,2048]{1,0:T(8,128)(2,1)S(1)} custom-call(s32[1]{0:T(128)} %bitcast.place_ref, bf16[128,1024]{1,0:T(8,128)(2,1)S(1)} %copy-done.2, bf16[8192,1024]{1,0:T(8,128)(2,1)} %w_ref.9), custom_call_target="tpu_custom_call" | custom-call | tf_op jit(solution)/shard_map/project/pallas_call | solution.py:737
  70.6 4.9 %all-to-all-start.3 = ((bf16[8,464,128]{2,1,0:T(8,128)(2,1)}), bf16[8,464,128]{2,1,0:T(8,128)(2,1)S(1)}, u32[]{:S(2)}, u32[]{:S(2)}) async-start(bf16[8,464,128]{2,1,0:T(8,128)(2,1)} %get-tuple-element.38), calls=%async_computation.3 | async-start | bytes 1900544 | tf_op jit(solution)/shard_map/all_to_all | solution.py:860
  75.5 3.2 %project.4 = f32[128,2048]{1,0:T(8,128)S(1)} custom-call(s32[1]{0:T(128)} %bitcast.place_ref, bf16[128,1024]{1,0:T(8,128)(2,1)S(1)} %copy-done.3, bf16[8192,1024]{1,0:T(8,128)(2,1)} %w_ref.9), custom_call_target="tpu_custom_call" | custom-call | tf_op jit(solution)/shard_map/project/pallas_call | solution.py:737
  78.7 5.2 %project.3 = (bf16[128,2048]{1,0:T(8,128)(2,1)S(1)}, f32[128,2048]{1,0:T(8,128)S(1)}) custom-call(s32[1]{0:T(128)} %bitcast.place_ref, bf16[128,1024]{1,0:T(8,128)(2,1)S(1)} %copy-done.3, bf16[8192,1024]{1,0:T(8,128)(2,1)} %w_ref.9), custom_call_target="tpu_custom_call" | custom-call | tf_op jit(solution)/shard_map/project/pallas_call | solution.py:737
  84.3 0.6 collective-permute-start.6
  84.9 2.7 %local.1.local_ref = f32[2,8,128,128]{3,2,1,0:T(8,128)} custom-call(bf16[3,128,1024]{2,1,0:T(8,128)(2,1)} %bitcast.11, bf16[3,8,1024]{2,1,0:T(8,128)(2,1)S(1)} %collective-permute-done.edge_ref, f32[3,7,1024]{2,1,0:T(8,128)S(1)} %bitcast.16), custom_call_target="tpu_custom_call" | custom-call | tf_op jit(solution)/shard_map/local/pallas_call | solution.py:940
  87.6 1.3 %collective-permute-start.7 = (bf16[8,1024]{1,0:T(8,128)(2,1)S(1)}, bf16[8,1024]{1,0:T(8,128)(2,1)S(1)}, u32[]{:S(2)}, u32[]{:S(2)}) collective-permute-start(bf16[8,1024]{1,0:T(8,128)(2,1)S(1)} %copy-done.5), channel_id=1, source_target_pairs={{4,0},{8,4},{12,8},{16,12},{20,16},{24,20},{28,24},{5,1},{9,5},{13... | collective-permute-start | bytes 49160 | tf_op jit(solution)/shard_map/ppermute | solution.py:32
  88.9 9.6 %collective-permute-done.6 = bf16[128,2048]{1,0:T(8,128)(2,1)S(1)} collective-permute-done((bf16[128,2048]{1,0:T(8,128)(2,1)S(1)}, bf16[128,2048]{1,0:T(8,128)(2,1)S(1)}, u32[]{:S(2)}, u32[]{:S(2)}) %collective-permute-start.6) | collective-permute-done | bytes 524320 | tf_op jit(solution)/shard_map/ppermute | solution.py:26
  98.5 1.0 add_convert_fusion.1
  99.5 0.5 all-to-all-done.3.got_ref
  100.0 2.9 %finish.1 = (bf16[3,128,1024]{2,1,0:T(8,128)(2,1)}, f32[128,1024]{1,0:T(8,128)}, f32[120,1024]{1,0:T(8,128)}, f32[3,7,1024]{2,1,0:T(8,128)}) custom-call(bf16[8,464,128]{2,1,0:T(8,128)(2,1)S(1)} %all-to-all-done.3.got_ref, f32[8,128,128]{2,1,0:T(8,128)} %get-tuple-element.39.query_grad_ref, bf16[8,1024]{1,0:T(8,128)(2,1)S(1)} %collective-permute-done.7.next_ref, ...), custom_call_target="tpu_custom_call" | custom-call | tf_op jit(solution)/shard_map/finish/pallas_call | solution.py:832
  (26 shorter events, 0.5 us)
Async XLA Ops:
  0.6 13.7 %copy-start = (f32[120,1024]{1,0:T(8,128)S(1)}, f32[120,1024]{1,0:T(8,128)}, u32[]{:S(2)}) copy-start(f32[120,1024]{1,0:T(8,128)} %param.8) | copy-start | bytes 1474564
  0.6 17.3 %collective-permute-start.3 = (bf16[128,2048]{1,0:T(8,128)(2,1)}, bf16[128,2048]{1,0:T(8,128)(2,1)S(1)}, u32[]{:S(2)}, u32[]{:S(2)}) collective-permute-start(bf16[128,2048]{1,0:T(8,128)(2,1)} %refs_0_.1), channel_id=1, source_target_pairs={{0,1},{1,0},{2,3},{3,2},{4,5},{5,4},{6,7},{7,6},{8,9},{9,8},{10,11... | collective-permute-start | bytes 1572872 | tf_op jit(solution)/shard_map/ppermute | solution.py:26
  1.2 15.3 %collective-permute-start.1 = (bf16[128,2048]{1,0:T(8,128)(2,1)}, bf16[128,2048]{1,0:T(8,128)(2,1)S(1)}, u32[]{:S(2)}, u32[]{:S(2)}) collective-permute-start(bf16[128,2048]{1,0:T(8,128)(2,1)} %refs_0_.1), channel_id=1, source_target_pairs={{0,2},{1,3},{2,0},{3,1},{4,6},{5,7},{6,4},{7,5},{8,10},{9,11},{10,... | collective-permute-start | bytes 1572872 | tf_op jit(solution)/shard_map/ppermute | solution.py:26
  6.0 20.8 %collective-permute-start = (bf16[3,8,1024]{2,1,0:T(8,128)(2,1)}, bf16[3,8,1024]{2,1,0:T(8,128)(2,1)S(1)}, u32[]{:S(2)}, u32[]{:S(2)}) collective-permute-start(bf16[3,8,1024]{2,1,0:T(8,128)(2,1)} %get-tuple-element.27), channel_id=1, source_target_pairs={{0,4},{4,8},{8,12},{12,16},{16,20},{20,24},{24,28},{1,5},{5,9},{9,... | collective-permute-start | bytes 147464 | tf_op jit(solution)/shard_map/ppermute | solution.py:32
  9.4 25.2 %all-to-all-start = ((bf16[8,384,128]{2,1,0:T(8,128)(2,1)}), bf16[8,384,128]{2,1,0:T(8,128)(2,1)}, u32[]{:S(2)}, u32[]{:S(2)}) async-start(bf16[8,384,128]{2,1,0:T(8,128)(2,1)} %get-tuple-element.25), calls=%async_computation | async-start | bytes 1572864 | tf_op jit(solution)/shard_map/all_to_all | solution.py:860
  16.5 5.5 %collective-permute-start.2 = (bf16[128,2048]{1,0:T(8,128)(2,1)S(1)}, bf16[128,2048]{1,0:T(8,128)(2,1)S(1)}, u32[]{:S(2)}, u32[]{:S(2)}) collective-permute-start(bf16[128,2048]{1,0:T(8,128)(2,1)S(1)} %collective-permute-done.1.refs_0_), channel_id=1, source_target_pairs={{0,1},{1,0},{2,3},{3,2},{4,5},{5,4},{6,7},{7,6},{8,9},{9,8},{10,11... | collective-permute-start | bytes 1572872 | tf_op jit(solution)/shard_map/ppermute | solution.py:26
  17.9 4.1 %copy-start.1 = (bf16[128,3,1024]{2,0,1:T(8,128)(2,1)S(1)}, bf16[128,3,1024]{2,0,1:T(8,128)(2,1)}, u32[]{:S(2)}) copy-start(bf16[128,3,1024]{2,0,1:T(8,128)(2,1)} %param.6) | copy-start | bytes 2359300
  17.9 4.1 %copy-start.4 = (f32[7,3,1024]{2,0,1:T(8,128)S(1)}, f32[7,3,1024]{2,0,1:T(8,128)}, u32[]{:S(2)}) copy-start(f32[7,3,1024]{2,0,1:T(8,128)} %param.7) | copy-start | bytes 258052
  34.6 14.7 %all-to-all-start.2 = ((bf16[8,128,128]{2,1,0:T(8,128)(2,1)}), bf16[8,128,128]{2,1,0:T(8,128)(2,1)S(1)}, u32[]{:S(2)}, u32[]{:S(2)}) async-start(bf16[8,128,128]{2,1,0:T(8,128)(2,1)} %get-tuple-element.32), calls=%async_computation.2 | async-start | bytes 524288 | tf_op jit(solution)/shard_map/all_to_all | solution.py:860
  49.2 14.5 %all-to-all-start.1 = ((bf16[8,128,128]{2,1,0:T(8,128)(2,1)}), bf16[8,128,128]{2,1,0:T(8,128)(2,1)S(1)}, u32[]{:S(2)}, u32[]{:S(2)}) async-start(bf16[8,128,128]{2,1,0:T(8,128)(2,1)} %get-tuple-element.26), calls=%async_computation.1 | async-start | bytes 524288 | tf_op jit(solution)/shard_map/all_to_all | solution.py:860
  66.3 1.0 copy-start.2
  67.2 8.3 %copy-start.3 = (bf16[128,1024]{1,0:T(8,128)(2,1)S(1)}, bf16[128,1024]{1,0:T(8,128)(2,1)}, u32[]{:S(2)}) copy-start(bf16[128,1024]{1,0:T(8,128)(2,1)} %get-tuple-element.35.product_ref) | copy-start | bytes 786436
  70.5 13.7 %collective-permute-start.5 = (bf16[128,2048]{1,0:T(8,128)(2,1)S(1)}, bf16[128,2048]{1,0:T(8,128)(2,1)S(1)}, u32[]{:S(2)}, u32[]{:S(2)}) collective-permute-start(bf16[128,2048]{1,0:T(8,128)(2,1)S(1)} %project.5), channel_id=1, source_target_pairs={{0,1},{1,0},{2,3},{3,2},{4,5},{5,4},{6,7},{7,6},{8,9},{9,8},{10,11... | collective-permute-start | bytes 1572872 | tf_op jit(solution)/shard_map/ppermute | solution.py:26
  70.6 29.4 %all-to-all-start.3 = ((bf16[8,464,128]{2,1,0:T(8,128)(2,1)}), bf16[8,464,128]{2,1,0:T(8,128)(2,1)S(1)}, u32[]{:S(2)}, u32[]{:S(2)}) async-start(bf16[8,464,128]{2,1,0:T(8,128)(2,1)} %get-tuple-element.38), calls=%async_computation.3 | async-start | bytes 1900544 | tf_op jit(solution)/shard_map/all_to_all | solution.py:860
  78.7 8.9 %copy-start.5 = (bf16[8,1024]{1,0:T(8,128)(2,1)S(1)}, bf16[8,1024]{1,0:T(8,128)(2,1)}, u32[]{:S(2)}) copy-start(bf16[8,1024]{1,0:T(8,128)(2,1)} %get-tuple-element.40) | copy-start | bytes 49156
  83.9 5.0 %collective-permute-start.4 = (bf16[128,2048]{1,0:T(8,128)(2,1)S(1)}, bf16[128,2048]{1,0:T(8,128)(2,1)S(1)}, u32[]{:S(2)}, u32[]{:S(2)}) collective-permute-start(bf16[128,2048]{1,0:T(8,128)(2,1)S(1)} %get-tuple-element.37), channel_id=1, source_target_pairs={{0,1},{1,0},{2,3},{3,2},{4,5},{5,4},{6,7},{7,6},{8,9},{9,8},{10,11... | collective-permute-start | bytes 1572872 | tf_op jit(solution)/shard_map/ppermute | solution.py:26
  84.3 14.2 %collective-permute-start.6 = (bf16[128,2048]{1,0:T(8,128)(2,1)S(1)}, bf16[128,2048]{1,0:T(8,128)(2,1)S(1)}, u32[]{:S(2)}, u32[]{:S(2)}) collective-permute-start(bf16[128,2048]{1,0:T(8,128)(2,1)S(1)} %add_convert_fusion.2), channel_id=1, source_target_pairs={{0,2},{1,3},{2,0},{3,1},{4,6},{5,7},{6,4},{7,5},{8,10},{9,11},{10,... | collective-permute-start | bytes 1572872 | tf_op jit(solution)/shard_map/ppermute | solution.py:26
  87.6 11.9 %collective-permute-start.7 = (bf16[8,1024]{1,0:T(8,128)(2,1)S(1)}, bf16[8,1024]{1,0:T(8,128)(2,1)S(1)}, u32[]{:S(2)}, u32[]{:S(2)}) collective-permute-start(bf16[8,1024]{1,0:T(8,128)(2,1)S(1)} %copy-done.5), channel_id=1, source_target_pairs={{4,0},{8,4},{12,8},{16,12},{20,16},{24,20},{28,24},{5,1},{9,5},{13... | collective-permute-start | bytes 49160 | tf_op jit(solution)/shard_map/ppermute | solution.py:32
